TPU v7x, 512 devices: a whole 4x8x8 slice. The times are simulated.
512 devices in a mesh: sec: 2 (over core), ctx: 64 (over x, z_hi, y), head: 4 (over z_lo).
Axes of the slice: x: 4, y: 8, z: 8 (z_hi: 2, z_lo: 4; z = z_hi * 4 + z_lo), core: 2. Of those that a mesh axis runs over, the one named last changes fastest.
Arguments:
- query_self: bfloat16 [12288, 2048], P('ctx', ('sec', 'head')), may hold values from -12 to 12
- key_self: bfloat16 [12288, 2048], P('ctx', ('sec', 'head')), may hold values from -6 to 6
- value_self: bfloat16 [12288, 2048], P('ctx', ('sec', 'head')), may hold values from -6 to 6
- query_cross: bfloat16 [12288, 2048], P('ctx', ('sec', 'head')), may hold values from -12 to 12
- neighbour_kv: bfloat16 [512, 128, 4096], P(('sec', 'ctx', 'head')), may hold values from -6 to 6
- neighbour_map: int32 [192, 2], P('ctx'), may hold values from 0 to 7, all different within a row
Outputs:
- self_out: bfloat16 [12288, 2048], P('ctx', ('sec', 'head'))
- cross_out: bfloat16 [12288, 2048], P('ctx', ('sec', 'head'))
Inputs may be any that keep to these rules, and one draw needn't show every extreme that they name: `neighbour_map`: entry v of stretch c names slot v % 1 of the device at index v // 1 along sec+head that shares stretch c's context shard; a stretch's two entries differ.
All inputs are finite; a program needn't handle non-finite values.
Results may differ from a plain program's by a relative error of at most 0.0035.
Values may be sent and summed in bfloat16 or wider, within the bound.
No kernel may reach another device: no remote copies, remote signals or barrier semaphores. Data moves between devices by JAX's collectives and lax.ppermute only.
A program may use at most 64 MiB of HBM per device.

v0:
```python
import math

import jax
import jax.numpy as jnp
from jax import lax
from jax.sharding import PartitionSpec as P

HD = 128
STRETCH = 64


MASKED_SCORE = -1e30


def attend_block(carried, queries, key_block, value_block, key_mask, score_scale):
    row_top, row_total, summed = carried
    scores = (
        jnp.einsum("qhd,khd->hqk", queries, key_block, preferred_element_type=jnp.float32)
        * score_scale
    )
    masked = jnp.where(key_mask, scores, MASKED_SCORE)
    new_top = jnp.maximum(row_top, jnp.max(masked, axis=-1))
    exp_scores = jnp.where(key_mask, jnp.exp(masked - new_top[:, :, None]), 0.0)
    factor = jnp.exp(row_top - new_top)
    row_total = row_total * factor + jnp.sum(exp_scores, axis=-1)
    update = jnp.einsum(
        "hqk,khd->qhd",
        exp_scores.astype(jnp.bfloat16),
        value_block,
        preferred_element_type=jnp.float32,
    )
    summed = summed * jnp.transpose(factor)[:, :, None] + update
    return (new_top, row_total, summed)


def attend_keys(carried, queries, key_rows, value_rows, positions, score_scale):
    key_count = key_rows.shape[0]
    head_count = queries.shape[1]
    block_rows = math.gcd(key_count, 1024)
    blocks = key_count // block_rows
    key_stack = key_rows.reshape(blocks, block_rows, head_count, HD)
    value_stack = value_rows.reshape(blocks, block_rows, head_count, HD)

    def fold_step(state_now, scanned):
        number, key_block, value_block = scanned
        places = number * block_rows + jnp.arange(block_rows, dtype=jnp.int32)
        key_mask = (places[None, None, :] <= positions[None, :, None]) & (
            places[None, None, :] >= 0
        )
        return (
            attend_block(state_now, queries, key_block, value_block, key_mask, score_scale),
            None,
        )

    carried, _ = lax.scan(
        fold_step, carried, (jnp.arange(blocks, dtype=jnp.int32), key_stack, value_stack)
    )
    return carried


def self_attention(query_self, key_self, value_self, score_scale):
    local_rows, local_width = query_self.shape
    head_count = local_width // HD
    queries = query_self.reshape(local_rows, head_count, HD)
    first_row = lax.axis_index("ctx") * local_rows
    positions = first_row + jnp.arange(local_rows, dtype=jnp.int32)
    carried = (
        jnp.full((head_count, local_rows), MASKED_SCORE, jnp.float32),
        jnp.zeros((head_count, local_rows), jnp.float32),
        jnp.zeros((local_rows, head_count, HD), jnp.float32),
    )
    carried = attend_keys(
        carried,
        queries,
        lax.all_gather(key_self, "ctx", axis=0, tiled=True),
        lax.all_gather(value_self, "ctx", axis=0, tiled=True),
        positions,
        score_scale,
    )
    row_top, row_total, summed = carried
    attended = summed / jnp.transpose(row_total)[:, :, None]
    return attended.reshape(local_rows, local_width).astype(jnp.bfloat16)


def cross_attention(query_cross, neighbour_kv, neighbour_map, score_scale):
    local_rows, local_width = query_cross.shape
    head_count = local_width // HD
    stretch_count = local_rows // STRETCH
    slot_count, block_len, features = neighbour_kv.shape
    group_count = features // (2 * local_width)
    stretch_first = lax.axis_index("ctx") * stretch_count
    keep_stretch = stretch_first + jnp.arange(stretch_count, dtype=jnp.int32) > 0
    parted = neighbour_kv.reshape(slot_count, block_len, group_count, 2 * local_width)
    received = lax.all_to_all(parted, ("sec", "head"), split_axis=2, concat_axis=0, tiled=True)
    received = received.reshape(group_count * slot_count, block_len, 2, head_count, HD)
    chosen = received[neighbour_map]
    chosen = chosen.reshape(stretch_count, neighbour_map.shape[1] * block_len, 2, head_count, HD)
    stretch_queries = query_cross.reshape(stretch_count, STRETCH, head_count, HD)
    scores = (
        jnp.einsum(
            "cqhd,ckhd->chqk", stretch_queries, chosen[:, :, 0], preferred_element_type=jnp.float32
        )
        * score_scale
    )
    row_top = jnp.max(scores, axis=-1, keepdims=True)
    exp_scores = jnp.exp(scores - row_top)
    row_total = jnp.sum(exp_scores, axis=-1)
    summed = jnp.einsum(
        "chqk,ckhd->cqhd",
        exp_scores.astype(jnp.bfloat16),
        chosen[:, :, 1],
        preferred_element_type=jnp.float32,
    )
    attended = summed / jnp.transpose(row_total, (0, 2, 1))[:, :, :, None]
    attended = attended.reshape(local_rows, local_width)
    keep_rows = jnp.repeat(keep_stretch, STRETCH)
    return jnp.where(keep_rows[:, None], attended, 0.0).astype(jnp.bfloat16)


def on_device(query_self, key_self, value_self, query_cross, neighbour_kv, neighbour_map):
    score_scale = 1.0 / math.sqrt(HD)
    self_out = self_attention(query_self, key_self, value_self, score_scale)
    cross_out = cross_attention(query_cross, neighbour_kv, neighbour_map, score_scale)
    return (self_out, cross_out)


def solution(mesh):
    return jax.shard_map(
        on_device,
        mesh=mesh,
        in_specs=(
            P("ctx", ("sec", "head")),
            P("ctx", ("sec", "head")),
            P("ctx", ("sec", "head")),
            P("ctx", ("sec", "head")),
            P(("sec", "ctx", "head"), None, None),
            P("ctx", None),
        ),
        out_specs=(P("ctx", ("sec", "head")), P("ctx", ("sec", "head"))),
        check_vma=False,
    )
```

profile of v0, /device:TPU:4, one launch (start us, length us, event | category | flops | bytes accessed | tf_op | source)
XLA Modules:
  0.0 453.8 jit_solution(10406228715060818741)
XLA Ops:
  7.2 0.7 all-gather.3.cloned.1.call-update
  8.0 0.7 all-gather.5.cloned.1.call-update
  8.7 2.3 copy.37
  10.9 7.4 %all-to-all-start = ((bf16[1,128,8,512]{1,3,0,2:T(8,128)(2,1)}), bf16[1,128,8,512]{1,3,0,2:T(8,128)(2,1)S(1)}, u32[]{:S(2)}, u32[]{:S(2)}) async-start(bf16[1,128,8,512]{1,3,0,2:T(8,128)(2,1)} %bitcast.1), calls=%async_computation | async-start | bytes 2097152 | tf_op jit(solution)/shard_map/all_to_all | solution.py:94
  18.8 26.6 %all-to-all-done = bf16[1,128,8,512]{1,3,0,2:T(8,128)(2,1)S(1)} async-done(((bf16[1,128,8,512]{1,3,0,2:T(8,128)(2,1)}), bf16[1,128,8,512]{1,3,0,2:T(8,128)(2,1)S(1)}, u32[]{:S(2)}, u32[]{:S(2)}) %all-to-all-start) | async-done | bytes 1048608 | tf_op jit(solution)/shard_map/all_to_all | solution.py:94
  45.4 0.7 copy.39
  46.1 0.7 gather_fusion
  47.9 0.7 fusion.18
  48.6 150.6 %all-gather.3.cloned.1.call-done = bf16[12288,256]{1,0:T(8,128)(2,1)} async-done(((bf16[192,256]{1,0:T(8,128)(2,1)}), bf16[12288,256]{1,0:T(8,128)(2,1)}) %all-gather.3.cloned.1.call-update) | async-done | bytes 6291472 | tf_op jit(solution)/shard_map/all_gather | solution.py:75
  199.2 9.7 %reshape.96 = bf16[12,1024,2,128]{3,2,1,0:T(2,128)(2,1)} reshape(bf16[12288,256]{1,0:T(8,128)(2,1)} %all-gather.3.cloned.1.call-done) | data formatting | bytes 12582912 | tf_op jit(solution)/shard_map/reshape | solution.py:41
  208.8 167.1 %all-gather.5.cloned.1.call-done = bf16[12288,256]{1,0:T(8,128)(2,1)} async-done(((bf16[192,256]{1,0:T(8,128)(2,1)}), bf16[12288,256]{1,0:T(8,128)(2,1)}) %all-gather.5.cloned.1.call-update) | async-done | bytes 6291472 | tf_op jit(solution)/shard_map/all_gather | solution.py:76
  375.9 9.7 %reshape.98 = bf16[12,1024,2,128]{3,2,1,0:T(2,128)(2,1)} reshape(bf16[12288,256]{1,0:T(8,128)(2,1)} %all-gather.5.cloned.1.call-done) | data formatting | bytes 12582912 | tf_op jit(solution)/shard_map/reshape | solution.py:42
  385.6 60.6 %while.15 = (s32[]{:T(128)}, f32[2,192]{1,0:T(2,128)S(1)}, f32[2,192]{1,0:T(2,128)S(1)}, f32[192,2,128]{2,0,1:T(8,128)S(1)}, s32[12]{0:T(128)S(1)}, /*index=5*/b...) while((s32[]{:T(128)}, f32[2,192]{1,0:T(2,128)S(1)}, ...), condition=%wide.region_3.4_spmd.clone, body=%wide.region_0.3_spmd.clone.sunk | while | flops 205411776 | bytes 9178801 | solution.py:55
  387.0 1.9 constant_dynamic-slice_fusion.3
  389.5 0.6 fusion.42
  390.7 0.6 dynamic_slice.19
  392.0 1.9 constant_dynamic-slice_fusion.3
  394.5 0.6 fusion.42
  395.7 0.6 dynamic_slice.19
  397.1 1.9 constant_dynamic-slice_fusion.3
  399.6 0.6 fusion.42
  400.8 0.6 dynamic_slice.19
  402.1 1.9 constant_dynamic-slice_fusion.3
  404.6 0.6 fusion.42
  405.8 0.6 dynamic_slice.19
  407.2 1.9 constant_dynamic-slice_fusion.3
  409.7 0.6 fusion.42
  410.9 0.6 dynamic_slice.19
  412.2 1.9 constant_dynamic-slice_fusion.3
  414.7 0.6 fusion.42
  415.9 0.6 dynamic_slice.19
  417.3 1.9 constant_dynamic-slice_fusion.3
  419.8 0.6 fusion.42
  421.0 0.6 dynamic_slice.19
  422.3 1.9 constant_dynamic-slice_fusion.3
  424.8 0.6 fusion.42
  426.0 0.6 dynamic_slice.19
  427.4 1.9 constant_dynamic-slice_fusion.3
  429.9 0.6 fusion.42
  432.4 1.9 constant_dynamic-slice_fusion.3
  434.9 0.6 fusion.42
  436.1 0.6 dynamic_slice.19
  437.5 1.9 constant_dynamic-slice_fusion.3
  440.0 0.6 fusion.42
  441.2 0.6 dynamic_slice.19
  442.5 1.9 constant_dynamic-slice_fusion.3
  445.0 0.6 fusion.42
  446.2 0.8 copy_bitcast_fusion.8
  (137 shorter events, 18.7 us)
Async XLA Ops:
  7.2 11.6 %copy-start = (bf16[192,256]{1,0:T(8,128)(2,1)S(1)}, bf16[192,256]{1,0:T(8,128)(2,1)}, u32[]{:S(2)}) copy-start(bf16[192,256]{1,0:T(8,128)(2,1)} %param.8) | copy-start | bytes 294916
  7.2 192.0 %all-gather.3.cloned.1.call-start = ((), (), s32[]{:S(2)}) async-start(), calls=%async_computation.1 | async-start | bytes 6389760 | tf_op jit(solution)/shard_map/all_gather | solution.py:75
  7.9 368.0 %all-gather.5.cloned.1.call-start = ((), (), s32[]{:S(2)}) async-start(), calls=%async_computation.2 | async-start | bytes 6389760 | tf_op jit(solution)/shard_map/all_gather | solution.py:76
  10.9 7.6 %copy-start.2 = (s32[3,2]{0,1:T(2,128)S(1)}, s32[3,2]{0,1:T(2,128)}, u32[]{:S(2)}) copy-start(s32[3,2]{0,1:T(2,128)} %param.13) | copy-start | bytes 76
  10.9 7.8 %copy-start.1 = (bf16[192,256]{1,0:T(8,128)(2,1)S(1)}, bf16[192,256]{1,0:T(8,128)(2,1)}, u32[]{:S(2)}) copy-start(bf16[192,256]{1,0:T(8,128)(2,1)} %param.11) | copy-start | bytes 294916
  10.9 34.5 %all-to-all-start = ((bf16[1,128,8,512]{1,3,0,2:T(8,128)(2,1)}), bf16[1,128,8,512]{1,3,0,2:T(8,128)(2,1)S(1)}, u32[]{:S(2)}, u32[]{:S(2)}) async-start(bf16[1,128,8,512]{1,3,0,2:T(8,128)(2,1)} %bitcast.1), calls=%async_computation | async-start | bytes 2097152 | tf_op jit(solution)/shard_map/all_to_all | solution.py:94
Sparse Core Ops, SparseCore 0:
  12.4 186.6 all-gather.2
  203.6 172.2 all-gather.4
where the time goes:
time: 455 us; the launch traced here: 454 us
  waiting for transfers between devices  346 us (76%)
  local copies, waits for them, and re-layouts  53.5 us (12%)
  matrix products  14.5 us (3%)
  between operations  14.2 us (3%)
  other arithmetic  11.1 us (2%)
  loops' own time  7.49 us (2%)
  starting transfers between devices  7.47 us (2%)
    all_gather x1, waiting for transfers between devices, self_attention(): lax.all_gather(value_self, 'ctx', axis=0, tiled=True)  167 us
    all_gather x1, waiting for transfers between devices, self_attention(): lax.all_gather(key_self, 'ctx', axis=0, tiled=True)  151 us
    dynamic_slice x24, local copies, waits for them, and re-layouts, attend_keys(): lax.scan(fold_step, carried, (jnp.arange(blocks, dtype=jnp.int32), key_st...  29.8 us
    all_to_all x1, waiting for transfers between devices, cross_attention(): lax.all_to_all(parted, ('sec', 'head'), split_axis=2, concat_axis=0, tile...  26.6 us
    reshape x1, local copies, waits for them, and re-layouts, attend_keys(): value_stack = value_rows.reshape(blocks, block_rows, head_count, HD)  9.73 us
    reshape x1, local copies, waits for them, and re-layouts, attend_keys(): key_stack = key_rows.reshape(blocks, block_rows, head_count, HD)  9.69 us
  transfers between devices with their start and end apart: 3, of which 3 were waited for; matrix products, arithmetic and copies ran while one was open for 3% of the time, Pallas kernels for 0%

commit v1 on v0

v1 whole, which is shorter than its diff:
```python
import functools
import math

import jax
import jax.numpy as jnp
from jax import lax
from jax.experimental import pallas as pl
from jax.experimental.pallas import tpu as pltpu
from jax.sharding import Mesh
from jax.sharding import PartitionSpec as P

HD = 128
STRETCH = 64
NX, NZ, NY = 4, 2, 8
ROWS = 192
WIDTH = 256
STAT_ROWS = 16
KEYS = NX * NZ * ROWS
CHUNK = 256
LOW = -1e30
FAR = 1 << 30
SCALE = 1.0 / math.sqrt(HD)
LOG2E = math.log2(math.e)


def partial_kernel(place_ref, kpos_ref, q_ref, kv0, kv1, kv2, kv3, kv4, kv5, kv6, kv7,
                   out_ref, k_scr, v_scr, s_scr, sem):
    i = pl.program_id(0)
    first = place_ref[0]
    pieces = (kv0, kv1, kv2, kv3, kv4, kv5, kv6, kv7)

    @pl.when(i == 0)
    def _():
        copies = []
        for p, kv in enumerate(pieces):
            copies.append(pltpu.make_async_copy(
                kv.at[pl.ds(0, ROWS), :], k_scr.at[pl.ds(p * ROWS, ROWS), :], sem.at[p, 0]))
            for h in range(2):
                copies.append(pltpu.make_async_copy(
                    kv.at[pl.ds(ROWS, ROWS), pl.ds(h * HD, HD)],
                    v_scr.at[h, pl.ds(p * ROWS, ROWS), pl.ds(0, HD)], sem.at[p, 1 + h]))
        for c in copies:
            c.start()
        v_scr[0, :, HD:] = jnp.ones((KEYS, HD), jnp.bfloat16)
        v_scr[1, :, HD:] = jnp.ones((KEYS, HD), jnp.bfloat16)
        for c in copies:
            c.wait()

    qpos = first + i * ROWS + lax.broadcasted_iota(jnp.int32, (ROWS, CHUNK), 0)
    c2 = SCALE * LOG2E
    for h in range(2):
        qh = q_ref[0, :, h * HD:(h + 1) * HD]
        top = jnp.full((ROWS, HD), LOW, jnp.float32)
        for c in range(KEYS // CHUNK):
            kc = k_scr[pl.ds(c * CHUNK, CHUNK), h * HD:(h + 1) * HD]
            s = lax.dot_general(qh, kc, (((1,), (1,)), ((), ())),
                                preferred_element_type=jnp.float32)
            kp = kpos_ref[0:1, c * CHUNK:(c + 1) * CHUNK]
            s = jnp.where(kp <= qpos, s, LOW)
            s_scr[:, c * CHUNK:(c + 1) * CHUNK] = s
            top = jnp.maximum(top, jnp.maximum(s[:, :HD], s[:, HD:]))
        top = jnp.broadcast_to(jnp.max(top, axis=1, keepdims=True), (ROWS, HD))
        off = jnp.maximum(top, -1e20) * c2
        off2 = jnp.concatenate([off, off], axis=1)
        acc = jnp.zeros((ROWS, 2 * HD), jnp.float32)
        for c in range(KEYS // CHUNK):
            s = s_scr[:, c * CHUNK:(c + 1) * CHUNK]
            p = jnp.exp2(s * c2 - off2).astype(jnp.bfloat16)
            acc = acc + lax.dot_general(p, v_scr[h, pl.ds(c * CHUNK, CHUNK), :],
                                        (((1,), (0,)), ((), ())),
                                        preferred_element_type=jnp.float32)
        total = jnp.maximum(acc[:, HD:], 1e-30)
        out_ref[0, 0:ROWS, h * HD:(h + 1) * HD] = (acc[:, :HD] / total).astype(jnp.bfloat16)
        stat = jnp.where(top > 0.5 * LOW, top * SCALE + jnp.log(total), LOW)
        row = jnp.transpose(stat)[0:STAT_ROWS // 2, :]
        hi = row.astype(jnp.bfloat16).astype(jnp.float32)
        mid = (row - hi).astype(jnp.bfloat16).astype(jnp.float32)
        low = row - hi - mid
        at = lax.broadcasted_iota(jnp.int32, row.shape, 0)
        coded = jnp.where(at == 0, hi, jnp.where(at == 1, mid, low))
        if h == 0:
            held = coded
        else:
            out_ref[0, ROWS:ROWS + STAT_ROWS, 0:ROWS] = jnp.concatenate(
                [held, coded], axis=0).astype(jnp.bfloat16)
    out_ref[0, ROWS:ROWS + STAT_ROWS, ROWS:] = jnp.zeros((STAT_ROWS, WIDTH - ROWS), jnp.bfloat16)


def partial_attention(place, kpos, q_all, pieces):
    whole = pl.BlockSpec(memory_space=pl.ANY)
    return pl.pallas_call(
        partial_kernel,
        out_shape=jax.ShapeDtypeStruct((NY, ROWS + STAT_ROWS, WIDTH), jnp.bfloat16),
        grid=(NY,),
        in_specs=[
            pl.BlockSpec(memory_space=pltpu.SMEM),
            pl.BlockSpec((1, KEYS), lambda i: (0, 0)),
            pl.BlockSpec((1, ROWS, WIDTH), lambda i: (i, 0, 0)),
        ] + [whole] * 8,
        out_specs=pl.BlockSpec((1, ROWS + STAT_ROWS, WIDTH), lambda i: (i, 0, 0)),
        scratch_shapes=[
            pltpu.VMEM((KEYS, WIDTH), jnp.bfloat16),
            pltpu.VMEM((2, KEYS, WIDTH), jnp.bfloat16),
            pltpu.VMEM((ROWS, KEYS), jnp.float32),
            pltpu.SemaphoreType.DMA((8, 3)),
        ],
        cost_estimate=pl.CostEstimate(
            flops=4 * NY * ROWS * KEYS * WIDTH, bytes_accessed=4 * KEYS * WIDTH,
            transcendentals=2 * NY * ROWS * KEYS),
        compiler_params=pltpu.CompilerParams(vmem_limit_bytes=12 << 20),
        name="partial_attention",
    )(place, kpos, q_all, *pieces)


def combine_kernel(part_ref, out_ref):
    stats = []
    for h in range(2):
        rows = []
        for j in range(NY):
            block = part_ref[j, pl.ds(ROWS, STAT_ROWS), :].astype(jnp.float32)
            b = block[8 * h:8 * h + 8]
            rows.append(b[0:1] + b[1:2] + b[2:3])
        top = functools.reduce(jnp.maximum, rows)
        ws = [jnp.exp(r - top) for r in rows]
        inv = 1.0 / functools.reduce(jnp.add, ws)
        stats += [w * inv for w in ws]
    table = jnp.concatenate(stats, axis=0)
    cols = jnp.transpose(table)[0:ROWS]
    for h in range(2):
        acc = jnp.zeros((ROWS, HD), jnp.float32)
        for j in range(NY):
            o = part_ref[j, 0:ROWS, h * HD:(h + 1) * HD].astype(jnp.float32)
            acc = acc + o * cols[:, h * NY + j:h * NY + j + 1]
        out_ref[:, h * HD:(h + 1) * HD] = acc.astype(jnp.bfloat16)


def combine(parts):
    return pl.pallas_call(
        combine_kernel,
        out_shape=jax.ShapeDtypeStruct((ROWS, WIDTH), jnp.bfloat16),
        in_specs=[pl.BlockSpec(memory_space=pltpu.VMEM)],
        out_specs=pl.BlockSpec(memory_space=pltpu.VMEM),
        compiler_params=pltpu.CompilerParams(vmem_limit_bytes=8 << 20),
        name="combine",
    )(parts)


def self_attention(query_self, key_self, value_self):
    x, zh, y = lax.axis_index("x"), lax.axis_index("zh"), lax.axis_index("y")
    group = x * NZ + zh
    kv = jnp.concatenate([key_self, value_self], axis=0)
    kvz = lax.ppermute(kv, "zh", [(0, 1), (1, 0)])
    pieces = [kv]
    groups = [group]
    for k in range(1, NX):
        pieces.append(lax.ppermute(kv, "x", [(a, a + k) for a in range(NX - k)]))
        groups.append(jnp.where(x >= k, group - NZ * k, FAR))
    pieces.append(kvz)
    groups.append(x * NZ + 1 - zh)
    for k in range(1, NX):
        pieces.append(lax.ppermute(kvz, "x", [(a, a + k) for a in range(NX - k)]))
        groups.append(jnp.where(x >= k, x * NZ + 1 - zh - NZ * k, FAR))
    q_all = lax.all_to_all(
        jnp.broadcast_to(query_self[None], (NY, ROWS, WIDTH)), "y", 0, 0, tiled=True)
    starts = jnp.stack([jnp.where(g == FAR, FAR, g * (NY * ROWS) + y * ROWS) for g in groups])
    kpos = (starts[:, None] + jnp.arange(ROWS, dtype=jnp.int32)[None, :]).reshape(1, KEYS)
    full = ((x == NX - 1) & (zh == NZ - 1)).astype(jnp.int32)
    place = jnp.stack([group * (NY * ROWS), full]).astype(jnp.int32)
    parts = partial_attention(place, kpos, q_all, pieces)
    received = lax.all_to_all(parts, "y", 0, 0, tiled=True)
    return combine(received)


def cross_attention(query_cross, neighbour_kv, neighbour_map):
    local_rows, local_width = query_cross.shape
    head_count = local_width // HD
    stretch_count = local_rows // STRETCH
    slot_count, block_len, features = neighbour_kv.shape
    group_count = features // (2 * local_width)
    stretch_first = lax.axis_index(("x", "zh", "y")) * stretch_count
    keep_stretch = stretch_first + jnp.arange(stretch_count, dtype=jnp.int32) > 0
    parted = neighbour_kv.reshape(slot_count, block_len, group_count, 2 * local_width)
    received = lax.all_to_all(parted, ("sec", "head"), split_axis=2, concat_axis=0, tiled=True)
    received = received.reshape(group_count * slot_count, block_len, 2, head_count, HD)
    chosen = received[neighbour_map]
    chosen = chosen.reshape(stretch_count, neighbour_map.shape[1] * block_len, 2, head_count, HD)
    stretch_queries = query_cross.reshape(stretch_count, STRETCH, head_count, HD)
    scores = jnp.einsum("cqhd,ckhd->chqk", stretch_queries, chosen[:, :, 0],
                        preferred_element_type=jnp.float32) * SCALE
    row_top = jnp.max(scores, axis=-1, keepdims=True)
    exp_scores = jnp.exp(scores - row_top)
    row_total = jnp.sum(exp_scores, axis=-1)
    summed = jnp.einsum("chqk,ckhd->cqhd", exp_scores.astype(jnp.bfloat16), chosen[:, :, 1],
                        preferred_element_type=jnp.float32)
    attended = summed / jnp.transpose(row_total, (0, 2, 1))[:, :, :, None]
    attended = attended.reshape(local_rows, local_width)
    keep_rows = jnp.repeat(keep_stretch, STRETCH)
    return jnp.where(keep_rows[:, None], attended, 0.0).astype(jnp.bfloat16)


def on_device(query_self, key_self, value_self, query_cross, neighbour_kv, neighbour_map):
    self_out = self_attention(query_self, key_self, value_self)
    cross_out = cross_attention(query_cross, neighbour_kv, neighbour_map)
    return (self_out, cross_out)


def solution(mesh):
    fine = Mesh(mesh.devices.reshape(2, NX, NZ, NY, 4), ("sec", "x", "zh", "y", "head"))
    rows, cols = ("x", "zh", "y"), ("sec", "head")
    return jax.shard_map(
        on_device,
        mesh=fine,
        in_specs=(
            P(rows, cols),
            P(rows, cols),
            P(rows, cols),
            P(rows, cols),
            P(("sec", "x", "zh", "y", "head"), None, None),
            P(rows, None),
        ),
        out_specs=(P(rows, cols), P(rows, cols)),
        check_vma=False,
    )
```

time: 455 us -> 133 us (0.29)
  the two profiles are of different devices: /device:TPU:4 before, /device:TPU:7 now
where the time goes in v1:
time: 133 us
  waiting for transfers between devices  74.3 us (56%)
  starting transfers between devices  34.1 us (26%)
  Pallas kernels  15 us (11%)
  local copies, waits for them, and re-layouts  6.9 us (5%)
    all_to_all x1, waiting for transfers between devices, self_attention(): lax.all_to_all(jnp.broadcast_to(query_self[None], (NY, ROWS, WIDTH)), 'y'...  22.2 us
    all_to_all x1, waiting for transfers between devices, self_attention(): received = lax.all_to_all(parts, 'y', 0, 0, tiled=True)  20.7 us
    ppermute x1, waiting for transfers between devices, self_attention(): kvz = lax.ppermute(kv, 'zh', [(0, 1), (1, 0)])  19.8 us
    pallas_call x1, Pallas kernels, partial_attention(): pl.pallas_call(partial_kernel, out_shape=jax.ShapeDtypeStruct((NY, ROWS +...  13.7 us
    ppermute x3, waiting for transfers between devices, self_attention(): pieces.append(lax.ppermute(kvz, 'x', [(a, a + k) for a in range(NX - k)]))  11.6 us
    ppermute x1, starting transfers between devices, self_attention(): kvz = lax.ppermute(kv, 'zh', [(0, 1), (1, 0)])  7.93 us
    all_to_all x1, starting transfers between devices, cross_attention(): lax.all_to_all(parted, ('sec', 'head'), split_axis=2, concat_axis=0, tile...  7.89 us
    all_to_all x1, starting transfers between devices, self_attention(): lax.all_to_all(jnp.broadcast_to(query_self[None], (NY, ROWS, WIDTH)), 'y'...  6.82 us
  transfers between devices with their start and end apart: 10, of which 6 were waited for; matrix products, arithmetic and copies ran while one was open for 4% of the time, Pallas kernels for 10%

profile of v1, /device:TPU:7, one launch (start us, length us, event | category | flops | bytes accessed | tf_op | source)
XLA Modules:
  0.0 132.9 jit_solution(16519412234312321197)
XLA Ops:
  0.6 0.0 copy-start
  0.6 2.0 %broadcast_in_dim.30 = bf16[8,192,256]{2,1,0:T(8,128)(2,1)} broadcast(bf16[192,256]{1,0:T(8,128)(2,1)} %param.6), dimensions={1,2} | broadcast | bytes 884736 | tf_op jit(solution)/shard_map/broadcast_in_dim | solution.py:164
  2.6 6.8 %all-to-all-start = ((bf16[8,192,256]{2,1,0:T(8,128)(2,1)}), bf16[8,192,256]{2,1,0:T(8,128)(2,1)S(1)}, u32[]{:S(2)}, u32[]{:S(2)}) async-start(bf16[8,192,256]{2,1,0:T(8,128)(2,1)} %broadcast_in_dim.30), calls=%async_computation | async-start | bytes 1572864 | tf_op jit(solution)/shard_map/all_to_all | solution.py:163
  9.4 0.0 copy-done
  9.4 1.3 copy.24
  10.8 22.2 %all-to-all-done.q_ref = bf16[8,192,256]{2,1,0:T(8,128)(2,1)S(1)} async-done(((bf16[8,192,256]{2,1,0:T(8,128)(2,1)}), bf16[8,192,256]{2,1,0:T(8,128)(2,1)S(1)}, u32[]{:S(2)}, u32[]{:S(2)}) %all-to-all-start) | async-done | bytes 786464 | tf_op jit(solution)/shard_map/all_to_all | solution.py:163
  33.0 7.9 %all-to-all-start.2 = ((bf16[1,128,8,512]{1,3,0,2:T(8,128)(2,1)}), bf16[1,128,8,512]{1,3,0,2:T(8,128)(2,1)S(1)}, u32[]{:S(2)}, u32[]{:S(2)}) async-start(bf16[1,128,8,512]{1,3,0,2:T(8,128)(2,1)} %bitcast.10), calls=%async_computation.2 | async-start | bytes 2097152 | tf_op jit(solution)/shard_map/all_to_all | solution.py:183
  40.9 0.0 copy-done.1
  40.9 0.9 copy-done.2
  41.8 7.9 %collective-permute-start.3 = (bf16[384,256]{1,0:T(8,128)(2,1)S(1)}, bf16[384,256]{1,0:T(8,128)(2,1)S(1)}, u32[]{:S(2)}, u32[]{:S(2)}) collective-permute-start(bf16[384,256]{1,0:T(8,128)(2,1)S(1)} %constant_dynamic-update-slice_fusion.kv0), channel_id=1, source_target_pairs={{0,32},{32,0},{1,33},{33,1},{2,34},{34,2},{3,35},{35,3},{4,36},{36... | collective-permute-start | bytes 589832 | tf_op jit(solution)/shard_map/ppermute | solution.py:152
  49.7 1.3 collective-permute-start
  51.0 1.3 collective-permute-start.1
  52.3 1.3 collective-permute-start.2
  53.7 0.1 stack.51
  53.8 19.8 %collective-permute-done.3.kv4 = bf16[384,256]{1,0:T(8,128)(2,1)S(1)} collective-permute-done((bf16[384,256]{1,0:T(8,128)(2,1)S(1)}, bf16[384,256]{1,0:T(8,128)(2,1)S(1)}, u32[]{:S(2)}, u32[]{:S(2)}) %collective-permute-start.3) | collective-permute-done | bytes 196640 | tf_op jit(solution)/shard_map/ppermute | solution.py:152
  73.6 1.3 collective-permute-start.4
  74.9 1.3 collective-permute-start.5
  76.2 0.0 collective-permute-done.kv1
  76.2 1.3 collective-permute-start.6
  77.5 0.1 iota_add_fusion
  77.6 0.1 add.90.kpos_ref
  77.7 0.1 pad_add_fusion.place_ref
  77.7 0.0 collective-permute-done.1.kv2
  77.7 0.0 collective-permute-done.2.kv3
  77.7 3.6 %collective-permute-done.4.kv5 = bf16[384,256]{1,0:T(8,128)(2,1)S(1)} collective-permute-done((bf16[384,256]{1,0:T(8,128)(2,1)S(1)}, bf16[384,256]{1,0:T(8,128)(2,1)S(1)}, u32[]{:S(2)}, u32[]{:S(2)}) %collective-permute-start.4) | collective-permute-done | bytes 196640 | tf_op jit(solution)/shard_map/ppermute | solution.py:161
  81.3 2.8 %collective-permute-done.5.kv6 = bf16[384,256]{1,0:T(8,128)(2,1)S(1)} collective-permute-done((bf16[384,256]{1,0:T(8,128)(2,1)S(1)}, bf16[384,256]{1,0:T(8,128)(2,1)S(1)}, u32[]{:S(2)}, u32[]{:S(2)}) %collective-permute-start.5) | collective-permute-done | bytes 196640 | tf_op jit(solution)/shard_map/ppermute | solution.py:161
  84.1 5.2 %collective-permute-done.6.kv7 = bf16[384,256]{1,0:T(8,128)(2,1)S(1)} collective-permute-done((bf16[384,256]{1,0:T(8,128)(2,1)S(1)}, bf16[384,256]{1,0:T(8,128)(2,1)S(1)}, u32[]{:S(2)}, u32[]{:S(2)}) %collective-permute-start.6) | collective-permute-done | bytes 196640 | tf_op jit(solution)/shard_map/ppermute | solution.py:161
  89.3 13.7 %partial_attention.1 = bf16[8,208,256]{2,1,0:T(8,128)(2,1)} custom-call(s32[2]{0:T(128)S(1)} %pad_add_fusion.place_ref, s32[1,1536]{1,0:T(1,128)S(1)} %add.90.kpos_ref, bf16[8,192,256]{2,1,0:T(8,128)(2,1)S(1)} %all-to-all-done.q_ref, bf16[384,256]{1,0:T(8,128)(2,1)S(1)} %constant_dynamic-update-slice_fusion.kv0, ...), custom_call_target="tpu_custom_call" | custom-call | flops 2415919104 | bytes 1572864 | tf_op jit(solution)/shard_map/partial_attention/pallas_call | solution.py:91
  103.0 0.0 copy-start.3
  103.0 0.0 all-to-all-done.2
  103.0 3.7 %all-to-all-start.1 = ((bf16[8,208,256]{2,1,0:T(8,128)(2,1)}), bf16[8,208,256]{2,1,0:T(8,128)(2,1)S(1)}, u32[]{:S(2)}, u32[]{:S(2)}) async-start(bf16[8,208,256]{2,1,0:T(8,128)(2,1)} %partial_attention.1), calls=%async_computation.1 | async-start | bytes 1703936 | tf_op jit(solution)/shard_map/all_to_all | solution.py:170
  106.7 0.1 broadcast_in_dim.31
  106.8 0.1 broadcast_in_dim.32
  106.9 0.6 copy-done.4
  107.5 0.1 copy.25
  107.6 0.1 reshape.56
  107.7 0.0 copy-done.3
  107.7 0.7 copy.26
  108.4 0.7 gather_fusion
  109.1 0.1 copy.27
  109.2 0.1 fusion.8
  109.2 0.3 fusion.9
  109.6 0.2 fusion.2
  109.8 0.3 fusion.1
  110.1 0.1 copy.31
  110.2 0.7 fusion.5
  110.9 20.7 %all-to-all-done.1.part_ref = bf16[8,208,256]{2,1,0:T(8,128)(2,1)S(1)} async-done(((bf16[8,208,256]{2,1,0:T(8,128)(2,1)}), bf16[8,208,256]{2,1,0:T(8,128)(2,1)S(1)}, u32[]{:S(2)}, u32[]{:S(2)}) %all-to-all-start.1) | async-done | bytes 852000 | tf_op jit(solution)/shard_map/all_to_all | solution.py:170
  131.6 1.3 combine.1
  (9 shorter events, 0.1 us)
Async XLA Ops:
  0.6 8.8 %copy-start = (bf16[1,128,4096]{2,1,0:T(8,128)(2,1)S(1)}, bf16[1,128,4096]{2,1,0:T(8,128)(2,1)}, u32[]{:S(2)}) copy-start(bf16[1,128,4096]{2,1,0:T(8,128)(2,1)} %param.10) | copy-start | bytes 3145732
  2.6 30.4 %all-to-all-start = ((bf16[8,192,256]{2,1,0:T(8,128)(2,1)}), bf16[8,192,256]{2,1,0:T(8,128)(2,1)S(1)}, u32[]{:S(2)}, u32[]{:S(2)}) async-start(bf16[8,192,256]{2,1,0:T(8,128)(2,1)} %broadcast_in_dim.30), calls=%async_computation | async-start | bytes 1572864 | tf_op jit(solution)/shard_map/all_to_all | solution.py:163
  33.0 7.9 %copy-start.1 = (bf16[192,256]{1,0:T(8,128)(2,1)S(1)}, bf16[192,256]{1,0:T(8,128)(2,1)}, u32[]{:S(2)}) copy-start(bf16[192,256]{1,0:T(8,128)(2,1)} %param.7) | copy-start | bytes 294916
  33.0 70.0 %all-to-all-start.2 = ((bf16[1,128,8,512]{1,3,0,2:T(8,128)(2,1)}), bf16[1,128,8,512]{1,3,0,2:T(8,128)(2,1)S(1)}, u32[]{:S(2)}, u32[]{:S(2)}) async-start(bf16[1,128,8,512]{1,3,0,2:T(8,128)(2,1)} %bitcast.10), calls=%async_computation.2 | async-start | bytes 2097152 | tf_op jit(solution)/shard_map/all_to_all | solution.py:183
  40.9 0.9 copy-start.2
  41.8 31.8 %collective-permute-start.3 = (bf16[384,256]{1,0:T(8,128)(2,1)S(1)}, bf16[384,256]{1,0:T(8,128)(2,1)S(1)}, u32[]{:S(2)}, u32[]{:S(2)}) collective-permute-start(bf16[384,256]{1,0:T(8,128)(2,1)S(1)} %constant_dynamic-update-slice_fusion.kv0), channel_id=1, source_target_pairs={{0,32},{32,0},{1,33},{33,1},{2,34},{34,2},{3,35},{35,3},{4,36},{36... | collective-permute-start | bytes 589832 | tf_op jit(solution)/shard_map/ppermute | solution.py:152
  49.7 26.4 %collective-permute-start = (bf16[384,256]{1,0:T(8,128)(2,1)S(1)}, bf16[384,256]{1,0:T(8,128)(2,1)S(1)}, u32[]{:S(2)}, u32[]{:S(2)}) collective-permute-start(bf16[384,256]{1,0:T(8,128)(2,1)S(1)} %constant_dynamic-update-slice_fusion.kv0), channel_id=1, source_target_pairs={{0,64},{64,128},{128,192},{1,65},{65,129},{129,193},{2,66},{66,130... | collective-permute-start | bytes 589832 | tf_op jit(solution)/shard_map/ppermute | solution.py:156
  51.0 26.7 %collective-permute-start.1 = (bf16[384,256]{1,0:T(8,128)(2,1)S(1)}, bf16[384,256]{1,0:T(8,128)(2,1)S(1)}, u32[]{:S(2)}, u32[]{:S(2)}) collective-permute-start(bf16[384,256]{1,0:T(8,128)(2,1)S(1)} %constant_dynamic-update-slice_fusion.kv0), channel_id=1, source_target_pairs={{0,128},{64,192},{1,129},{65,193},{2,130},{66,194},{3,131},{67,195... | collective-permute-start | bytes 589832 | tf_op jit(solution)/shard_map/ppermute | solution.py:156
  52.3 25.4 %collective-permute-start.2 = (bf16[384,256]{1,0:T(8,128)(2,1)S(1)}, bf16[384,256]{1,0:T(8,128)(2,1)S(1)}, u32[]{:S(2)}, u32[]{:S(2)}) collective-permute-start(bf16[384,256]{1,0:T(8,128)(2,1)S(1)} %constant_dynamic-update-slice_fusion.kv0), channel_id=1, source_target_pairs={{0,192},{1,193},{2,194},{3,195},{4,196},{5,197},{6,198},{7,199},{8... | collective-permute-start | bytes 589832 | tf_op jit(solution)/shard_map/ppermute | solution.py:156
  73.6 7.7 %collective-permute-start.4 = (bf16[384,256]{1,0:T(8,128)(2,1)S(1)}, bf16[384,256]{1,0:T(8,128)(2,1)S(1)}, u32[]{:S(2)}, u32[]{:S(2)}) collective-permute-start(bf16[384,256]{1,0:T(8,128)(2,1)S(1)} %collective-permute-done.3.kv4), channel_id=1, source_target_pairs={{0,64},{64,128},{128,192},{1,65},{65,129},{129,193},{2,66},{66,130... | collective-permute-start | bytes 589832 | tf_op jit(solution)/shard_map/ppermute | solution.py:161
  74.9 9.2 %collective-permute-start.5 = (bf16[384,256]{1,0:T(8,128)(2,1)S(1)}, bf16[384,256]{1,0:T(8,128)(2,1)S(1)}, u32[]{:S(2)}, u32[]{:S(2)}) collective-permute-start(bf16[384,256]{1,0:T(8,128)(2,1)S(1)} %collective-permute-done.3.kv4), channel_id=1, source_target_pairs={{0,128},{64,192},{1,129},{65,193},{2,130},{66,194},{3,131},{67,195... | collective-permute-start | bytes 589832 | tf_op jit(solution)/shard_map/ppermute | solution.py:161
  76.2 13.1 %collective-permute-start.6 = (bf16[384,256]{1,0:T(8,128)(2,1)S(1)}, bf16[384,256]{1,0:T(8,128)(2,1)S(1)}, u32[]{:S(2)}, u32[]{:S(2)}) collective-permute-start(bf16[384,256]{1,0:T(8,128)(2,1)S(1)} %collective-permute-done.3.kv4), channel_id=1, source_target_pairs={{0,192},{1,193},{2,194},{3,195},{4,196},{5,197},{6,198},{7,199},{8... | collective-permute-start | bytes 589832 | tf_op jit(solution)/shard_map/ppermute | solution.py:161
  103.0 4.7 %copy-start.3 = (bf16[192,256]{1,0:T(8,128)(2,1)S(1)}, bf16[192,256]{1,0:T(8,128)(2,1)}, u32[]{:S(2)}) copy-start(bf16[192,256]{1,0:T(8,128)(2,1)} %param.9) | copy-start | bytes 294916
  103.0 28.6 %all-to-all-start.1 = ((bf16[8,208,256]{2,1,0:T(8,128)(2,1)}), bf16[8,208,256]{2,1,0:T(8,128)(2,1)S(1)}, u32[]{:S(2)}, u32[]{:S(2)}) async-start(bf16[8,208,256]{2,1,0:T(8,128)(2,1)} %partial_attention.1), calls=%async_computation.1 | async-start | bytes 1703936 | tf_op jit(solution)/shard_map/all_to_all | solution.py:170
  106.8 0.7 copy-start.4

commit v2 on v1

v2 whole, which is shorter than its diff:
```python
import functools
import math

import jax
import jax.numpy as jnp
from jax import lax
from jax.experimental import pallas as pl
from jax.experimental.pallas import tpu as pltpu
from jax.sharding import Mesh
from jax.sharding import PartitionSpec as P

HD = 128
STRETCH = 64
NX, NZ, NY = 4, 2, 8
ROWS = 192
WIDTH = 256
STAT_ROWS = 16
PIECES = NX * NZ
KEYS = PIECES * ROWS
CHUNK = 256
BLOCK = 128
GROUPS = 8
GROUP_WIDTH = 512
STRETCHES = ROWS // STRETCH
LOW = -1e30
SCALE = 1.0 / math.sqrt(HD)
C2 = SCALE * math.log2(math.e)
SHARDS = 4
TILE = SHARDS * ROWS

ANY = pl.BlockSpec(memory_space=pl.ANY)
IN_SMEM = pl.BlockSpec(memory_space=pltpu.SMEM)
IN_VMEM = pl.BlockSpec(memory_space=pltpu.VMEM)


def code_stat(stat):
    row = jnp.transpose(stat)[0:STAT_ROWS // 2, :]
    hi = row.astype(jnp.bfloat16).astype(jnp.float32)
    mid = (row - hi).astype(jnp.bfloat16).astype(jnp.float32)
    low = row - hi - mid
    at = lax.broadcasted_iota(jnp.int32, row.shape, 0)
    return jnp.where(at == 0, hi, jnp.where(at == 1, mid, low))


def partial_kernel(place_ref, q_ref, *refs):
    pieces, out_ref = refs[:PIECES], refs[PIECES]
    k_scr, v_scr, s_scr, sem = refs[PIECES + 1:]
    x, zh, y = place_ref[0], place_ref[1], place_ref[2]
    i = pl.program_id(0)

    @pl.when(i == 0)
    def _():
        copies = []
        for p, kv in enumerate(pieces):
            for h in range(2):
                copies.append(pltpu.make_async_copy(
                    kv.at[pl.ds(0, ROWS), pl.ds(h * HD, HD)],
                    k_scr.at[pl.ds(p * ROWS, ROWS), pl.ds(2 * h * HD, HD)], sem.at[p, h]))
                copies.append(pltpu.make_async_copy(
                    kv.at[pl.ds(ROWS, ROWS), pl.ds(h * HD, HD)],
                    v_scr.at[pl.ds(p * ROWS, ROWS), pl.ds(2 * h * HD, HD)], sem.at[p, 2 + h]))
        for c in copies:
            c.start()
        v_scr[:, HD:2 * HD] = jnp.ones((KEYS, HD), jnp.bfloat16)
        lane0 = lax.broadcasted_iota(jnp.int32, (ROWS, HD), 1) == 0
        for p in range(PIECES):
            hidden = jnp.logical_or(x < p % NX, jnp.logical_and(zh == 0, p == NX))
            bias = jnp.where(hidden, LOW, 0.0)
            k_scr[pl.ds(p * ROWS, ROWS), HD:2 * HD] = jnp.where(lane0, bias, 0.0).astype(jnp.bfloat16)
        for c in copies:
            c.wait()

    one = jnp.where(lax.broadcasted_iota(jnp.int32, (TILE, HD), 1) == 0, 1.0, 0.0).astype(jnp.bfloat16)
    row = lax.broadcasted_iota(jnp.int32, (TILE, CHUNK), 0)
    col = lax.broadcasted_iota(jnp.int32, (TILE, CHUNK), 1)
    seen = jnp.logical_or(col >= ROWS, col - row <= i * TILE - y * ROWS)
    coded = []
    for h in range(2):
        qh = q_ref[:, :, h * HD:(h + 1) * HD].reshape(TILE, HD)
        qh = jnp.concatenate([qh, one] if h == 0 else [one, qh], axis=1)
        top = jnp.full((TILE, HD), LOW, jnp.float32)
        for c in range(KEYS // CHUNK):
            kc = k_scr[pl.ds(c * CHUNK, CHUNK), h * HD:(h + 2) * HD]
            s = lax.dot_general(qh, kc, (((1,), (1,)), ((), ())), preferred_element_type=jnp.float32)
            if c == 0:
                s = jnp.where(seen, s, LOW)
            s_scr[:, c * CHUNK:(c + 1) * CHUNK] = s
            top = jnp.maximum(top, jnp.maximum(s[:, :HD], s[:, HD:]))
        top = jnp.broadcast_to(jnp.max(top, axis=1, keepdims=True), (TILE, HD))
        off = jnp.maximum(top, -1e20) * C2
        off = jnp.concatenate([off, off], axis=1)
        acc = None
        for c in range(KEYS // CHUNK):
            p = jnp.exp2(s_scr[:, c * CHUNK:(c + 1) * CHUNK] * C2 - off).astype(jnp.bfloat16)
            d = lax.dot_general(p, v_scr[pl.ds(c * CHUNK, CHUNK), h * HD:(h + 2) * HD],
                                (((1,), (0,)), ((), ())), preferred_element_type=jnp.float32)
            acc = d if acc is None else acc + d
        main, total = (acc[:, :HD], acc[:, HD:]) if h == 0 else (acc[:, HD:], acc[:, :HD])
        total = jnp.maximum(total, 1e-30)
        out_ref[:, 0:ROWS, h * HD:(h + 1) * HD] = (main / total).astype(jnp.bfloat16).reshape(
            SHARDS, ROWS, HD)
        stat = jnp.where(top > 0.5 * LOW, top * SCALE + jnp.log(total), LOW)
        coded.append([code_stat(stat[j * ROWS:(j + 1) * ROWS]) for j in range(SHARDS)])
    for j in range(SHARDS):
        out_ref[j, ROWS:, 0:ROWS] = jnp.concatenate([coded[0][j], coded[1][j]], axis=0).astype(jnp.bfloat16)
        out_ref[j, ROWS:, ROWS:] = jnp.zeros((STAT_ROWS, WIDTH - ROWS), jnp.bfloat16)


def partial_attention(place, q_all, pieces):
    return pl.pallas_call(
        partial_kernel,
        out_shape=jax.ShapeDtypeStruct((NY, ROWS + STAT_ROWS, WIDTH), jnp.bfloat16),
        grid=(NY // SHARDS,),
        in_specs=[IN_SMEM, pl.BlockSpec((SHARDS, ROWS, WIDTH), lambda i: (i, 0, 0))] + [ANY] * PIECES,
        out_specs=pl.BlockSpec((SHARDS, ROWS + STAT_ROWS, WIDTH), lambda i: (i, 0, 0)),
        scratch_shapes=[
            pltpu.VMEM((KEYS, 3 * HD), jnp.bfloat16),
            pltpu.VMEM((KEYS, 3 * HD), jnp.bfloat16),
            pltpu.VMEM((TILE, KEYS), jnp.float32),
            pltpu.SemaphoreType.DMA((PIECES, 4)),
        ],
        cost_estimate=pl.CostEstimate(
            flops=4 * NY * ROWS * KEYS * WIDTH, bytes_accessed=4 * KEYS * WIDTH,
            transcendentals=2 * NY * ROWS * KEYS),
        compiler_params=pltpu.CompilerParams(vmem_limit_bytes=18 << 20),
        name="partial_attention",
    )(place, q_all, *pieces)


def combine_kernel(part_ref, out_ref):
    parts = [part_ref.at[j] for j in range(NY)]
    stats = []
    for h in range(2):
        rows = []
        for part in parts:
            b = part[pl.ds(ROWS, STAT_ROWS), :].astype(jnp.float32)[8 * h:8 * h + 8]
            rows.append(b[0:1] + b[1:2] + b[2:3])
        top = functools.reduce(jnp.maximum, rows)
        ws = [jnp.exp(r - top) for r in rows]
        inv = 1.0 / functools.reduce(jnp.add, ws)
        stats += [w * inv for w in ws]
    cols = jnp.transpose(jnp.concatenate(stats, axis=0))[0:ROWS]
    for h in range(2):
        acc = jnp.zeros((ROWS, HD), jnp.float32)
        for j, part in enumerate(parts):
            o = part[0:ROWS, h * HD:(h + 1) * HD].astype(jnp.float32)
            acc = acc + o * cols[:, h * NY + j:h * NY + j + 1]
        out_ref[:, h * HD:(h + 1) * HD] = acc.astype(jnp.bfloat16)


def combine(parts):
    return pl.pallas_call(
        combine_kernel,
        out_shape=jax.ShapeDtypeStruct((ROWS, WIDTH), jnp.bfloat16),
        in_specs=[IN_VMEM],
        out_specs=IN_VMEM,
        compiler_params=pltpu.CompilerParams(vmem_limit_bytes=8 << 20),
        name="combine",
    )(parts)


def split_kernel(place_ref, nkv_ref, *refs):
    outs, sem = refs[:GROUPS - 1], refs[GROUPS - 1]
    me = place_ref[3]
    copies = []
    for k in range(1, GROUPS):
        at = pl.multiple_of((me ^ k) * GROUP_WIDTH, GROUP_WIDTH)
        copies.append(pltpu.make_async_copy(
            nkv_ref.at[0, :, pl.ds(at, GROUP_WIDTH)], outs[k - 1], sem.at[k - 1]))
    for c in copies:
        c.start()
    for c in copies:
        c.wait()


def split_groups(place, neighbour_kv):
    piece = jax.ShapeDtypeStruct((BLOCK, GROUP_WIDTH), jnp.bfloat16)
    return pl.pallas_call(
        split_kernel,
        out_shape=[piece] * (GROUPS - 1),
        in_specs=[IN_SMEM, ANY],
        out_specs=[IN_VMEM] * (GROUPS - 1),
        scratch_shapes=[pltpu.SemaphoreType.DMA((GROUPS - 1,))],
        compiler_params=pltpu.CompilerParams(vmem_limit_bytes=8 << 20),
        name="split_groups",
    )(place, neighbour_kv)


def cross_kernel(place_ref, map_ref, q_ref, nkv_ref, *refs):
    pieces = refs[:GROUPS - 1]
    out_ref, scr, sem = refs[GROUPS - 1:]
    me = place_ref[3]
    at = pl.multiple_of(me * GROUP_WIDTH, GROUP_WIDTH)
    copies = [pltpu.make_async_copy(
        nkv_ref.at[0, :, pl.ds(at, GROUP_WIDTH)], scr.at[0], sem.at[0])]
    for k in range(1, GROUPS):
        copies.append(pltpu.make_async_copy(pieces[k - 1], scr.at[k], sem.at[k]))
    for c in copies:
        c.start()
    for c in copies:
        c.wait()
    for c in range(STRETCHES):
        slots = [map_ref[c, r] ^ me for r in range(2)]
        keep = place_ref[4] * STRETCHES + c > 0
        for h in range(2):
            qh = q_ref[c * STRETCH:(c + 1) * STRETCH, h * HD:(h + 1) * HD]
            s = [lax.dot_general(qh, scr[slot, :, h * HD:(h + 1) * HD], (((1,), (1,)), ((), ())),
                                 preferred_element_type=jnp.float32) for slot in slots]
            top = jnp.max(jnp.maximum(s[0], s[1]), axis=1, keepdims=True) * C2
            p = [jnp.exp2(a * C2 - top) for a in s]
            total = jnp.sum(p[0] + p[1], axis=1, keepdims=True)
            o = sum(lax.dot_general(a.astype(jnp.bfloat16), scr[slot, :, WIDTH + h * HD:WIDTH + (h + 1) * HD],
                                    (((1,), (0,)), ((), ())), preferred_element_type=jnp.float32)
                    for a, slot in zip(p, slots))
            out_ref[c * STRETCH:(c + 1) * STRETCH, h * HD:(h + 1) * HD] = jnp.where(
                keep, o / total, 0.0).astype(jnp.bfloat16)


def cross(place, neighbour_map, query_cross, neighbour_kv, pieces):
    return pl.pallas_call(
        cross_kernel,
        out_shape=jax.ShapeDtypeStruct((ROWS, WIDTH), jnp.bfloat16),
        in_specs=[IN_SMEM, IN_SMEM, IN_VMEM, ANY] + [ANY] * (GROUPS - 1),
        out_specs=IN_VMEM,
        scratch_shapes=[
            pltpu.VMEM((GROUPS, BLOCK, GROUP_WIDTH), jnp.bfloat16),
            pltpu.SemaphoreType.DMA((GROUPS,)),
        ],
        cost_estimate=pl.CostEstimate(
            flops=8 * ROWS * 2 * BLOCK * WIDTH, bytes_accessed=2 << 20, transcendentals=4 * ROWS * BLOCK),
        compiler_params=pltpu.CompilerParams(vmem_limit_bytes=8 << 20),
        name="cross_attention",
    )(place, neighbour_map, query_cross, neighbour_kv, *pieces)


def on_device(query_self, key_self, value_self, query_cross, neighbour_kv, neighbour_map):
    x, zh, y = lax.axis_index("x"), lax.axis_index("zh"), lax.axis_index("y")
    me = lax.axis_index(("sec", "head"))
    place = jnp.stack([x, zh, y, me, lax.axis_index(("x", "zh", "y"))]).astype(jnp.int32)

    kv = jnp.concatenate([key_self, value_self], axis=0)
    kvz = lax.ppermute(kv, "zh", [(0, 1), (1, 0)])
    pieces = [kv]
    for k in range(1, NX):
        pieces.append(lax.ppermute(kv, "x", [(a, a + k) for a in range(NX - k)]))
    pieces.append(kvz)
    for k in range(1, NX):
        pieces.append(lax.ppermute(kvz, "x", [(a, a + k) for a in range(NX - k)]))
    q_all = lax.all_to_all(
        jnp.broadcast_to(query_self[None], (NY, ROWS, WIDTH)), "y", 0, 0, tiled=True)

    outgoing = split_groups(place, neighbour_kv)
    arrived = [lax.ppermute(outgoing[k - 1], ("sec", "head"), [(a, a ^ k) for a in range(GROUPS)])
               for k in range(1, GROUPS)]

    parts = partial_attention(place, q_all, pieces)
    received = lax.all_to_all(parts, "y", 0, 0, tiled=True)
    self_out = combine(received)
    cross_out = cross(place, neighbour_map, query_cross, neighbour_kv, arrived)
    return (self_out, cross_out)


def solution(mesh):
    fine = Mesh(mesh.devices.reshape(2, NX, NZ, NY, 4), ("sec", "x", "zh", "y", "head"))
    rows, cols = ("x", "zh", "y"), ("sec", "head")
    return jax.shard_map(
        on_device,
        mesh=fine,
        in_specs=(
            P(rows, cols),
            P(rows, cols),
            P(rows, cols),
            P(rows, cols),
            P(("sec", "x", "zh", "y", "head"), None, None),
            P(rows, None),
        ),
        out_specs=(P(rows, cols), P(rows, cols)),
        check_vma=False,
    )
```

time: 133 us -> 101 us (0.76)
  the two profiles are of different devices: /device:TPU:7 before, /device:TPU:79 now
where the time goes in v2:
time: 101 us; the launch traced here: 100 us
  starting transfers between devices  54.1 us (54%)
  waiting for transfers between devices  25.1 us (25%)
  Pallas kernels  17.2 us (17%)
  local copies, waits for them, and re-layouts  2.92 us (3%)
    ppermute x7, starting transfers between devices, on_device(): lax.ppermute(outgoing[k - 1], ('sec', 'head'), [(a, a ^ k) for a in range...  22.7 us
    pallas_call x1, Pallas kernels, partial_attention(): pl.pallas_call(partial_kernel, out_shape=jax.ShapeDtypeStruct((NY, ROWS +...  10.3 us
    ppermute x7, waiting for transfers between devices, on_device(): lax.ppermute(outgoing[k - 1], ('sec', 'head'), [(a, a ^ k) for a in range...  9.85 us
    ppermute x1, starting transfers between devices, on_device(): kvz = lax.ppermute(kv, 'zh', [(0, 1), (1, 0)])  9.73 us
    all_to_all x1, starting transfers between devices, on_device(): lax.all_to_all(jnp.broadcast_to(query_self[None], (NY, ROWS, WIDTH)), 'y'...  7.12 us
    all_to_all x1, starting transfers between devices, on_device(): received = lax.all_to_all(parts, 'y', 0, 0, tiled=True)  6.79 us
    ppermute x3, waiting for transfers between devices, on_device(): pieces.append(lax.ppermute(kvz, 'x', [(a, a + k) for a in range(NX - k)]))  6.07 us
    ppermute x3, waiting for transfers between devices, on_device(): pieces.append(lax.ppermute(kv, 'x', [(a, a + k) for a in range(NX - k)]))  5.69 us
  transfers between devices with their start and end apart: 16, of which 5 were waited for; matrix products, arithmetic and copies ran while one was open for 0% of the time, Pallas kernels for 6%

profile of v2, /device:TPU:79, one launch (start us, length us, event | category | flops | bytes accessed | tf_op | source)
XLA Modules:
  0.0 100.1 jit_solution(16845874114394198005)
XLA Ops:
  0.6 1.8 %broadcast_in_dim.2 = bf16[8,192,256]{2,1,0:T(8,128)(2,1)} broadcast(bf16[192,256]{1,0:T(8,128)(2,1)} %param.6), dimensions={1,2} | broadcast | bytes 884736 | tf_op jit(solution)/shard_map/broadcast_in_dim | solution.py:250
  2.5 0.0 copy-start.2
  2.5 7.1 %all-to-all-start = ((bf16[8,192,256]{2,1,0:T(8,128)(2,1)}), bf16[8,192,256]{2,1,0:T(8,128)(2,1)S(1)}, u32[]{:S(2)}, u32[]{:S(2)}) async-start(bf16[8,192,256]{2,1,0:T(8,128)(2,1)} %broadcast_in_dim.2), calls=%async_computation | async-start | bytes 1572864 | tf_op jit(solution)/shard_map/all_to_all | solution.py:249
  9.6 0.0 copy-done.2
  9.6 0.0 copy-start.3
  9.6 0.9 copy-done.3
  10.5 9.7 %collective-permute-start.3 = (bf16[384,256]{1,0:T(8,128)(2,1)S(1)}, bf16[384,256]{1,0:T(8,128)(2,1)S(1)}, u32[]{:S(2)}, u32[]{:S(2)}) collective-permute-start(bf16[384,256]{1,0:T(8,128)(2,1)S(1)} %constant_dynamic-update-slice_fusion.refs_0_), channel_id=1, source_target_pairs={{0,32},{32,0},{1,33},{33,1},{2,34},{34,2},{3,35},{35,3},{4,36},{36... | collective-permute-start | bytes 589832 | tf_op jit(solution)/shard_map/ppermute | solution.py:242
  20.2 1.3 %collective-permute-start = (bf16[384,256]{1,0:T(8,128)(2,1)S(1)}, bf16[384,256]{1,0:T(8,128)(2,1)S(1)}, u32[]{:S(2)}, u32[]{:S(2)}) collective-permute-start(bf16[384,256]{1,0:T(8,128)(2,1)S(1)} %constant_dynamic-update-slice_fusion.refs_0_), channel_id=1, source_target_pairs={{0,64},{64,128},{128,192},{1,65},{65,129},{129,193},{2,66},{66,130... | collective-permute-start | bytes 589832 | tf_op jit(solution)/shard_map/ppermute | solution.py:245
  21.5 1.3 %collective-permute-start.1 = (bf16[384,256]{1,0:T(8,128)(2,1)S(1)}, bf16[384,256]{1,0:T(8,128)(2,1)S(1)}, u32[]{:S(2)}, u32[]{:S(2)}) collective-permute-start(bf16[384,256]{1,0:T(8,128)(2,1)S(1)} %constant_dynamic-update-slice_fusion.refs_0_), channel_id=1, source_target_pairs={{0,128},{64,192},{1,129},{65,193},{2,130},{66,194},{3,131},{67,195... | collective-permute-start | bytes 589832 | tf_op jit(solution)/shard_map/ppermute | solution.py:245
  22.8 1.3 %collective-permute-start.2 = (bf16[384,256]{1,0:T(8,128)(2,1)S(1)}, bf16[384,256]{1,0:T(8,128)(2,1)S(1)}, u32[]{:S(2)}, u32[]{:S(2)}) collective-permute-start(bf16[384,256]{1,0:T(8,128)(2,1)S(1)} %constant_dynamic-update-slice_fusion.refs_0_), channel_id=1, source_target_pairs={{0,192},{1,193},{2,194},{3,195},{4,196},{5,197},{6,198},{7,199},{8... | collective-permute-start | bytes 589832 | tf_op jit(solution)/shard_map/ppermute | solution.py:245
  24.1 3.5 %collective-permute-done.3.refs_4_ = bf16[384,256]{1,0:T(8,128)(2,1)S(1)} collective-permute-done((bf16[384,256]{1,0:T(8,128)(2,1)S(1)}, bf16[384,256]{1,0:T(8,128)(2,1)S(1)}, u32[]{:S(2)}, u32[]{:S(2)}) %collective-permute-start.3) | collective-permute-done | bytes 196640 | tf_op jit(solution)/shard_map/ppermute | solution.py:242
  27.6 1.3 %collective-permute-start.4 = (bf16[384,256]{1,0:T(8,128)(2,1)S(1)}, bf16[384,256]{1,0:T(8,128)(2,1)S(1)}, u32[]{:S(2)}, u32[]{:S(2)}) collective-permute-start(bf16[384,256]{1,0:T(8,128)(2,1)S(1)} %collective-permute-done.3.refs_4_), channel_id=1, source_target_pairs={{0,64},{64,128},{128,192},{1,65},{65,129},{129,193},{2,66},{66,130... | collective-permute-start | bytes 589832 | tf_op jit(solution)/shard_map/ppermute | solution.py:248
  28.9 1.3 %collective-permute-start.5 = (bf16[384,256]{1,0:T(8,128)(2,1)S(1)}, bf16[384,256]{1,0:T(8,128)(2,1)S(1)}, u32[]{:S(2)}, u32[]{:S(2)}) collective-permute-start(bf16[384,256]{1,0:T(8,128)(2,1)S(1)} %collective-permute-done.3.refs_4_), channel_id=1, source_target_pairs={{0,128},{64,192},{1,129},{65,193},{2,130},{66,194},{3,131},{67,195... | collective-permute-start | bytes 589832 | tf_op jit(solution)/shard_map/ppermute | solution.py:248
  30.2 0.0 collective-permute-done.refs_1_
  30.2 1.3 %collective-permute-start.6 = (bf16[384,256]{1,0:T(8,128)(2,1)S(1)}, bf16[384,256]{1,0:T(8,128)(2,1)S(1)}, u32[]{:S(2)}, u32[]{:S(2)}) collective-permute-start(bf16[384,256]{1,0:T(8,128)(2,1)S(1)} %collective-permute-done.3.refs_4_), channel_id=1, source_target_pairs={{0,192},{1,193},{2,194},{3,195},{4,196},{5,197},{6,198},{7,199},{8... | collective-permute-start | bytes 589832 | tf_op jit(solution)/shard_map/ppermute | solution.py:248
  31.5 0.1 stack.23.place_ref
  31.6 0.0 collective-permute-done.1.refs_2_
  31.6 5.7 %collective-permute-done.2.refs_3_ = bf16[384,256]{1,0:T(8,128)(2,1)S(1)} collective-permute-done((bf16[384,256]{1,0:T(8,128)(2,1)S(1)}, bf16[384,256]{1,0:T(8,128)(2,1)S(1)}, u32[]{:S(2)}, u32[]{:S(2)}) %collective-permute-start.2) | collective-permute-done | bytes 196640 | tf_op jit(solution)/shard_map/ppermute | solution.py:245
  37.3 0.0 collective-permute-done.4.refs_5_
  37.3 0.0 collective-permute-done.5.refs_6_
  37.3 6.1 %collective-permute-done.6.refs_7_ = bf16[384,256]{1,0:T(8,128)(2,1)S(1)} collective-permute-done((bf16[384,256]{1,0:T(8,128)(2,1)S(1)}, bf16[384,256]{1,0:T(8,128)(2,1)S(1)}, u32[]{:S(2)}, u32[]{:S(2)}) %collective-permute-start.6) | collective-permute-done | bytes 196640 | tf_op jit(solution)/shard_map/ppermute | solution.py:248
  43.4 0.0 all-to-all-done.q_ref
  43.4 10.3 %partial_attention.1 = bf16[8,208,256]{2,1,0:T(8,128)(2,1)} custom-call(s32[5]{0:T(128)S(1)} %stack.23.place_ref, bf16[8,192,256]{2,1,0:T(8,128)(2,1)S(1)} %all-to-all-done.q_ref, bf16[384,256]{1,0:T(8,128)(2,1)S(1)} %constant_dynamic-update-slice_fusion.refs_0_, bf16[384,256]{1,0:T(8,128)(2,1)S(1)} %collective-permute-done.refs_1_, ...), custom_call_target="tpu_custom_call" | custom-call | flops 2415919104 | bytes 1572864 | tf_op jit(solution)/shard_map/partial_attention/pallas_call | solution.py:110
  53.7 0.0 copy-start
  53.7 6.8 %all-to-all-start.1 = ((bf16[8,208,256]{2,1,0:T(8,128)(2,1)}), bf16[8,208,256]{2,1,0:T(8,128)(2,1)S(1)}, u32[]{:S(2)}, u32[]{:S(2)}) async-start(bf16[8,208,256]{2,1,0:T(8,128)(2,1)} %partial_attention.1), calls=%async_computation.1 | async-start | bytes 1703936 | tf_op jit(solution)/shard_map/all_to_all | solution.py:257
  60.5 0.0 copy-done
  60.5 1.4 %split_groups.1 = (bf16[128,512]{1,0:T(8,128)(2,1)S(1)}, bf16[128,512]{1,0:T(8,128)(2,1)S(1)}, bf16[128,512]{1,0:T(8,128)(2,1)}, bf16[128,512]{1,0:T(8,128)(2,1)...) custom-call(s32[5]{0:T(128)S(1)} %stack.23.place_ref, ...), custom_call_target="tpu_custom_call" | custom-call | tf_op jit(solution)/shard_map/split_groups/pallas_call | solution.py:178
  61.9 3.2 %collective-permute-start.7 = (bf16[128,512]{1,0:T(8,128)(2,1)S(1)}, bf16[128,512]{1,0:T(8,128)(2,1)S(1)}, u32[]{:S(2)}, u32[]{:S(2)}) collective-permute-start(bf16[128,512]{1,0:T(8,128)(2,1)S(1)} %get-tuple-element.9), channel_id=1, source_target_pairs={{0,1},{1,0},{2,3},{3,2},{256,257},{257,256},{258,259},{259,258},{4... | collective-permute-start | bytes 393224 | tf_op jit(solution)/shard_map/ppermute | solution.py:253
  65.1 5.1 %collective-permute-start.8 = (bf16[128,512]{1,0:T(8,128)(2,1)S(1)}, bf16[128,512]{1,0:T(8,128)(2,1)S(1)}, u32[]{:S(2)}, u32[]{:S(2)}) collective-permute-start(bf16[128,512]{1,0:T(8,128)(2,1)S(1)} %get-tuple-element.10), channel_id=1, source_target_pairs={{0,2},{1,3},{2,0},{3,1},{256,258},{257,259},{258,256},{259,257},{4... | collective-permute-start | bytes 393224 | tf_op jit(solution)/shard_map/ppermute | solution.py:253
  70.2 1.9 %collective-permute-start.9 = (bf16[128,512]{1,0:T(8,128)(2,1)}, bf16[128,512]{1,0:T(8,128)(2,1)S(1)}, u32[]{:S(2)}, u32[]{:S(2)}) collective-permute-start(bf16[128,512]{1,0:T(8,128)(2,1)} %get-tuple-element.11), channel_id=1, source_target_pairs={{0,3},{1,2},{2,1},{3,0},{256,259},{257,258},{258,257},{259,256},{4... | collective-permute-start | bytes 393224 | tf_op jit(solution)/shard_map/ppermute | solution.py:253
  72.2 3.5 %collective-permute-start.10 = (bf16[128,512]{1,0:T(8,128)(2,1)S(1)}, bf16[128,512]{1,0:T(8,128)(2,1)S(1)}, u32[]{:S(2)}, u32[]{:S(2)}) collective-permute-start(bf16[128,512]{1,0:T(8,128)(2,1)S(1)} %get-tuple-element.12), channel_id=1, source_target_pairs={{0,256},{1,257},{2,258},{3,259},{256,0},{257,1},{258,2},{259,3},{4... | collective-permute-start | bytes 393224 | tf_op jit(solution)/shard_map/ppermute | solution.py:253
  75.7 3.0 %collective-permute-start.11 = (bf16[128,512]{1,0:T(8,128)(2,1)S(1)}, bf16[128,512]{1,0:T(8,128)(2,1)S(1)}, u32[]{:S(2)}, u32[]{:S(2)}) collective-permute-start(bf16[128,512]{1,0:T(8,128)(2,1)S(1)} %get-tuple-element.13), channel_id=1, source_target_pairs={{0,257},{1,256},{2,259},{3,258},{256,1},{257,0},{258,3},{259,2},{4... | collective-permute-start | bytes 393224 | tf_op jit(solution)/shard_map/ppermute | solution.py:253
  78.7 0.0 collective-permute-done.7.refs_0_
  78.7 0.0 copy-start.4
  78.7 4.0 %collective-permute-start.12 = (bf16[128,512]{1,0:T(8,128)(2,1)S(1)}, bf16[128,512]{1,0:T(8,128)(2,1)S(1)}, u32[]{:S(2)}, u32[]{:S(2)}) collective-permute-start(bf16[128,512]{1,0:T(8,128)(2,1)S(1)} %get-tuple-element.14), channel_id=1, source_target_pairs={{0,258},{1,259},{2,256},{3,257},{256,2},{257,3},{258,0},{259,1},{4... | collective-permute-start | bytes 393224 | tf_op jit(solution)/shard_map/ppermute | solution.py:253
  82.7 0.0 collective-permute-done.8.refs_1_
  82.8 1.9 %collective-permute-start.13 = (bf16[128,512]{1,0:T(8,128)(2,1)S(1)}, bf16[128,512]{1,0:T(8,128)(2,1)S(1)}, u32[]{:S(2)}, u32[]{:S(2)}) collective-permute-start(bf16[128,512]{1,0:T(8,128)(2,1)S(1)} %get-tuple-element.15), channel_id=1, source_target_pairs={{0,259},{1,258},{2,257},{3,256},{256,3},{257,2},{258,1},{259,0},{4... | collective-permute-start | bytes 393224 | tf_op jit(solution)/shard_map/ppermute | solution.py:253
  84.7 0.0 copy-done.4
  84.7 0.1 copy.8.map_ref
  84.8 0.0 collective-permute-done.9.refs_2_
  84.8 0.0 collective-permute-done.10.refs_3_
  84.8 0.0 collective-permute-done.11.refs_4_
  84.8 6.7 %collective-permute-done.12.refs_5_ = bf16[128,512]{1,0:T(8,128)(2,1)S(1)} collective-permute-done((bf16[128,512]{1,0:T(8,128)(2,1)S(1)}, bf16[128,512]{1,0:T(8,128)(2,1)S(1)}, u32[]{:S(2)}, u32[]{:S(2)}) %collective-permute-start.12) | collective-permute-done | bytes 131104 | tf_op jit(solution)/shard_map/ppermute | solution.py:253
  91.5 3.2 %collective-permute-done.13.refs_6_ = bf16[128,512]{1,0:T(8,128)(2,1)S(1)} collective-permute-done((bf16[128,512]{1,0:T(8,128)(2,1)S(1)}, bf16[128,512]{1,0:T(8,128)(2,1)S(1)}, u32[]{:S(2)}, u32[]{:S(2)}) %collective-permute-start.13) | collective-permute-done | bytes 131104 | tf_op jit(solution)/shard_map/ppermute | solution.py:253
  94.6 0.0 copy-done.1
  94.6 4.1 %cross_attention.1 = bf16[192,256]{1,0:T(8,128)(2,1)} custom-call(s32[5]{0:T(128)S(1)} %stack.23.place_ref, s32[3,2]{1,0:T(4,128)S(1)} %copy.8.map_ref, bf16[192,256]{1,0:T(8,128)(2,1)S(1)} %copy-done.1, bf16[1,128,4096]{2,1,0:T(8,128)(2,1)S(1)} %copy-done, bf16[128,512]{1,0:T(8,128)(2,1)S(1)} %collective-permute-done.7.refs_0_, ...), custom_call_target="tpu_custom_call" | custom-call | flops 100663296 | bytes 2097152 | tf_op jit(solution)/shard_map/cross_attention/pallas_call | solution.py:220
  98.8 0.0 all-to-all-done.1.part_ref
  98.8 1.3 %combine.1 = bf16[192,256]{1,0:T(8,128)(2,1)} custom-call(bf16[8,208,256]{2,1,0:T(8,128)(2,1)S(1)} %all-to-all-done.1.part_ref), custom_call_target="tpu_custom_call" | custom-call | tf_op jit(solution)/shard_map/combine/pallas_call | solution.py:152
  (3 shorter events, 0.0 us)
Async XLA Ops:
  2.5 7.1 %copy-start.2 = (bf16[192,256]{1,0:T(8,128)(2,1)S(1)}, bf16[192,256]{1,0:T(8,128)(2,1)}, u32[]{:S(2)}) copy-start(bf16[192,256]{1,0:T(8,128)(2,1)} %param.7) | copy-start | bytes 294916
  2.5 40.9 %all-to-all-start = ((bf16[8,192,256]{2,1,0:T(8,128)(2,1)}), bf16[8,192,256]{2,1,0:T(8,128)(2,1)S(1)}, u32[]{:S(2)}, u32[]{:S(2)}) async-start(bf16[8,192,256]{2,1,0:T(8,128)(2,1)} %broadcast_in_dim.2), calls=%async_computation | async-start | bytes 1572864 | tf_op jit(solution)/shard_map/all_to_all | solution.py:249
  9.6 0.9 copy-start.3
  10.5 17.1 %collective-permute-start.3 = (bf16[384,256]{1,0:T(8,128)(2,1)S(1)}, bf16[384,256]{1,0:T(8,128)(2,1)S(1)}, u32[]{:S(2)}, u32[]{:S(2)}) collective-permute-start(bf16[384,256]{1,0:T(8,128)(2,1)S(1)} %constant_dynamic-update-slice_fusion.refs_0_), channel_id=1, source_target_pairs={{0,32},{32,0},{1,33},{33,1},{2,34},{34,2},{3,35},{35,3},{4,36},{36... | collective-permute-start | bytes 589832 | tf_op jit(solution)/shard_map/ppermute | solution.py:242
  20.2 10.0 %collective-permute-start = (bf16[384,256]{1,0:T(8,128)(2,1)S(1)}, bf16[384,256]{1,0:T(8,128)(2,1)S(1)}, u32[]{:S(2)}, u32[]{:S(2)}) collective-permute-start(bf16[384,256]{1,0:T(8,128)(2,1)S(1)} %constant_dynamic-update-slice_fusion.refs_0_), channel_id=1, source_target_pairs={{0,64},{64,128},{128,192},{1,65},{65,129},{129,193},{2,66},{66,130... | collective-permute-start | bytes 589832 | tf_op jit(solution)/shard_map/ppermute | solution.py:245
  21.5 10.1 %collective-permute-start.1 = (bf16[384,256]{1,0:T(8,128)(2,1)S(1)}, bf16[384,256]{1,0:T(8,128)(2,1)S(1)}, u32[]{:S(2)}, u32[]{:S(2)}) collective-permute-start(bf16[384,256]{1,0:T(8,128)(2,1)S(1)} %constant_dynamic-update-slice_fusion.refs_0_), channel_id=1, source_target_pairs={{0,128},{64,192},{1,129},{65,193},{2,130},{66,194},{3,131},{67,195... | collective-permute-start | bytes 589832 | tf_op jit(solution)/shard_map/ppermute | solution.py:245
  22.8 14.5 %collective-permute-start.2 = (bf16[384,256]{1,0:T(8,128)(2,1)S(1)}, bf16[384,256]{1,0:T(8,128)(2,1)S(1)}, u32[]{:S(2)}, u32[]{:S(2)}) collective-permute-start(bf16[384,256]{1,0:T(8,128)(2,1)S(1)} %constant_dynamic-update-slice_fusion.refs_0_), channel_id=1, source_target_pairs={{0,192},{1,193},{2,194},{3,195},{4,196},{5,197},{6,198},{7,199},{8... | collective-permute-start | bytes 589832 | tf_op jit(solution)/shard_map/ppermute | solution.py:245
  27.6 9.7 %collective-permute-start.4 = (bf16[384,256]{1,0:T(8,128)(2,1)S(1)}, bf16[384,256]{1,0:T(8,128)(2,1)S(1)}, u32[]{:S(2)}, u32[]{:S(2)}) collective-permute-start(bf16[384,256]{1,0:T(8,128)(2,1)S(1)} %collective-permute-done.3.refs_4_), channel_id=1, source_target_pairs={{0,64},{64,128},{128,192},{1,65},{65,129},{129,193},{2,66},{66,130... | collective-permute-start | bytes 589832 | tf_op jit(solution)/shard_map/ppermute | solution.py:248
  28.9 8.4 %collective-permute-start.5 = (bf16[384,256]{1,0:T(8,128)(2,1)S(1)}, bf16[384,256]{1,0:T(8,128)(2,1)S(1)}, u32[]{:S(2)}, u32[]{:S(2)}) collective-permute-start(bf16[384,256]{1,0:T(8,128)(2,1)S(1)} %collective-permute-done.3.refs_4_), channel_id=1, source_target_pairs={{0,128},{64,192},{1,129},{65,193},{2,130},{66,194},{3,131},{67,195... | collective-permute-start | bytes 589832 | tf_op jit(solution)/shard_map/ppermute | solution.py:248
  30.2 13.2 %collective-permute-start.6 = (bf16[384,256]{1,0:T(8,128)(2,1)S(1)}, bf16[384,256]{1,0:T(8,128)(2,1)S(1)}, u32[]{:S(2)}, u32[]{:S(2)}) collective-permute-start(bf16[384,256]{1,0:T(8,128)(2,1)S(1)} %collective-permute-done.3.refs_4_), channel_id=1, source_target_pairs={{0,192},{1,193},{2,194},{3,195},{4,196},{5,197},{6,198},{7,199},{8... | collective-permute-start | bytes 589832 | tf_op jit(solution)/shard_map/ppermute | solution.py:248
  53.7 6.8 %copy-start = (bf16[1,128,4096]{2,1,0:T(8,128)(2,1)S(1)}, bf16[1,128,4096]{2,1,0:T(8,128)(2,1)}, u32[]{:S(2)}) copy-start(bf16[1,128,4096]{2,1,0:T(8,128)(2,1)} %nkv_ref.3) | copy-start | bytes 3145732
  53.7 45.1 %all-to-all-start.1 = ((bf16[8,208,256]{2,1,0:T(8,128)(2,1)}), bf16[8,208,256]{2,1,0:T(8,128)(2,1)S(1)}, u32[]{:S(2)}, u32[]{:S(2)}) async-start(bf16[8,208,256]{2,1,0:T(8,128)(2,1)} %partial_attention.1), calls=%async_computation.1 | async-start | bytes 1703936 | tf_op jit(solution)/shard_map/all_to_all | solution.py:257
  60.5 34.1 %copy-start.1 = (bf16[192,256]{1,0:T(8,128)(2,1)S(1)}, bf16[192,256]{1,0:T(8,128)(2,1)}, u32[]{:S(2)}) copy-start(bf16[192,256]{1,0:T(8,128)(2,1)} %q_ref.1) | copy-start | bytes 294916
  61.9 16.8 %collective-permute-start.7 = (bf16[128,512]{1,0:T(8,128)(2,1)S(1)}, bf16[128,512]{1,0:T(8,128)(2,1)S(1)}, u32[]{:S(2)}, u32[]{:S(2)}) collective-permute-start(bf16[128,512]{1,0:T(8,128)(2,1)S(1)} %get-tuple-element.9), channel_id=1, source_target_pairs={{0,1},{1,0},{2,3},{3,2},{256,257},{257,256},{258,259},{259,258},{4... | collective-permute-start | bytes 393224 | tf_op jit(solution)/shard_map/ppermute | solution.py:253
  65.1 17.6 %collective-permute-start.8 = (bf16[128,512]{1,0:T(8,128)(2,1)S(1)}, bf16[128,512]{1,0:T(8,128)(2,1)S(1)}, u32[]{:S(2)}, u32[]{:S(2)}) collective-permute-start(bf16[128,512]{1,0:T(8,128)(2,1)S(1)} %get-tuple-element.10), channel_id=1, source_target_pairs={{0,2},{1,3},{2,0},{3,1},{256,258},{257,259},{258,256},{259,257},{4... | collective-permute-start | bytes 393224 | tf_op jit(solution)/shard_map/ppermute | solution.py:253
  70.2 14.6 %collective-permute-start.9 = (bf16[128,512]{1,0:T(8,128)(2,1)}, bf16[128,512]{1,0:T(8,128)(2,1)S(1)}, u32[]{:S(2)}, u32[]{:S(2)}) collective-permute-start(bf16[128,512]{1,0:T(8,128)(2,1)} %get-tuple-element.11), channel_id=1, source_target_pairs={{0,3},{1,2},{2,1},{3,0},{256,259},{257,258},{258,257},{259,256},{4... | collective-permute-start | bytes 393224 | tf_op jit(solution)/shard_map/ppermute | solution.py:253
  72.2 12.6 %collective-permute-start.10 = (bf16[128,512]{1,0:T(8,128)(2,1)S(1)}, bf16[128,512]{1,0:T(8,128)(2,1)S(1)}, u32[]{:S(2)}, u32[]{:S(2)}) collective-permute-start(bf16[128,512]{1,0:T(8,128)(2,1)S(1)} %get-tuple-element.12), channel_id=1, source_target_pairs={{0,256},{1,257},{2,258},{3,259},{256,0},{257,1},{258,2},{259,3},{4... | collective-permute-start | bytes 393224 | tf_op jit(solution)/shard_map/ppermute | solution.py:253
  75.7 9.1 %collective-permute-start.11 = (bf16[128,512]{1,0:T(8,128)(2,1)S(1)}, bf16[128,512]{1,0:T(8,128)(2,1)S(1)}, u32[]{:S(2)}, u32[]{:S(2)}) collective-permute-start(bf16[128,512]{1,0:T(8,128)(2,1)S(1)} %get-tuple-element.13), channel_id=1, source_target_pairs={{0,257},{1,256},{2,259},{3,258},{256,1},{257,0},{258,3},{259,2},{4... | collective-permute-start | bytes 393224 | tf_op jit(solution)/shard_map/ppermute | solution.py:253
  78.7 6.0 %copy-start.4 = (s32[3,2]{0,1:T(2,128)S(1)}, s32[3,2]{0,1:T(2,128)}, u32[]{:S(2)}) copy-start(s32[3,2]{0,1:T(2,128)} %param.11) | copy-start | bytes 76
  78.7 12.7 %collective-permute-start.12 = (bf16[128,512]{1,0:T(8,128)(2,1)S(1)}, bf16[128,512]{1,0:T(8,128)(2,1)S(1)}, u32[]{:S(2)}, u32[]{:S(2)}) collective-permute-start(bf16[128,512]{1,0:T(8,128)(2,1)S(1)} %get-tuple-element.14), channel_id=1, source_target_pairs={{0,258},{1,259},{2,256},{3,257},{256,2},{257,3},{258,0},{259,1},{4... | collective-permute-start | bytes 393224 | tf_op jit(solution)/shard_map/ppermute | solution.py:253
  82.8 11.9 %collective-permute-start.13 = (bf16[128,512]{1,0:T(8,128)(2,1)S(1)}, bf16[128,512]{1,0:T(8,128)(2,1)S(1)}, u32[]{:S(2)}, u32[]{:S(2)}) collective-permute-start(bf16[128,512]{1,0:T(8,128)(2,1)S(1)} %get-tuple-element.15), channel_id=1, source_target_pairs={{0,259},{1,258},{2,257},{3,256},{256,3},{257,2},{258,1},{259,0},{4... | collective-permute-start | bytes 393224 | tf_op jit(solution)/shard_map/ppermute | solution.py:253

commit v3 on v2

--- a/solution.py
+++ b/solution.py
@@ -20,6 +20,7 @@
 CHUNK = 256
 BLOCK = 128
 GROUPS = 8
+HEADS = 4
 GROUP_WIDTH = 512
 STRETCHES = ROWS // STRETCH
 LOW = -1e30
@@ -159,48 +160,55 @@
     )(parts)
 
 
-def split_kernel(place_ref, nkv_ref, *refs):
-    outs, sem = refs[:GROUPS - 1], refs[GROUPS - 1]
+def split_kernel(place_ref, nkv_ref, twin_ref, *refs):
+    outs, sem = refs[:HEADS - 1], refs[HEADS - 1]
     me = place_ref[3]
     copies = []
-    for k in range(1, GROUPS):
+    for k in range(1, HEADS):
         at = pl.multiple_of((me ^ k) * GROUP_WIDTH, GROUP_WIDTH)
+        near = pl.multiple_of(((me ^ k) & (HEADS - 1)) * GROUP_WIDTH, GROUP_WIDTH)
         copies.append(pltpu.make_async_copy(
-            nkv_ref.at[0, :, pl.ds(at, GROUP_WIDTH)], outs[k - 1], sem.at[k - 1]))
+            nkv_ref.at[0, :, pl.ds(at, GROUP_WIDTH)], outs[k - 1].at[0], sem.at[k - 1, 0]))
+        copies.append(pltpu.make_async_copy(
+            twin_ref.at[:, pl.ds(near, GROUP_WIDTH)], outs[k - 1].at[1], sem.at[k - 1, 1]))
     for c in copies:
         c.start()
     for c in copies:
         c.wait()
 
 
-def split_groups(place, neighbour_kv):
-    piece = jax.ShapeDtypeStruct((BLOCK, GROUP_WIDTH), jnp.bfloat16)
+def split_groups(place, neighbour_kv, twin):
+    piece = jax.ShapeDtypeStruct((2, BLOCK, GROUP_WIDTH), jnp.bfloat16)
     return pl.pallas_call(
         split_kernel,
-        out_shape=[piece] * (GROUPS - 1),
-        in_specs=[IN_SMEM, ANY],
-        out_specs=[IN_VMEM] * (GROUPS - 1),
-        scratch_shapes=[pltpu.SemaphoreType.DMA((GROUPS - 1,))],
+        out_shape=[piece] * (HEADS - 1),
+        in_specs=[IN_SMEM, ANY, ANY],
+        out_specs=[IN_VMEM] * (HEADS - 1),
+        scratch_shapes=[pltpu.SemaphoreType.DMA((HEADS - 1, 2))],
         compiler_params=pltpu.CompilerParams(vmem_limit_bytes=8 << 20),
         name="split_groups",
-    )(place, neighbour_kv)
-
-
-def cross_kernel(place_ref, map_ref, q_ref, nkv_ref, *refs):
-    pieces = refs[:GROUPS - 1]
-    out_ref, scr, sem = refs[GROUPS - 1:]
+    )(place, neighbour_kv, twin)
+
+
+def cross_kernel(place_ref, map_ref, q_ref, nkv_ref, twin_ref, *refs):
+    pieces = refs[:HEADS - 1]
+    out_ref, scr, sem = refs[HEADS - 1:]
     me = place_ref[3]
     at = pl.multiple_of(me * GROUP_WIDTH, GROUP_WIDTH)
-    copies = [pltpu.make_async_copy(
-        nkv_ref.at[0, :, pl.ds(at, GROUP_WIDTH)], scr.at[0], sem.at[0])]
-    for k in range(1, GROUPS):
-        copies.append(pltpu.make_async_copy(pieces[k - 1], scr.at[k], sem.at[k]))
+    near = pl.multiple_of((me & (HEADS - 1)) * GROUP_WIDTH, GROUP_WIDTH)
+    copies = [
+        pltpu.make_async_copy(nkv_ref.at[0, :, pl.ds(at, GROUP_WIDTH)], scr.at[0], sem.at[0]),
+        pltpu.make_async_copy(twin_ref.at[:, pl.ds(near, GROUP_WIDTH)], scr.at[1], sem.at[1]),
+    ]
+    for k in range(1, HEADS):
+        copies.append(pltpu.make_async_copy(pieces[k - 1], scr.at[pl.ds(2 * k, 2)], sem.at[2 * k]))
     for c in copies:
         c.start()
     for c in copies:
         c.wait()
     for c in range(STRETCHES):
-        slots = [map_ref[c, r] ^ me for r in range(2)]
+        flips = [map_ref[c, r] ^ me for r in range(2)]
+        slots = [(f & (HEADS - 1)) * 2 + ((f >> 2) & 1) for f in flips]
         keep = place_ref[4] * STRETCHES + c > 0
         for h in range(2):
             qh = q_ref[c * STRETCH:(c + 1) * STRETCH, h * HD:(h + 1) * HD]
@@ -216,11 +224,11 @@
                 keep, o / total, 0.0).astype(jnp.bfloat16)
 
 
-def cross(place, neighbour_map, query_cross, neighbour_kv, pieces):
+def cross(place, neighbour_map, query_cross, neighbour_kv, twin, pieces):
     return pl.pallas_call(
         cross_kernel,
         out_shape=jax.ShapeDtypeStruct((ROWS, WIDTH), jnp.bfloat16),
-        in_specs=[IN_SMEM, IN_SMEM, IN_VMEM, ANY] + [ANY] * (GROUPS - 1),
+        in_specs=[IN_SMEM, IN_SMEM, IN_VMEM, ANY, ANY] + [ANY] * (HEADS - 1),
         out_specs=IN_VMEM,
         scratch_shapes=[
             pltpu.VMEM((GROUPS, BLOCK, GROUP_WIDTH), jnp.bfloat16),
@@ -230,7 +238,7 @@
             flops=8 * ROWS * 2 * BLOCK * WIDTH, bytes_accessed=2 << 20, transcendentals=4 * ROWS * BLOCK),
         compiler_params=pltpu.CompilerParams(vmem_limit_bytes=8 << 20),
         name="cross_attention",
-    )(place, neighbour_map, query_cross, neighbour_kv, *pieces)
+    )(place, neighbour_map, query_cross, neighbour_kv, twin, *pieces)
 
 
 def on_device(query_self, key_self, value_self, query_cross, neighbour_kv, neighbour_map):
@@ -249,14 +257,19 @@
     q_all = lax.all_to_all(
         jnp.broadcast_to(query_self[None], (NY, ROWS, WIDTH)), "y", 0, 0, tiled=True)
 
-    outgoing = split_groups(place, neighbour_kv)
-    arrived = [lax.ppermute(outgoing[k - 1], ("sec", "head"), [(a, a ^ k) for a in range(GROUPS)])
-               for k in range(1, GROUPS)]
+    half = HEADS * GROUP_WIDTH
+    mine = lax.dynamic_slice(
+        neighbour_kv[0], (0, (1 - lax.axis_index("sec")) * half), (BLOCK, half))
+    twin = lax.ppermute(mine, "sec", [(0, 1), (1, 0)])
+    outgoing = split_groups(place, neighbour_kv, twin)
+    arrived = [lax.ppermute(outgoing[k - 1], "head", [(a, a ^ k) for a in range(HEADS)])
+               for k in range(1, HEADS)]
 
     parts = partial_attention(place, q_all, pieces)
+    cross_out = cross(place, neighbour_map, query_cross, neighbour_kv, twin, arrived)
+    parts, cross_out = lax.optimization_barrier((parts, cross_out))
     received = lax.all_to_all(parts, "y", 0, 0, tiled=True)
     self_out = combine(received)
-    cross_out = cross(place, neighbour_map, query_cross, neighbour_kv, arrived)
     return (self_out, cross_out)
 
 

time: 101 us -> 115 us (1.14)
  the two profiles are of different devices: /device:TPU:79 before, /device:TPU:6 now
where the time goes in v3:
time: 115 us; the launch traced here: 114 us
  starting transfers between devices  37.9 us (33%)
  blocking collectives  30.8 us (27%)
  waiting for transfers between devices  25.1 us (22%)
  Pallas kernels  15.5 us (13%)
  local copies, waits for them, and re-layouts  3.78 us (3%)
    all_to_all x1, blocking collectives, on_device(): received = lax.all_to_all(parts, 'y', 0, 0, tiled=True)  30.8 us
    ppermute x1, waiting for transfers between devices, on_device(): kvz = lax.ppermute(kv, 'zh', [(0, 1), (1, 0)])  14.1 us
    ppermute x3, starting transfers between devices, on_device(): lax.ppermute(outgoing[k - 1], 'head', [(a, a ^ k) for a in range(HEADS)])  12.4 us
    pallas_call x1, Pallas kernels, partial_attention(): pl.pallas_call(partial_kernel, out_shape=jax.ShapeDtypeStruct((NY, ROWS +...  10.5 us
    ppermute x1, starting transfers between devices, on_device(): kvz = lax.ppermute(kv, 'zh', [(0, 1), (1, 0)])  8.74 us
    all_to_all x1, starting transfers between devices, on_device(): lax.all_to_all(jnp.broadcast_to(query_self[None], (NY, ROWS, WIDTH)), 'y'...  7.1 us
    ppermute x3, waiting for transfers between devices, on_device(): pieces.append(lax.ppermute(kv, 'x', [(a, a + k) for a in range(NX - k)]))  6.05 us
    ppermute x3, starting transfers between devices, on_device(): pieces.append(lax.ppermute(kvz, 'x', [(a, a + k) for a in range(NX - k)]))  3.88 us
  transfers between devices with their start and end apart: 12, of which 4 were waited for; matrix products, arithmetic and copies ran while one was open for 0% of the time, Pallas kernels for 3%

profile of v3, /device:TPU:6, one launch (start us, length us, event | category | flops | bytes accessed | tf_op | source)
XLA Modules:
  0.0 114.0 jit_solution(9937439549526076965)
XLA Ops:
  0.6 0.0 copy-start
  0.6 1.9 %broadcast_in_dim.2 = bf16[8,192,256]{2,1,0:T(8,128)(2,1)} broadcast(bf16[192,256]{1,0:T(8,128)(2,1)} %param.6), dimensions={1,2} | broadcast | bytes 884736 | tf_op jit(solution)/shard_map/broadcast_in_dim | solution.py:258
  2.6 7.1 %all-to-all-start = ((bf16[8,192,256]{2,1,0:T(8,128)(2,1)}), bf16[8,192,256]{2,1,0:T(8,128)(2,1)S(1)}, u32[]{:S(2)}, u32[]{:S(2)}) async-start(bf16[8,192,256]{2,1,0:T(8,128)(2,1)} %broadcast_in_dim.2), calls=%async_computation | async-start | bytes 1572864 | tf_op jit(solution)/shard_map/all_to_all | solution.py:257
  9.7 0.0 copy-done
  9.7 0.0 copy-start.4
  9.7 1.9 %collective-permute-start.7 = (bf16[128,2048]{1,0:T(8,128)(2,1)S(1)}, bf16[128,2048]{1,0:T(8,128)(2,1)S(1)}, u32[]{:S(2)}, u32[]{:S(2)}) collective-permute-start(bf16[128,2048]{1,0:T(8,128)(2,1)S(1)} %dynamic-slice_bitcast_fusion), channel_id=1, source_target_pairs={{0,256},{256,0},{1,257},{257,1},{2,258},{258,2},{3,259},{259,3},{4... | collective-permute-start | bytes 1572872 | tf_op jit(solution)/shard_map/ppermute | solution.py:263
  11.7 0.1 stack.23.place_ref
  11.8 0.0 copy-done.4
  11.8 0.0 copy-start.5
  11.8 1.8 %collective-permute-done.7.twin_ref = bf16[128,2048]{1,0:T(8,128)(2,1)S(1)} collective-permute-done((bf16[128,2048]{1,0:T(8,128)(2,1)S(1)}, bf16[128,2048]{1,0:T(8,128)(2,1)S(1)}, u32[]{:S(2)}, u32[]{:S(2)}) %collective-permute-start.7) | collective-permute-done | bytes 524320 | tf_op jit(solution)/shard_map/ppermute | solution.py:263
  13.5 0.7 split_groups.1
  14.3 4.3 %collective-permute-start.8 = (bf16[2,128,512]{2,1,0:T(8,128)(2,1)S(1)}, bf16[2,128,512]{2,1,0:T(8,128)(2,1)S(1)}, u32[]{:S(2)}, u32[]{:S(2)}) collective-permute-start(bf16[2,128,512]{2,1,0:T(8,128)(2,1)S(1)} %get-tuple-element.7), channel_id=1, source_target_pairs={{0,1},{1,0},{2,3},{3,2},{4,5},{5,4},{6,7},{7,6},{8,9},{9,8},{10,11... | collective-permute-start | bytes 786440 | tf_op jit(solution)/shard_map/ppermute | solution.py:265
  18.6 6.1 %collective-permute-start.9 = (bf16[2,128,512]{2,1,0:T(8,128)(2,1)S(1)}, bf16[2,128,512]{2,1,0:T(8,128)(2,1)S(1)}, u32[]{:S(2)}, u32[]{:S(2)}) collective-permute-start(bf16[2,128,512]{2,1,0:T(8,128)(2,1)S(1)} %get-tuple-element.8), channel_id=1, source_target_pairs={{0,2},{1,3},{2,0},{3,1},{4,6},{5,7},{6,4},{7,5},{8,10},{9,11},{10,... | collective-permute-start | bytes 786440 | tf_op jit(solution)/shard_map/ppermute | solution.py:265
  24.7 0.0 copy-start.6
  24.7 0.0 copy-start.1
  24.7 2.1 %collective-permute-start.10 = (bf16[2,128,512]{2,1,0:T(8,128)(2,1)S(1)}, bf16[2,128,512]{2,1,0:T(8,128)(2,1)S(1)}, u32[]{:S(2)}, u32[]{:S(2)}) collective-permute-start(bf16[2,128,512]{2,1,0:T(8,128)(2,1)S(1)} %get-tuple-element.9), channel_id=1, source_target_pairs={{0,3},{1,2},{2,1},{3,0},{4,7},{5,6},{6,5},{7,4},{8,11},{9,10},{10,... | collective-permute-start | bytes 786440 | tf_op jit(solution)/shard_map/ppermute | solution.py:265
  26.7 0.0 copy-done.5
  26.8 1.3 %collective-permute-start = (bf16[384,256]{1,0:T(8,128)(2,1)S(1)}, bf16[384,256]{1,0:T(8,128)(2,1)S(1)}, u32[]{:S(2)}, u32[]{:S(2)}) collective-permute-start(bf16[384,256]{1,0:T(8,128)(2,1)S(1)} %constant_dynamic-update-slice_fusion.refs_0_), channel_id=1, source_target_pairs={{0,64},{64,128},{128,192},{1,65},{65,129},{129,193},{2,66},{66,130... | collective-permute-start | bytes 589832 | tf_op jit(solution)/shard_map/ppermute | solution.py:253
  28.1 8.7 %collective-permute-start.3 = (bf16[384,256]{1,0:T(8,128)(2,1)S(1)}, bf16[384,256]{1,0:T(8,128)(2,1)}, u32[]{:S(2)}, u32[]{:S(2)}) collective-permute-start(bf16[384,256]{1,0:T(8,128)(2,1)S(1)} %constant_dynamic-update-slice_fusion.refs_0_), channel_id=1, source_target_pairs={{0,32},{32,0},{1,33},{33,1},{2,34},{34,2},{3,35},{35,3},{4,36},{36... | collective-permute-start | bytes 589832 | tf_op jit(solution)/shard_map/ppermute | solution.py:250
  36.8 0.0 collective-permute-done.refs_1_
  36.8 0.0 copy-start.2
  36.8 0.7 copy-done.2
  37.5 1.3 %collective-permute-start.1 = (bf16[384,256]{1,0:T(8,128)(2,1)S(1)}, bf16[384,256]{1,0:T(8,128)(2,1)}, u32[]{:S(2)}, u32[]{:S(2)}) collective-permute-start(bf16[384,256]{1,0:T(8,128)(2,1)S(1)} %constant_dynamic-update-slice_fusion.refs_0_), channel_id=1, source_target_pairs={{0,128},{64,192},{1,129},{65,193},{2,130},{66,194},{3,131},{67,195... | collective-permute-start | bytes 589832 | tf_op jit(solution)/shard_map/ppermute | solution.py:253
  38.8 14.1 %collective-permute-done.3.refs_4_ = bf16[384,256]{1,0:T(8,128)(2,1)} collective-permute-done((bf16[384,256]{1,0:T(8,128)(2,1)S(1)}, bf16[384,256]{1,0:T(8,128)(2,1)}, u32[]{:S(2)}, u32[]{:S(2)}) %collective-permute-start.3) | collective-permute-done | bytes 196640 | tf_op jit(solution)/shard_map/ppermute | solution.py:250
  52.9 1.3 %collective-permute-start.2 = (bf16[384,256]{1,0:T(8,128)(2,1)S(1)}, bf16[384,256]{1,0:T(8,128)(2,1)}, u32[]{:S(2)}, u32[]{:S(2)}) collective-permute-start(bf16[384,256]{1,0:T(8,128)(2,1)S(1)} %constant_dynamic-update-slice_fusion.refs_0_), channel_id=1, source_target_pairs={{0,192},{1,193},{2,194},{3,195},{4,196},{5,197},{6,198},{7,199},{8... | collective-permute-start | bytes 589832 | tf_op jit(solution)/shard_map/ppermute | solution.py:253
  54.2 0.0 collective-permute-done.8.refs_0_
  54.2 1.3 %collective-permute-start.4 = (bf16[384,256]{1,0:T(8,128)(2,1)}, bf16[384,256]{1,0:T(8,128)(2,1)}, u32[]{:S(2)}, u32[]{:S(2)}) collective-permute-start(bf16[384,256]{1,0:T(8,128)(2,1)} %collective-permute-done.3.refs_4_), channel_id=1, source_target_pairs={{0,64},{64,128},{128,192},{1,65},{65,129},{129,193},{2,66},{66,130... | collective-permute-start | bytes 589832 | tf_op jit(solution)/shard_map/ppermute | solution.py:256
  55.5 0.0 collective-permute-done.9.refs_1_
  55.5 1.3 %collective-permute-start.5 = (bf16[384,256]{1,0:T(8,128)(2,1)}, bf16[384,256]{1,0:T(8,128)(2,1)}, u32[]{:S(2)}, u32[]{:S(2)}) collective-permute-start(bf16[384,256]{1,0:T(8,128)(2,1)} %collective-permute-done.3.refs_4_), channel_id=1, source_target_pairs={{0,128},{64,192},{1,129},{65,193},{2,130},{66,194},{3,131},{67,195... | collective-permute-start | bytes 589832 | tf_op jit(solution)/shard_map/ppermute | solution.py:256
  56.8 0.0 collective-permute-done.10.refs_2_
  56.8 1.3 %collective-permute-start.6 = (bf16[384,256]{1,0:T(8,128)(2,1)}, bf16[384,256]{1,0:T(8,128)(2,1)}, u32[]{:S(2)}, u32[]{:S(2)}) collective-permute-start(bf16[384,256]{1,0:T(8,128)(2,1)} %collective-permute-done.3.refs_4_), channel_id=1, source_target_pairs={{0,192},{1,193},{2,194},{3,195},{4,196},{5,197},{6,198},{7,199},{8... | collective-permute-start | bytes 589832 | tf_op jit(solution)/shard_map/ppermute | solution.py:256
  58.1 0.0 copy-done.6
  58.1 0.1 copy.8.map_ref
  58.2 0.0 copy-done.1
  58.2 3.0 %cross_attention.1 = bf16[192,256]{1,0:T(8,128)(2,1)} custom-call(s32[5]{0:T(128)S(1)} %stack.23.place_ref, s32[3,2]{1,0:T(4,128)S(1)} %copy.8.map_ref, bf16[192,256]{1,0:T(8,128)(2,1)S(1)} %copy-done.1, bf16[1,128,4096]{2,1,0:T(8,128)(2,1)S(1)} %copy-done, bf16[128,2048]{1,0:T(8,128)(2,1)S(1)} %collective-permute-done.7.twin_ref, ...), custom_call_target="tpu_custom_call" | custom-call | flops 100663296 | bytes 2097152 | tf_op jit(solution)/shard_map/cross_attention/pallas_call | solution.py:228
  61.2 0.0 collective-permute-done.1.refs_2_
  61.3 6.0 %collective-permute-done.2.refs_3_ = bf16[384,256]{1,0:T(8,128)(2,1)} collective-permute-done((bf16[384,256]{1,0:T(8,128)(2,1)S(1)}, bf16[384,256]{1,0:T(8,128)(2,1)}, u32[]{:S(2)}, u32[]{:S(2)}) %collective-permute-start.2) | collective-permute-done | bytes 196640 | tf_op jit(solution)/shard_map/ppermute | solution.py:253
  67.3 0.0 collective-permute-done.4.refs_5_
  67.3 0.0 collective-permute-done.5.refs_6_
  67.3 3.2 %collective-permute-done.6.refs_7_ = bf16[384,256]{1,0:T(8,128)(2,1)} collective-permute-done((bf16[384,256]{1,0:T(8,128)(2,1)}, bf16[384,256]{1,0:T(8,128)(2,1)}, u32[]{:S(2)}, u32[]{:S(2)}) %collective-permute-start.6) | collective-permute-done | bytes 196640 | tf_op jit(solution)/shard_map/ppermute | solution.py:256
  70.5 0.0 all-to-all-done.q_ref
  70.5 0.0 copy-start.3
  70.5 0.9 copy-done.3
  71.5 10.5 %partial_attention.1 = bf16[8,208,256]{2,1,0:T(8,128)(2,1)S(1)} custom-call(s32[5]{0:T(128)S(1)} %stack.23.place_ref, bf16[8,192,256]{2,1,0:T(8,128)(2,1)S(1)} %all-to-all-done.q_ref, bf16[384,256]{1,0:T(8,128)(2,1)S(1)} %constant_dynamic-update-slice_fusion.refs_0_, bf16[384,256]{1,0:T(8,128)(2,1)S(1)} %copy-done.3, ...), custom_call_target="tpu_custom_call" | custom-call | flops 2415919104 | bytes 1572864 | tf_op jit(solution)/shard_map/partial_attention/pallas_call | solution.py:111
  81.9 30.8 %all_to_all.10.part_ref = bf16[8,208,256]{2,1,0:T(8,128)(2,1)S(1)} all-to-all(bf16[8,208,256]{2,1,0:T(8,128)(2,1)S(1)} %partial_attention.1), channel_id=1, replica_groups=mesh['sec'=2,'x'=4,'zh'=2,'y'=8,'head'=4] {'y'}, dimensions={0} | all-to-all | bytes 1703936 | tf_op jit(solution)/shard_map/all_to_all | solution.py:271
  112.7 1.3 %combine.1 = bf16[192,256]{1,0:T(8,128)(2,1)} custom-call(bf16[8,208,256]{2,1,0:T(8,128)(2,1)S(1)} %all_to_all.10.part_ref), custom_call_target="tpu_custom_call" | custom-call | tf_op jit(solution)/shard_map/combine/pallas_call | solution.py:153
  (3 shorter events, 0.1 us)
Async XLA Ops:
  0.6 9.0 %copy-start = (bf16[1,128,4096]{2,1,0:T(8,128)(2,1)S(1)}, bf16[1,128,4096]{2,1,0:T(8,128)(2,1)}, u32[]{:S(2)}) copy-start(bf16[1,128,4096]{2,1,0:T(8,128)(2,1)} %nkv_ref.3) | copy-start | bytes 3145732
  2.6 68.0 %all-to-all-start = ((bf16[8,192,256]{2,1,0:T(8,128)(2,1)}), bf16[8,192,256]{2,1,0:T(8,128)(2,1)S(1)}, u32[]{:S(2)}, u32[]{:S(2)}) async-start(bf16[8,192,256]{2,1,0:T(8,128)(2,1)} %broadcast_in_dim.2), calls=%async_computation | async-start | bytes 1572864 | tf_op jit(solution)/shard_map/all_to_all | solution.py:257
  9.7 2.1 %copy-start.4 = (bf16[192,256]{1,0:T(8,128)(2,1)S(1)}, bf16[192,256]{1,0:T(8,128)(2,1)}, u32[]{:S(2)}) copy-start(bf16[192,256]{1,0:T(8,128)(2,1)} %param.7) | copy-start | bytes 294916
  9.7 3.8 %collective-permute-start.7 = (bf16[128,2048]{1,0:T(8,128)(2,1)S(1)}, bf16[128,2048]{1,0:T(8,128)(2,1)S(1)}, u32[]{:S(2)}, u32[]{:S(2)}) collective-permute-start(bf16[128,2048]{1,0:T(8,128)(2,1)S(1)} %dynamic-slice_bitcast_fusion), channel_id=1, source_target_pairs={{0,256},{256,0},{1,257},{257,1},{2,258},{258,2},{3,259},{259,3},{4... | collective-permute-start | bytes 1572872 | tf_op jit(solution)/shard_map/ppermute | solution.py:263
  11.8 15.0 %copy-start.5 = (bf16[192,256]{1,0:T(8,128)(2,1)S(1)}, bf16[192,256]{1,0:T(8,128)(2,1)}, u32[]{:S(2)}) copy-start(bf16[192,256]{1,0:T(8,128)(2,1)} %param.8) | copy-start | bytes 294916
  14.3 39.9 %collective-permute-start.8 = (bf16[2,128,512]{2,1,0:T(8,128)(2,1)S(1)}, bf16[2,128,512]{2,1,0:T(8,128)(2,1)S(1)}, u32[]{:S(2)}, u32[]{:S(2)}) collective-permute-start(bf16[2,128,512]{2,1,0:T(8,128)(2,1)S(1)} %get-tuple-element.7), channel_id=1, source_target_pairs={{0,1},{1,0},{2,3},{3,2},{4,5},{5,4},{6,7},{7,6},{8,9},{9,8},{10,11... | collective-permute-start | bytes 786440 | tf_op jit(solution)/shard_map/ppermute | solution.py:265
  18.6 36.9 %collective-permute-start.9 = (bf16[2,128,512]{2,1,0:T(8,128)(2,1)S(1)}, bf16[2,128,512]{2,1,0:T(8,128)(2,1)S(1)}, u32[]{:S(2)}, u32[]{:S(2)}) collective-permute-start(bf16[2,128,512]{2,1,0:T(8,128)(2,1)S(1)} %get-tuple-element.8), channel_id=1, source_target_pairs={{0,2},{1,3},{2,0},{3,1},{4,6},{5,7},{6,4},{7,5},{8,10},{9,11},{10,... | collective-permute-start | bytes 786440 | tf_op jit(solution)/shard_map/ppermute | solution.py:265
  24.7 33.4 %copy-start.6 = (s32[3,2]{0,1:T(2,128)S(1)}, s32[3,2]{0,1:T(2,128)}, u32[]{:S(2)}) copy-start(s32[3,2]{0,1:T(2,128)} %param.11) | copy-start | bytes 76
  24.7 33.5 %copy-start.1 = (bf16[192,256]{1,0:T(8,128)(2,1)S(1)}, bf16[192,256]{1,0:T(8,128)(2,1)}, u32[]{:S(2)}) copy-start(bf16[192,256]{1,0:T(8,128)(2,1)} %q_ref.1) | copy-start | bytes 294916
  24.7 32.1 %collective-permute-start.10 = (bf16[2,128,512]{2,1,0:T(8,128)(2,1)S(1)}, bf16[2,128,512]{2,1,0:T(8,128)(2,1)S(1)}, u32[]{:S(2)}, u32[]{:S(2)}) collective-permute-start(bf16[2,128,512]{2,1,0:T(8,128)(2,1)S(1)} %get-tuple-element.9), channel_id=1, source_target_pairs={{0,3},{1,2},{2,1},{3,0},{4,7},{5,6},{6,5},{7,4},{8,11},{9,10},{10,... | collective-permute-start | bytes 786440 | tf_op jit(solution)/shard_map/ppermute | solution.py:265
  26.8 10.1 %collective-permute-start = (bf16[384,256]{1,0:T(8,128)(2,1)S(1)}, bf16[384,256]{1,0:T(8,128)(2,1)S(1)}, u32[]{:S(2)}, u32[]{:S(2)}) collective-permute-start(bf16[384,256]{1,0:T(8,128)(2,1)S(1)} %constant_dynamic-update-slice_fusion.refs_0_), channel_id=1, source_target_pairs={{0,64},{64,128},{128,192},{1,65},{65,129},{129,193},{2,66},{66,130... | collective-permute-start | bytes 589832 | tf_op jit(solution)/shard_map/ppermute | solution.py:253
  28.1 24.8 %collective-permute-start.3 = (bf16[384,256]{1,0:T(8,128)(2,1)S(1)}, bf16[384,256]{1,0:T(8,128)(2,1)}, u32[]{:S(2)}, u32[]{:S(2)}) collective-permute-start(bf16[384,256]{1,0:T(8,128)(2,1)S(1)} %constant_dynamic-update-slice_fusion.refs_0_), channel_id=1, source_target_pairs={{0,32},{32,0},{1,33},{33,1},{2,34},{34,2},{3,35},{35,3},{4,36},{36... | collective-permute-start | bytes 589832 | tf_op jit(solution)/shard_map/ppermute | solution.py:250
  36.8 0.7 copy-start.2
  37.5 23.8 %collective-permute-start.1 = (bf16[384,256]{1,0:T(8,128)(2,1)S(1)}, bf16[384,256]{1,0:T(8,128)(2,1)}, u32[]{:S(2)}, u32[]{:S(2)}) collective-permute-start(bf16[384,256]{1,0:T(8,128)(2,1)S(1)} %constant_dynamic-update-slice_fusion.refs_0_), channel_id=1, source_target_pairs={{0,128},{64,192},{1,129},{65,193},{2,130},{66,194},{3,131},{67,195... | collective-permute-start | bytes 589832 | tf_op jit(solution)/shard_map/ppermute | solution.py:253
  52.9 14.4 %collective-permute-start.2 = (bf16[384,256]{1,0:T(8,128)(2,1)S(1)}, bf16[384,256]{1,0:T(8,128)(2,1)}, u32[]{:S(2)}, u32[]{:S(2)}) collective-permute-start(bf16[384,256]{1,0:T(8,128)(2,1)S(1)} %constant_dynamic-update-slice_fusion.refs_0_), channel_id=1, source_target_pairs={{0,192},{1,193},{2,194},{3,195},{4,196},{5,197},{6,198},{7,199},{8... | collective-permute-start | bytes 589832 | tf_op jit(solution)/shard_map/ppermute | solution.py:253
  54.2 13.1 %collective-permute-start.4 = (bf16[384,256]{1,0:T(8,128)(2,1)}, bf16[384,256]{1,0:T(8,128)(2,1)}, u32[]{:S(2)}, u32[]{:S(2)}) collective-permute-start(bf16[384,256]{1,0:T(8,128)(2,1)} %collective-permute-done.3.refs_4_), channel_id=1, source_target_pairs={{0,64},{64,128},{128,192},{1,65},{65,129},{129,193},{2,66},{66,130... | collective-permute-start | bytes 589832 | tf_op jit(solution)/shard_map/ppermute | solution.py:256
  55.5 11.8 %collective-permute-start.5 = (bf16[384,256]{1,0:T(8,128)(2,1)}, bf16[384,256]{1,0:T(8,128)(2,1)}, u32[]{:S(2)}, u32[]{:S(2)}) collective-permute-start(bf16[384,256]{1,0:T(8,128)(2,1)} %collective-permute-done.3.refs_4_), channel_id=1, source_target_pairs={{0,128},{64,192},{1,129},{65,193},{2,130},{66,194},{3,131},{67,195... | collective-permute-start | bytes 589832 | tf_op jit(solution)/shard_map/ppermute | solution.py:256
  56.8 13.7 %collective-permute-start.6 = (bf16[384,256]{1,0:T(8,128)(2,1)}, bf16[384,256]{1,0:T(8,128)(2,1)}, u32[]{:S(2)}, u32[]{:S(2)}) collective-permute-start(bf16[384,256]{1,0:T(8,128)(2,1)} %collective-permute-done.3.refs_4_), channel_id=1, source_target_pairs={{0,192},{1,193},{2,194},{3,195},{4,196},{5,197},{6,198},{7,199},{8... | collective-permute-start | bytes 589832 | tf_op jit(solution)/shard_map/ppermute | solution.py:256
  70.5 0.9 copy-start.3

commit v4 on v3

--- a/solution.py
+++ b/solution.py
@@ -44,21 +44,22 @@
 
 
 def partial_kernel(place_ref, q_ref, *refs):
-    pieces, out_ref = refs[:PIECES], refs[PIECES]
-    k_scr, v_scr, s_scr, sem = refs[PIECES + 1:]
+    pieces, out_ref = refs[:NX], refs[NX]
+    k_scr, v_scr, s_scr, sem = refs[NX + 1:]
     x, zh, y = place_ref[0], place_ref[1], place_ref[2]
     i = pl.program_id(0)
 
     @pl.when(i == 0)
     def _():
         copies = []
-        for p, kv in enumerate(pieces):
+        for p in range(PIECES):
+            kv, at = pieces[p % NX], p // NX * 2 * ROWS
             for h in range(2):
                 copies.append(pltpu.make_async_copy(
-                    kv.at[pl.ds(0, ROWS), pl.ds(h * HD, HD)],
+                    kv.at[pl.ds(at, ROWS), pl.ds(h * HD, HD)],
                     k_scr.at[pl.ds(p * ROWS, ROWS), pl.ds(2 * h * HD, HD)], sem.at[p, h]))
                 copies.append(pltpu.make_async_copy(
-                    kv.at[pl.ds(ROWS, ROWS), pl.ds(h * HD, HD)],
+                    kv.at[pl.ds(at + ROWS, ROWS), pl.ds(h * HD, HD)],
                     v_scr.at[pl.ds(p * ROWS, ROWS), pl.ds(2 * h * HD, HD)], sem.at[p, 2 + h]))
         for c in copies:
             c.start()
@@ -112,7 +113,7 @@
         partial_kernel,
         out_shape=jax.ShapeDtypeStruct((NY, ROWS + STAT_ROWS, WIDTH), jnp.bfloat16),
         grid=(NY // SHARDS,),
-        in_specs=[IN_SMEM, pl.BlockSpec((SHARDS, ROWS, WIDTH), lambda i: (i, 0, 0))] + [ANY] * PIECES,
+        in_specs=[IN_SMEM, pl.BlockSpec((SHARDS, ROWS, WIDTH), lambda i: (i, 0, 0))] + [ANY] * NX,
         out_specs=pl.BlockSpec((SHARDS, ROWS + STAT_ROWS, WIDTH), lambda i: (i, 0, 0)),
         scratch_shapes=[
             pltpu.VMEM((KEYS, 3 * HD), jnp.bfloat16),
@@ -248,12 +249,10 @@
 
     kv = jnp.concatenate([key_self, value_self], axis=0)
     kvz = lax.ppermute(kv, "zh", [(0, 1), (1, 0)])
-    pieces = [kv]
+    both = jnp.concatenate([kv, kvz], axis=0)
+    pieces = [both]
     for k in range(1, NX):
-        pieces.append(lax.ppermute(kv, "x", [(a, a + k) for a in range(NX - k)]))
-    pieces.append(kvz)
-    for k in range(1, NX):
-        pieces.append(lax.ppermute(kvz, "x", [(a, a + k) for a in range(NX - k)]))
+        pieces.append(lax.ppermute(both, "x", [(a, a + k) for a in range(NX - k)]))
     q_all = lax.all_to_all(
         jnp.broadcast_to(query_self[None], (NY, ROWS, WIDTH)), "y", 0, 0, tiled=True)
 
@@ -267,7 +266,6 @@
 
     parts = partial_attention(place, q_all, pieces)
     cross_out = cross(place, neighbour_map, query_cross, neighbour_kv, twin, arrived)
-    parts, cross_out = lax.optimization_barrier((parts, cross_out))
     received = lax.all_to_all(parts, "y", 0, 0, tiled=True)
     self_out = combine(received)
     return (self_out, cross_out)

time: 115 us -> 111 us (0.965)
  the two profiles are of different devices: /device:TPU:6 before, /device:TPU:142 now
where the time goes in v4:
time: 111 us; the launch traced here: 110 us
  waiting for transfers between devices  51.5 us (46%)
  starting transfers between devices  39.3 us (35%)
  Pallas kernels  16.3 us (15%)
  local copies, waits for them, and re-layouts  2.12 us (2%)
    ppermute x3, waiting for transfers between devices, on_device(): lax.ppermute(outgoing[k - 1], 'head', [(a, a ^ k) for a in range(HEADS)])  20.9 us
    ppermute x3, waiting for transfers between devices, on_device(): pieces.append(lax.ppermute(both, 'x', [(a, a + k) for a in range(NX - k)]))  20.1 us
    pallas_call x1, Pallas kernels, partial_attention(): pl.pallas_call(partial_kernel, out_shape=jax.ShapeDtypeStruct((NY, ROWS +...  10.3 us
    ppermute x3, starting transfers between devices, on_device(): lax.ppermute(outgoing[k - 1], 'head', [(a, a ^ k) for a in range(HEADS)])  9.21 us
    ppermute x1, starting transfers between devices, on_device(): kvz = lax.ppermute(kv, 'zh', [(0, 1), (1, 0)])  9.12 us
    ppermute x1, waiting for transfers between devices, on_device(): kvz = lax.ppermute(kv, 'zh', [(0, 1), (1, 0)])  8.59 us
    all_to_all x1, starting transfers between devices, on_device(): lax.all_to_all(jnp.broadcast_to(query_self[None], (NY, ROWS, WIDTH)), 'y'...  7.68 us
    all_to_all x1, starting transfers between devices, on_device(): received = lax.all_to_all(parts, 'y', 0, 0, tiled=True)  7.35 us
  transfers between devices with their start and end apart: 10, of which 8 were waited for; matrix products, arithmetic and copies ran while one was open for 0% of the time, Pallas kernels for 4%

profile of v4, /device:TPU:142, one launch (start us, length us, event | category | flops | bytes accessed | tf_op | source)
XLA Modules:
  0.0 110.0 jit_solution(12081870026786683920)
XLA Ops:
  0.6 1.8 %broadcast_in_dim.2 = bf16[8,192,256]{2,1,0:T(8,128)(2,1)} broadcast(bf16[192,256]{1,0:T(8,128)(2,1)} %param.6), dimensions={1,2} | broadcast | bytes 884736 | tf_op jit(solution)/shard_map/broadcast_in_dim | solution.py:257
  2.5 0.0 copy-start.2
  2.5 0.0 copy-start.3
  2.5 7.7 %all-to-all-start = ((bf16[8,192,256]{2,1,0:T(8,128)(2,1)}), bf16[8,192,256]{2,1,0:T(8,128)(2,1)S(1)}, u32[]{:S(2)}, u32[]{:S(2)}) async-start(bf16[8,192,256]{2,1,0:T(8,128)(2,1)} %broadcast_in_dim.2), calls=%async_computation | async-start | bytes 1572864 | tf_op jit(solution)/shard_map/all_to_all | solution.py:256
  10.2 0.0 copy-done.2
  10.2 0.0 copy-done.3
  10.2 9.1 %collective-permute-start = (bf16[384,256]{1,0:T(8,128)(2,1)S(1)}, bf16[384,256]{1,0:T(8,128)(2,1)S(1)}, u32[]{:S(2)}, u32[]{:S(2)}) collective-permute-start(bf16[384,256]{1,0:T(8,128)(2,1)S(1)} %pad_maximum_fusion), channel_id=1, source_target_pairs={{0,32},{32,0},{1,33},{33,1},{2,34},{34,2},{3,35},{35,3},{4,36},{36... | collective-permute-start | bytes 589832 | tf_op jit(solution)/shard_map/ppermute | solution.py:251
  19.3 8.6 %collective-permute-done = bf16[384,256]{1,0:T(8,128)(2,1)S(1)} collective-permute-done((bf16[384,256]{1,0:T(8,128)(2,1)S(1)}, bf16[384,256]{1,0:T(8,128)(2,1)S(1)}, u32[]{:S(2)}, u32[]{:S(2)}) %collective-permute-start) | collective-permute-done | bytes 196640 | tf_op jit(solution)/shard_map/ppermute | solution.py:251
  27.9 1.3 %collective-permute-start.1 = (bf16[768,256]{1,0:T(8,128)(2,1)S(1)}, bf16[768,256]{1,0:T(8,128)(2,1)S(1)}, u32[]{:S(2)}, u32[]{:S(2)}) collective-permute-start(bf16[768,256]{1,0:T(8,128)(2,1)S(1)} %constant_dynamic-update-slice_fusion.refs_0_), channel_id=1, source_target_pairs={{0,64},{64,128},{128,192},{1,65},{65,129},{129,193},{2,66},{66,130... | collective-permute-start | bytes 1179656 | tf_op jit(solution)/shard_map/ppermute | solution.py:255
  29.2 1.3 %collective-permute-start.2 = (bf16[768,256]{1,0:T(8,128)(2,1)S(1)}, bf16[768,256]{1,0:T(8,128)(2,1)S(1)}, u32[]{:S(2)}, u32[]{:S(2)}) collective-permute-start(bf16[768,256]{1,0:T(8,128)(2,1)S(1)} %constant_dynamic-update-slice_fusion.refs_0_), channel_id=1, source_target_pairs={{0,128},{64,192},{1,129},{65,193},{2,130},{66,194},{3,131},{67,195... | collective-permute-start | bytes 1179656 | tf_op jit(solution)/shard_map/ppermute | solution.py:255
  30.5 1.3 %collective-permute-start.3 = (bf16[768,256]{1,0:T(8,128)(2,1)S(1)}, bf16[768,256]{1,0:T(8,128)(2,1)S(1)}, u32[]{:S(2)}, u32[]{:S(2)}) collective-permute-start(bf16[768,256]{1,0:T(8,128)(2,1)S(1)} %constant_dynamic-update-slice_fusion.refs_0_), channel_id=1, source_target_pairs={{0,192},{1,193},{2,194},{3,195},{4,196},{5,197},{6,198},{7,199},{8... | collective-permute-start | bytes 1179656 | tf_op jit(solution)/shard_map/ppermute | solution.py:255
  31.9 0.1 stack.23.place_ref
  31.9 8.8 %collective-permute-done.1.refs_1_ = bf16[768,256]{1,0:T(8,128)(2,1)S(1)} collective-permute-done((bf16[768,256]{1,0:T(8,128)(2,1)S(1)}, bf16[768,256]{1,0:T(8,128)(2,1)S(1)}, u32[]{:S(2)}, u32[]{:S(2)}) %collective-permute-start.1) | collective-permute-done | bytes 393248 | tf_op jit(solution)/shard_map/ppermute | solution.py:255
  40.8 2.9 %collective-permute-done.2.refs_2_ = bf16[768,256]{1,0:T(8,128)(2,1)S(1)} collective-permute-done((bf16[768,256]{1,0:T(8,128)(2,1)S(1)}, bf16[768,256]{1,0:T(8,128)(2,1)S(1)}, u32[]{:S(2)}, u32[]{:S(2)}) %collective-permute-start.2) | collective-permute-done | bytes 393248 | tf_op jit(solution)/shard_map/ppermute | solution.py:255
  43.7 8.3 %collective-permute-done.3.refs_3_ = bf16[768,256]{1,0:T(8,128)(2,1)S(1)} collective-permute-done((bf16[768,256]{1,0:T(8,128)(2,1)S(1)}, bf16[768,256]{1,0:T(8,128)(2,1)S(1)}, u32[]{:S(2)}, u32[]{:S(2)}) %collective-permute-start.3) | collective-permute-done | bytes 393248 | tf_op jit(solution)/shard_map/ppermute | solution.py:255
  52.0 0.0 all-to-all-done.q_ref
  52.0 10.3 %partial_attention.1 = bf16[8,208,256]{2,1,0:T(8,128)(2,1)} custom-call(s32[5]{0:T(128)S(1)} %stack.23.place_ref, bf16[8,192,256]{2,1,0:T(8,128)(2,1)S(1)} %all-to-all-done.q_ref, bf16[768,256]{1,0:T(8,128)(2,1)S(1)} %constant_dynamic-update-slice_fusion.refs_0_, bf16[768,256]{1,0:T(8,128)(2,1)S(1)} %collective-permute-done.1.refs_1_, ...), custom_call_target="tpu_custom_call" | custom-call | flops 2415919104 | bytes 1572864 | tf_op jit(solution)/shard_map/partial_attention/pallas_call | solution.py:112
  62.3 0.0 copy-start
  62.3 7.3 %all-to-all-start.1 = ((bf16[8,208,256]{2,1,0:T(8,128)(2,1)}), bf16[8,208,256]{2,1,0:T(8,128)(2,1)S(1)}, u32[]{:S(2)}, u32[]{:S(2)}) async-start(bf16[8,208,256]{2,1,0:T(8,128)(2,1)} %partial_attention.1), calls=%async_computation.1 | async-start | bytes 1703936 | tf_op jit(solution)/shard_map/all_to_all | solution.py:269
  69.7 0.0 copy-done
  69.8 0.0 copy-start.1
  69.8 2.1 %collective-permute-start.4 = (bf16[128,2048]{1,0:T(8,128)(2,1)S(1)}, bf16[128,2048]{1,0:T(8,128)(2,1)S(1)}, u32[]{:S(2)}, u32[]{:S(2)}) collective-permute-start(bf16[128,2048]{1,0:T(8,128)(2,1)S(1)} %dynamic-slice_bitcast_fusion), channel_id=1, source_target_pairs={{0,256},{256,0},{1,257},{257,1},{2,258},{258,2},{3,259},{259,3},{4... | collective-permute-start | bytes 1572872 | tf_op jit(solution)/shard_map/ppermute | solution.py:262
  71.8 1.9 %collective-permute-done.4.twin_ref = bf16[128,2048]{1,0:T(8,128)(2,1)S(1)} collective-permute-done((bf16[128,2048]{1,0:T(8,128)(2,1)S(1)}, bf16[128,2048]{1,0:T(8,128)(2,1)S(1)}, u32[]{:S(2)}, u32[]{:S(2)}) %collective-permute-start.4) | collective-permute-done | bytes 524320 | tf_op jit(solution)/shard_map/ppermute | solution.py:262
  73.7 1.6 %split_groups.1 = (bf16[2,128,512]{2,1,0:T(8,128)(2,1)}, bf16[2,128,512]{2,1,0:T(8,128)(2,1)}, bf16[2,128,512]{2,1,0:T(8,128)(2,1)}) custom-call(s32[5]{0:T(128)S(1)} %stack.23.place_ref, bf16[1,128,4096]{2,1,0:T(8,128)(2,1)S(1)} %copy-done, bf16[128,2048]{1,0:T(8,128)(2,1)S(1)} %collective-permute-done.4.twin_ref), custom_call_target="tpu_custom_call" | custom-call | tf_op jit(solution)/shard_map/split_groups/pallas_call | solution.py:183
  75.3 1.9 %collective-permute-start.5 = (bf16[2,128,512]{2,1,0:T(8,128)(2,1)}, bf16[2,128,512]{2,1,0:T(8,128)(2,1)S(1)}, u32[]{:S(2)}, u32[]{:S(2)}) collective-permute-start(bf16[2,128,512]{2,1,0:T(8,128)(2,1)} %get-tuple-element.5), channel_id=1, source_target_pairs={{0,1},{1,0},{2,3},{3,2},{4,5},{5,4},{6,7},{7,6},{8,9},{9,8},{10,11... | collective-permute-start | bytes 786440 | tf_op jit(solution)/shard_map/ppermute | solution.py:264
  77.3 0.0 copy-start.4
  77.3 1.9 %collective-permute-start.6 = (bf16[2,128,512]{2,1,0:T(8,128)(2,1)}, bf16[2,128,512]{2,1,0:T(8,128)(2,1)S(1)}, u32[]{:S(2)}, u32[]{:S(2)}) collective-permute-start(bf16[2,128,512]{2,1,0:T(8,128)(2,1)} %get-tuple-element.6), channel_id=1, source_target_pairs={{0,2},{1,3},{2,0},{3,1},{4,6},{5,7},{6,4},{7,5},{8,10},{9,11},{10,... | collective-permute-start | bytes 786440 | tf_op jit(solution)/shard_map/ppermute | solution.py:264
  79.2 5.4 %collective-permute-start.7 = (bf16[2,128,512]{2,1,0:T(8,128)(2,1)}, bf16[2,128,512]{2,1,0:T(8,128)(2,1)S(1)}, u32[]{:S(2)}, u32[]{:S(2)}) collective-permute-start(bf16[2,128,512]{2,1,0:T(8,128)(2,1)} %get-tuple-element.7), channel_id=1, source_target_pairs={{0,3},{1,2},{2,1},{3,0},{4,7},{5,6},{6,5},{7,4},{8,11},{9,10},{10,... | collective-permute-start | bytes 786440 | tf_op jit(solution)/shard_map/ppermute | solution.py:264
  84.6 0.0 copy-done.4
  84.6 0.1 copy.8.map_ref
  84.7 1.9 %collective-permute-done.5.refs_0_ = bf16[2,128,512]{2,1,0:T(8,128)(2,1)S(1)} collective-permute-done((bf16[2,128,512]{2,1,0:T(8,128)(2,1)}, bf16[2,128,512]{2,1,0:T(8,128)(2,1)S(1)}, u32[]{:S(2)}, u32[]{:S(2)}) %collective-permute-start.5) | collective-permute-done | bytes 262176 | tf_op jit(solution)/shard_map/ppermute | solution.py:264
  86.6 10.9 %collective-permute-done.6.refs_1_ = bf16[2,128,512]{2,1,0:T(8,128)(2,1)S(1)} collective-permute-done((bf16[2,128,512]{2,1,0:T(8,128)(2,1)}, bf16[2,128,512]{2,1,0:T(8,128)(2,1)S(1)}, u32[]{:S(2)}, u32[]{:S(2)}) %collective-permute-start.6) | collective-permute-done | bytes 262176 | tf_op jit(solution)/shard_map/ppermute | solution.py:264
  97.5 8.1 %collective-permute-done.7.refs_2_ = bf16[2,128,512]{2,1,0:T(8,128)(2,1)S(1)} collective-permute-done((bf16[2,128,512]{2,1,0:T(8,128)(2,1)}, bf16[2,128,512]{2,1,0:T(8,128)(2,1)S(1)}, u32[]{:S(2)}, u32[]{:S(2)}) %collective-permute-start.7) | collective-permute-done | bytes 262176 | tf_op jit(solution)/shard_map/ppermute | solution.py:264
  105.6 0.0 copy-done.1
  105.6 3.0 %cross_attention.1 = bf16[192,256]{1,0:T(8,128)(2,1)} custom-call(s32[5]{0:T(128)S(1)} %stack.23.place_ref, s32[3,2]{1,0:T(4,128)S(1)} %copy.8.map_ref, bf16[192,256]{1,0:T(8,128)(2,1)S(1)} %copy-done.1, bf16[1,128,4096]{2,1,0:T(8,128)(2,1)S(1)} %copy-done, bf16[128,2048]{1,0:T(8,128)(2,1)S(1)} %collective-permute-done.4.twin_ref, ...), custom_call_target="tpu_custom_call" | custom-call | flops 100663296 | bytes 2097152 | tf_op jit(solution)/shard_map/cross_attention/pallas_call | solution.py:229
  108.7 0.0 all-to-all-done.1.part_ref
  108.7 1.3 %combine.1 = bf16[192,256]{1,0:T(8,128)(2,1)} custom-call(bf16[8,208,256]{2,1,0:T(8,128)(2,1)S(1)} %all-to-all-done.1.part_ref), custom_call_target="tpu_custom_call" | custom-call | tf_op jit(solution)/shard_map/combine/pallas_call | solution.py:154
  (5 shorter events, 0.1 us)
Async XLA Ops:
  2.5 7.7 %copy-start.2 = (bf16[192,256]{1,0:T(8,128)(2,1)S(1)}, bf16[192,256]{1,0:T(8,128)(2,1)}, u32[]{:S(2)}) copy-start(bf16[192,256]{1,0:T(8,128)(2,1)} %param.7) | copy-start | bytes 294916
  2.5 7.7 %copy-start.3 = (bf16[192,256]{1,0:T(8,128)(2,1)S(1)}, bf16[192,256]{1,0:T(8,128)(2,1)}, u32[]{:S(2)}) copy-start(bf16[192,256]{1,0:T(8,128)(2,1)} %param.8) | copy-start | bytes 294916
  2.5 49.5 %all-to-all-start = ((bf16[8,192,256]{2,1,0:T(8,128)(2,1)}), bf16[8,192,256]{2,1,0:T(8,128)(2,1)S(1)}, u32[]{:S(2)}, u32[]{:S(2)}) async-start(bf16[8,192,256]{2,1,0:T(8,128)(2,1)} %broadcast_in_dim.2), calls=%async_computation | async-start | bytes 1572864 | tf_op jit(solution)/shard_map/all_to_all | solution.py:256
  10.2 17.7 %collective-permute-start = (bf16[384,256]{1,0:T(8,128)(2,1)S(1)}, bf16[384,256]{1,0:T(8,128)(2,1)S(1)}, u32[]{:S(2)}, u32[]{:S(2)}) collective-permute-start(bf16[384,256]{1,0:T(8,128)(2,1)S(1)} %pad_maximum_fusion), channel_id=1, source_target_pairs={{0,32},{32,0},{1,33},{33,1},{2,34},{34,2},{3,35},{35,3},{4,36},{36... | collective-permute-start | bytes 589832 | tf_op jit(solution)/shard_map/ppermute | solution.py:251
  27.9 12.8 %collective-permute-start.1 = (bf16[768,256]{1,0:T(8,128)(2,1)S(1)}, bf16[768,256]{1,0:T(8,128)(2,1)S(1)}, u32[]{:S(2)}, u32[]{:S(2)}) collective-permute-start(bf16[768,256]{1,0:T(8,128)(2,1)S(1)} %constant_dynamic-update-slice_fusion.refs_0_), channel_id=1, source_target_pairs={{0,64},{64,128},{128,192},{1,65},{65,129},{129,193},{2,66},{66,130... | collective-permute-start | bytes 1179656 | tf_op jit(solution)/shard_map/ppermute | solution.py:255
  29.2 14.4 %collective-permute-start.2 = (bf16[768,256]{1,0:T(8,128)(2,1)S(1)}, bf16[768,256]{1,0:T(8,128)(2,1)S(1)}, u32[]{:S(2)}, u32[]{:S(2)}) collective-permute-start(bf16[768,256]{1,0:T(8,128)(2,1)S(1)} %constant_dynamic-update-slice_fusion.refs_0_), channel_id=1, source_target_pairs={{0,128},{64,192},{1,129},{65,193},{2,130},{66,194},{3,131},{67,195... | collective-permute-start | bytes 1179656 | tf_op jit(solution)/shard_map/ppermute | solution.py:255
  30.5 21.5 %collective-permute-start.3 = (bf16[768,256]{1,0:T(8,128)(2,1)S(1)}, bf16[768,256]{1,0:T(8,128)(2,1)S(1)}, u32[]{:S(2)}, u32[]{:S(2)}) collective-permute-start(bf16[768,256]{1,0:T(8,128)(2,1)S(1)} %constant_dynamic-update-slice_fusion.refs_0_), channel_id=1, source_target_pairs={{0,192},{1,193},{2,194},{3,195},{4,196},{5,197},{6,198},{7,199},{8... | collective-permute-start | bytes 1179656 | tf_op jit(solution)/shard_map/ppermute | solution.py:255
  62.3 7.4 %copy-start = (bf16[1,128,4096]{2,1,0:T(8,128)(2,1)S(1)}, bf16[1,128,4096]{2,1,0:T(8,128)(2,1)}, u32[]{:S(2)}) copy-start(bf16[1,128,4096]{2,1,0:T(8,128)(2,1)} %nkv_ref.3) | copy-start | bytes 3145732
  62.3 46.3 %all-to-all-start.1 = ((bf16[8,208,256]{2,1,0:T(8,128)(2,1)}), bf16[8,208,256]{2,1,0:T(8,128)(2,1)S(1)}, u32[]{:S(2)}, u32[]{:S(2)}) async-start(bf16[8,208,256]{2,1,0:T(8,128)(2,1)} %partial_attention.1), calls=%async_computation.1 | async-start | bytes 1703936 | tf_op jit(solution)/shard_map/all_to_all | solution.py:269
  69.8 35.9 %copy-start.1 = (bf16[192,256]{1,0:T(8,128)(2,1)S(1)}, bf16[192,256]{1,0:T(8,128)(2,1)}, u32[]{:S(2)}) copy-start(bf16[192,256]{1,0:T(8,128)(2,1)} %q_ref.1) | copy-start | bytes 294916
  69.8 3.9 %collective-permute-start.4 = (bf16[128,2048]{1,0:T(8,128)(2,1)S(1)}, bf16[128,2048]{1,0:T(8,128)(2,1)S(1)}, u32[]{:S(2)}, u32[]{:S(2)}) collective-permute-start(bf16[128,2048]{1,0:T(8,128)(2,1)S(1)} %dynamic-slice_bitcast_fusion), channel_id=1, source_target_pairs={{0,256},{256,0},{1,257},{257,1},{2,258},{258,2},{3,259},{259,3},{4... | collective-permute-start | bytes 1572872 | tf_op jit(solution)/shard_map/ppermute | solution.py:262
  75.3 11.3 %collective-permute-start.5 = (bf16[2,128,512]{2,1,0:T(8,128)(2,1)}, bf16[2,128,512]{2,1,0:T(8,128)(2,1)S(1)}, u32[]{:S(2)}, u32[]{:S(2)}) collective-permute-start(bf16[2,128,512]{2,1,0:T(8,128)(2,1)} %get-tuple-element.5), channel_id=1, source_target_pairs={{0,1},{1,0},{2,3},{3,2},{4,5},{5,4},{6,7},{7,6},{8,9},{9,8},{10,11... | collective-permute-start | bytes 786440 | tf_op jit(solution)/shard_map/ppermute | solution.py:264
  77.3 7.3 %copy-start.4 = (s32[3,2]{0,1:T(2,128)S(1)}, s32[3,2]{0,1:T(2,128)}, u32[]{:S(2)}) copy-start(s32[3,2]{0,1:T(2,128)} %param.11) | copy-start | bytes 76
  77.3 20.2 %collective-permute-start.6 = (bf16[2,128,512]{2,1,0:T(8,128)(2,1)}, bf16[2,128,512]{2,1,0:T(8,128)(2,1)S(1)}, u32[]{:S(2)}, u32[]{:S(2)}) collective-permute-start(bf16[2,128,512]{2,1,0:T(8,128)(2,1)} %get-tuple-element.6), channel_id=1, source_target_pairs={{0,2},{1,3},{2,0},{3,1},{4,6},{5,7},{6,4},{7,5},{8,10},{9,11},{10,... | collective-permute-start | bytes 786440 | tf_op jit(solution)/shard_map/ppermute | solution.py:264
  79.2 26.4 %collective-permute-start.7 = (bf16[2,128,512]{2,1,0:T(8,128)(2,1)}, bf16[2,128,512]{2,1,0:T(8,128)(2,1)S(1)}, u32[]{:S(2)}, u32[]{:S(2)}) collective-permute-start(bf16[2,128,512]{2,1,0:T(8,128)(2,1)} %get-tuple-element.7), channel_id=1, source_target_pairs={{0,3},{1,2},{2,1},{3,0},{4,7},{5,6},{6,5},{7,4},{8,11},{9,10},{10,... | collective-permute-start | bytes 786440 | tf_op jit(solution)/shard_map/ppermute | solution.py:264

commit v5 on v3

--- a/solution.py
+++ b/solution.py
@@ -52,13 +52,14 @@
     @pl.when(i == 0)
     def _():
         copies = []
-        for p, kv in enumerate(pieces):
+        for p in range(PIECES):
+            kv, at = pieces[p], 0
             for h in range(2):
                 copies.append(pltpu.make_async_copy(
-                    kv.at[pl.ds(0, ROWS), pl.ds(h * HD, HD)],
+                    kv.at[pl.ds(at, ROWS), pl.ds(h * HD, HD)],
                     k_scr.at[pl.ds(p * ROWS, ROWS), pl.ds(2 * h * HD, HD)], sem.at[p, h]))
                 copies.append(pltpu.make_async_copy(
-                    kv.at[pl.ds(ROWS, ROWS), pl.ds(h * HD, HD)],
+                    kv.at[pl.ds(at + ROWS, ROWS), pl.ds(h * HD, HD)],
                     v_scr.at[pl.ds(p * ROWS, ROWS), pl.ds(2 * h * HD, HD)], sem.at[p, 2 + h]))
         for c in copies:
             c.start()
@@ -241,12 +242,46 @@
     )(place, neighbour_map, query_cross, neighbour_kv, twin, *pieces)
 
 
+def pack_kernel(q_ref, k_ref, v_ref, kv_ref, copies_ref, scr, sem):
+    loads = [pltpu.make_async_copy(ref, scr.at[pl.ds(i * ROWS, ROWS), :], sem.at[i])
+             for i, ref in enumerate((k_ref, v_ref, q_ref))]
+    for c in loads:
+        c.start()
+    loads[0].wait()
+    loads[1].wait()
+    stores = [pltpu.make_async_copy(scr.at[pl.ds(0, 2 * ROWS), :], kv_ref, sem.at[3])]
+    stores[0].start()
+    loads[2].wait()
+    for j in range(NY):
+        stores.append(pltpu.make_async_copy(
+            scr.at[pl.ds(2 * ROWS, ROWS), :], copies_ref.at[j], sem.at[4 + j]))
+        stores[-1].start()
+    for c in stores:
+        c.wait()
+
+
+def pack(query, key, value):
+    return pl.pallas_call(
+        pack_kernel,
+        out_shape=[jax.ShapeDtypeStruct((2 * ROWS, WIDTH), jnp.bfloat16),
+                   jax.ShapeDtypeStruct((NY, ROWS, WIDTH), jnp.bfloat16)],
+        in_specs=[pl.BlockSpec(memory_space=pltpu.HBM)] * 3,
+        out_specs=[ANY] * 2,
+        scratch_shapes=[
+            pltpu.VMEM((3 * ROWS, WIDTH), jnp.bfloat16),
+            pltpu.SemaphoreType.DMA((4 + NY,)),
+        ],
+        compiler_params=pltpu.CompilerParams(vmem_limit_bytes=4 << 20),
+        name="pack",
+    )(query, key, value)
+
+
 def on_device(query_self, key_self, value_self, query_cross, neighbour_kv, neighbour_map):
     x, zh, y = lax.axis_index("x"), lax.axis_index("zh"), lax.axis_index("y")
     me = lax.axis_index(("sec", "head"))
     place = jnp.stack([x, zh, y, me, lax.axis_index(("x", "zh", "y"))]).astype(jnp.int32)
 
-    kv = jnp.concatenate([key_self, value_self], axis=0)
+    kv, copies = pack(query_self, key_self, value_self)
     kvz = lax.ppermute(kv, "zh", [(0, 1), (1, 0)])
     pieces = [kv]
     for k in range(1, NX):
@@ -254,8 +289,7 @@
     pieces.append(kvz)
     for k in range(1, NX):
         pieces.append(lax.ppermute(kvz, "x", [(a, a + k) for a in range(NX - k)]))
-    q_all = lax.all_to_all(
-        jnp.broadcast_to(query_self[None], (NY, ROWS, WIDTH)), "y", 0, 0, tiled=True)
+    q_all = lax.all_to_all(copies, "y", 0, 0, tiled=True)
 
     half = HEADS * GROUP_WIDTH
     mine = lax.dynamic_slice(
@@ -267,7 +301,6 @@
 
     parts = partial_attention(place, q_all, pieces)
     cross_out = cross(place, neighbour_map, query_cross, neighbour_kv, twin, arrived)
-    parts, cross_out = lax.optimization_barrier((parts, cross_out))
     received = lax.all_to_all(parts, "y", 0, 0, tiled=True)
     self_out = combine(received)
     return (self_out, cross_out)

time: 115 us -> 105 us (0.913)
  the two profiles are of different devices: /device:TPU:6 before, /device:TPU:142 now
where the time goes in v5:
time: 105 us; the launch traced here: 104 us
  starting transfers between devices  43 us (41%)
  waiting for transfers between devices  39.3 us (37%)
  Pallas kernels  17.9 us (17%)
  local copies, waits for them, and re-layouts  2.91 us (3%)
    ppermute x3, waiting for transfers between devices, on_device(): lax.ppermute(outgoing[k - 1], 'head', [(a, a ^ k) for a in range(HEADS)])  21.1 us
    pallas_call x1, Pallas kernels, partial_attention(): pl.pallas_call(partial_kernel, out_shape=jax.ShapeDtypeStruct((NY, ROWS +...  10.3 us
    ppermute x3, waiting for transfers between devices, on_device(): pieces.append(lax.ppermute(kvz, 'x', [(a, a + k) for a in range(NX - k)]))  9.53 us
    ppermute x3, starting transfers between devices, on_device(): lax.ppermute(outgoing[k - 1], 'head', [(a, a ^ k) for a in range(HEADS)])  9.21 us
    ppermute x1, starting transfers between devices, on_device(): kvz = lax.ppermute(kv, 'zh', [(0, 1), (1, 0)])  9.11 us
    all_to_all x1, starting transfers between devices, on_device(): q_all = lax.all_to_all(copies, 'y', 0, 0, tiled=True)  7.56 us
    all_to_all x1, starting transfers between devices, on_device(): received = lax.all_to_all(parts, 'y', 0, 0, tiled=True)  7.35 us
    ppermute x1, waiting for transfers between devices, on_device(): kvz = lax.ppermute(kv, 'zh', [(0, 1), (1, 0)])  4.72 us
  transfers between devices with their start and end apart: 13, of which 9 were waited for; matrix products, arithmetic and copies ran while one was open for 0% of the time, Pallas kernels for 5%

profile of v5, /device:TPU:142, one launch (start us, length us, event | category | flops | bytes accessed | tf_op | source)
XLA Modules:
  0.0 104.0 jit_solution(2578899825175862811)
XLA Ops:
  0.6 0.0 copy-start.2
  0.6 0.9 copy-done.2
  1.5 0.0 copy-start.3
  1.5 0.9 copy-done.3
  2.4 0.0 copy-start.4
  2.4 0.9 copy-done.4
  3.3 1.6 %pack.1 = (bf16[384,256]{1,0:T(8,128)(2,1)S(1)}, bf16[8,192,256]{2,1,0:T(8,128)(2,1)}) custom-call(bf16[192,256]{1,0:T(8,128)(2,1)S(1)} %copy-done.2, bf16[192,256]{1,0:T(8,128)(2,1)S(1)} %copy-done.3, bf16[192,256]{1,0:T(8,128)(2,1)S(1)} %copy-done.4), custom_call_target="tpu_custom_call" | custom-call | tf_op jit(solution)/shard_map/pack/pallas_call | solution.py:264
  4.9 7.6 %all-to-all-start = ((bf16[8,192,256]{2,1,0:T(8,128)(2,1)}), bf16[8,192,256]{2,1,0:T(8,128)(2,1)S(1)}, u32[]{:S(2)}, u32[]{:S(2)}) async-start(bf16[8,192,256]{2,1,0:T(8,128)(2,1)} %get-tuple-element.7), calls=%async_computation | async-start | bytes 1572864 | tf_op jit(solution)/shard_map/all_to_all | solution.py:292
  12.5 9.1 %collective-permute-start.3 = (bf16[384,256]{1,0:T(8,128)(2,1)S(1)}, bf16[384,256]{1,0:T(8,128)(2,1)S(1)}, u32[]{:S(2)}, u32[]{:S(2)}) collective-permute-start(bf16[384,256]{1,0:T(8,128)(2,1)S(1)} %get-tuple-element.8.refs_0_), channel_id=1, source_target_pairs={{0,32},{32,0},{1,33},{33,1},{2,34},{34,2},{3,35},{35,3},{4,36},{36... | collective-permute-start | bytes 589832 | tf_op jit(solution)/shard_map/ppermute | solution.py:285
  21.6 1.3 %collective-permute-start = (bf16[384,256]{1,0:T(8,128)(2,1)S(1)}, bf16[384,256]{1,0:T(8,128)(2,1)S(1)}, u32[]{:S(2)}, u32[]{:S(2)}) collective-permute-start(bf16[384,256]{1,0:T(8,128)(2,1)S(1)} %get-tuple-element.8.refs_0_), channel_id=1, source_target_pairs={{0,64},{64,128},{128,192},{1,65},{65,129},{129,193},{2,66},{66,130... | collective-permute-start | bytes 589832 | tf_op jit(solution)/shard_map/ppermute | solution.py:288
  22.9 1.3 %collective-permute-start.1 = (bf16[384,256]{1,0:T(8,128)(2,1)S(1)}, bf16[384,256]{1,0:T(8,128)(2,1)S(1)}, u32[]{:S(2)}, u32[]{:S(2)}) collective-permute-start(bf16[384,256]{1,0:T(8,128)(2,1)S(1)} %get-tuple-element.8.refs_0_), channel_id=1, source_target_pairs={{0,128},{64,192},{1,129},{65,193},{2,130},{66,194},{3,131},{67,195... | collective-permute-start | bytes 589832 | tf_op jit(solution)/shard_map/ppermute | solution.py:288
  24.2 1.3 %collective-permute-start.2 = (bf16[384,256]{1,0:T(8,128)(2,1)S(1)}, bf16[384,256]{1,0:T(8,128)(2,1)S(1)}, u32[]{:S(2)}, u32[]{:S(2)}) collective-permute-start(bf16[384,256]{1,0:T(8,128)(2,1)S(1)} %get-tuple-element.8.refs_0_), channel_id=1, source_target_pairs={{0,192},{1,193},{2,194},{3,195},{4,196},{5,197},{6,198},{7,199},{8... | collective-permute-start | bytes 589832 | tf_op jit(solution)/shard_map/ppermute | solution.py:288
  25.5 4.7 %collective-permute-done.3.refs_4_ = bf16[384,256]{1,0:T(8,128)(2,1)S(1)} collective-permute-done((bf16[384,256]{1,0:T(8,128)(2,1)S(1)}, bf16[384,256]{1,0:T(8,128)(2,1)S(1)}, u32[]{:S(2)}, u32[]{:S(2)}) %collective-permute-start.3) | collective-permute-done | bytes 196640 | tf_op jit(solution)/shard_map/ppermute | solution.py:285
  30.2 1.3 %collective-permute-start.4 = (bf16[384,256]{1,0:T(8,128)(2,1)S(1)}, bf16[384,256]{1,0:T(8,128)(2,1)S(1)}, u32[]{:S(2)}, u32[]{:S(2)}) collective-permute-start(bf16[384,256]{1,0:T(8,128)(2,1)S(1)} %collective-permute-done.3.refs_4_), channel_id=1, source_target_pairs={{0,64},{64,128},{128,192},{1,65},{65,129},{129,193},{2,66},{66,130... | collective-permute-start | bytes 589832 | tf_op jit(solution)/shard_map/ppermute | solution.py:291
  31.5 1.3 %collective-permute-start.5 = (bf16[384,256]{1,0:T(8,128)(2,1)S(1)}, bf16[384,256]{1,0:T(8,128)(2,1)S(1)}, u32[]{:S(2)}, u32[]{:S(2)}) collective-permute-start(bf16[384,256]{1,0:T(8,128)(2,1)S(1)} %collective-permute-done.3.refs_4_), channel_id=1, source_target_pairs={{0,128},{64,192},{1,129},{65,193},{2,130},{66,194},{3,131},{67,195... | collective-permute-start | bytes 589832 | tf_op jit(solution)/shard_map/ppermute | solution.py:291
  32.8 0.0 collective-permute-done.refs_1_
  32.8 1.3 %collective-permute-start.6 = (bf16[384,256]{1,0:T(8,128)(2,1)S(1)}, bf16[384,256]{1,0:T(8,128)(2,1)S(1)}, u32[]{:S(2)}, u32[]{:S(2)}) collective-permute-start(bf16[384,256]{1,0:T(8,128)(2,1)S(1)} %collective-permute-done.3.refs_4_), channel_id=1, source_target_pairs={{0,192},{1,193},{2,194},{3,195},{4,196},{5,197},{6,198},{7,199},{8... | collective-permute-start | bytes 589832 | tf_op jit(solution)/shard_map/ppermute | solution.py:291
  34.1 0.1 stack.23.place_ref
  34.2 0.0 collective-permute-done.1.refs_2_
  34.2 2.1 %collective-permute-done.2.refs_3_ = bf16[384,256]{1,0:T(8,128)(2,1)S(1)} collective-permute-done((bf16[384,256]{1,0:T(8,128)(2,1)S(1)}, bf16[384,256]{1,0:T(8,128)(2,1)S(1)}, u32[]{:S(2)}, u32[]{:S(2)}) %collective-permute-start.2) | collective-permute-done | bytes 196640 | tf_op jit(solution)/shard_map/ppermute | solution.py:288
  36.3 2.5 %collective-permute-done.4.refs_5_ = bf16[384,256]{1,0:T(8,128)(2,1)S(1)} collective-permute-done((bf16[384,256]{1,0:T(8,128)(2,1)S(1)}, bf16[384,256]{1,0:T(8,128)(2,1)S(1)}, u32[]{:S(2)}, u32[]{:S(2)}) %collective-permute-start.4) | collective-permute-done | bytes 196640 | tf_op jit(solution)/shard_map/ppermute | solution.py:291
  38.8 2.9 %collective-permute-done.5.refs_6_ = bf16[384,256]{1,0:T(8,128)(2,1)S(1)} collective-permute-done((bf16[384,256]{1,0:T(8,128)(2,1)S(1)}, bf16[384,256]{1,0:T(8,128)(2,1)S(1)}, u32[]{:S(2)}, u32[]{:S(2)}) %collective-permute-start.5) | collective-permute-done | bytes 196640 | tf_op jit(solution)/shard_map/ppermute | solution.py:291
  41.7 4.1 %collective-permute-done.6.refs_7_ = bf16[384,256]{1,0:T(8,128)(2,1)S(1)} collective-permute-done((bf16[384,256]{1,0:T(8,128)(2,1)S(1)}, bf16[384,256]{1,0:T(8,128)(2,1)S(1)}, u32[]{:S(2)}, u32[]{:S(2)}) %collective-permute-start.6) | collective-permute-done | bytes 196640 | tf_op jit(solution)/shard_map/ppermute | solution.py:291
  45.8 0.0 all-to-all-done.q_ref
  45.8 10.3 %partial_attention.1 = bf16[8,208,256]{2,1,0:T(8,128)(2,1)} custom-call(s32[5]{0:T(128)S(1)} %stack.23.place_ref, bf16[8,192,256]{2,1,0:T(8,128)(2,1)S(1)} %all-to-all-done.q_ref, bf16[384,256]{1,0:T(8,128)(2,1)S(1)} %get-tuple-element.8.refs_0_, bf16[384,256]{1,0:T(8,128)(2,1)S(1)} %collective-permute-done.refs_1_, ...), custom_call_target="tpu_custom_call" | custom-call | flops 2415919104 | bytes 1572864 | tf_op jit(solution)/shard_map/partial_attention/pallas_call | solution.py:112
  56.2 0.0 copy-start
  56.2 7.3 %all-to-all-start.1 = ((bf16[8,208,256]{2,1,0:T(8,128)(2,1)}), bf16[8,208,256]{2,1,0:T(8,128)(2,1)S(1)}, u32[]{:S(2)}, u32[]{:S(2)}) async-start(bf16[8,208,256]{2,1,0:T(8,128)(2,1)} %partial_attention.1), calls=%async_computation.1 | async-start | bytes 1703936 | tf_op jit(solution)/shard_map/all_to_all | solution.py:304
  63.5 0.0 copy-done
  63.6 0.0 copy-start.1
  63.6 2.1 %collective-permute-start.7 = (bf16[128,2048]{1,0:T(8,128)(2,1)S(1)}, bf16[128,2048]{1,0:T(8,128)(2,1)S(1)}, u32[]{:S(2)}, u32[]{:S(2)}) collective-permute-start(bf16[128,2048]{1,0:T(8,128)(2,1)S(1)} %dynamic-slice_bitcast_fusion), channel_id=1, source_target_pairs={{0,256},{256,0},{1,257},{257,1},{2,258},{258,2},{3,259},{259,3},{4... | collective-permute-start | bytes 1572872 | tf_op jit(solution)/shard_map/ppermute | solution.py:297
  65.6 1.9 %collective-permute-done.7.twin_ref = bf16[128,2048]{1,0:T(8,128)(2,1)S(1)} collective-permute-done((bf16[128,2048]{1,0:T(8,128)(2,1)S(1)}, bf16[128,2048]{1,0:T(8,128)(2,1)S(1)}, u32[]{:S(2)}, u32[]{:S(2)}) %collective-permute-start.7) | collective-permute-done | bytes 524320 | tf_op jit(solution)/shard_map/ppermute | solution.py:297
  67.5 1.7 %split_groups.1 = (bf16[2,128,512]{2,1,0:T(8,128)(2,1)}, bf16[2,128,512]{2,1,0:T(8,128)(2,1)}, bf16[2,128,512]{2,1,0:T(8,128)(2,1)}) custom-call(s32[5]{0:T(128)S(1)} %stack.23.place_ref, bf16[1,128,4096]{2,1,0:T(8,128)(2,1)S(1)} %copy-done, bf16[128,2048]{1,0:T(8,128)(2,1)S(1)} %collective-permute-done.7.twin_ref), custom_call_target="tpu_custom_call" | custom-call | tf_op jit(solution)/shard_map/split_groups/pallas_call | solution.py:183
  69.2 2.3 %collective-permute-start.8 = (bf16[2,128,512]{2,1,0:T(8,128)(2,1)}, bf16[2,128,512]{2,1,0:T(8,128)(2,1)S(1)}, u32[]{:S(2)}, u32[]{:S(2)}) collective-permute-start(bf16[2,128,512]{2,1,0:T(8,128)(2,1)} %get-tuple-element.9), channel_id=1, source_target_pairs={{0,1},{1,0},{2,3},{3,2},{4,5},{5,4},{6,7},{7,6},{8,9},{9,8},{10,11... | collective-permute-start | bytes 786440 | tf_op jit(solution)/shard_map/ppermute | solution.py:299
  71.5 0.0 copy-start.5
  71.5 2.4 %collective-permute-start.9 = (bf16[2,128,512]{2,1,0:T(8,128)(2,1)}, bf16[2,128,512]{2,1,0:T(8,128)(2,1)S(1)}, u32[]{:S(2)}, u32[]{:S(2)}) collective-permute-start(bf16[2,128,512]{2,1,0:T(8,128)(2,1)} %get-tuple-element.10), channel_id=1, source_target_pairs={{0,2},{1,3},{2,0},{3,1},{4,6},{5,7},{6,4},{7,5},{8,10},{9,11},{10,... | collective-permute-start | bytes 786440 | tf_op jit(solution)/shard_map/ppermute | solution.py:299
  73.9 4.5 %collective-permute-start.10 = (bf16[2,128,512]{2,1,0:T(8,128)(2,1)}, bf16[2,128,512]{2,1,0:T(8,128)(2,1)S(1)}, u32[]{:S(2)}, u32[]{:S(2)}) collective-permute-start(bf16[2,128,512]{2,1,0:T(8,128)(2,1)} %get-tuple-element.11), channel_id=1, source_target_pairs={{0,3},{1,2},{2,1},{3,0},{4,7},{5,6},{6,5},{7,4},{8,11},{9,10},{10,... | collective-permute-start | bytes 786440 | tf_op jit(solution)/shard_map/ppermute | solution.py:299
  78.4 0.0 copy-done.5
  78.4 0.1 copy.8.map_ref
  78.5 1.9 %collective-permute-done.8.refs_0_ = bf16[2,128,512]{2,1,0:T(8,128)(2,1)S(1)} collective-permute-done((bf16[2,128,512]{2,1,0:T(8,128)(2,1)}, bf16[2,128,512]{2,1,0:T(8,128)(2,1)S(1)}, u32[]{:S(2)}, u32[]{:S(2)}) %collective-permute-start.8) | collective-permute-done | bytes 262176 | tf_op jit(solution)/shard_map/ppermute | solution.py:299
  80.5 11.7 %collective-permute-done.9.refs_1_ = bf16[2,128,512]{2,1,0:T(8,128)(2,1)S(1)} collective-permute-done((bf16[2,128,512]{2,1,0:T(8,128)(2,1)}, bf16[2,128,512]{2,1,0:T(8,128)(2,1)S(1)}, u32[]{:S(2)}, u32[]{:S(2)}) %collective-permute-start.9) | collective-permute-done | bytes 262176 | tf_op jit(solution)/shard_map/ppermute | solution.py:299
  92.2 7.4 %collective-permute-done.10.refs_2_ = bf16[2,128,512]{2,1,0:T(8,128)(2,1)S(1)} collective-permute-done((bf16[2,128,512]{2,1,0:T(8,128)(2,1)}, bf16[2,128,512]{2,1,0:T(8,128)(2,1)S(1)}, u32[]{:S(2)}, u32[]{:S(2)}) %collective-permute-start.10) | collective-permute-done | bytes 262176 | tf_op jit(solution)/shard_map/ppermute | solution.py:299
  99.6 0.0 copy-done.1
  99.6 3.0 %cross_attention.1 = bf16[192,256]{1,0:T(8,128)(2,1)} custom-call(s32[5]{0:T(128)S(1)} %stack.23.place_ref, s32[3,2]{1,0:T(4,128)S(1)} %copy.8.map_ref, bf16[192,256]{1,0:T(8,128)(2,1)S(1)} %copy-done.1, bf16[1,128,4096]{2,1,0:T(8,128)(2,1)S(1)} %copy-done, bf16[128,2048]{1,0:T(8,128)(2,1)S(1)} %collective-permute-done.7.twin_ref, ...), custom_call_target="tpu_custom_call" | custom-call | flops 100663296 | bytes 2097152 | tf_op jit(solution)/shard_map/cross_attention/pallas_call | solution.py:229
  102.6 0.0 all-to-all-done.1.part_ref
  102.7 1.3 %combine.1 = bf16[192,256]{1,0:T(8,128)(2,1)} custom-call(bf16[8,208,256]{2,1,0:T(8,128)(2,1)S(1)} %all-to-all-done.1.part_ref), custom_call_target="tpu_custom_call" | custom-call | tf_op jit(solution)/shard_map/combine/pallas_call | solution.py:154
  (1 shorter events, 0.0 us)
Async XLA Ops:
  0.6 0.9 copy-start.2
  1.5 0.9 copy-start.3
  2.4 0.9 copy-start.4
  4.9 40.9 %all-to-all-start = ((bf16[8,192,256]{2,1,0:T(8,128)(2,1)}), bf16[8,192,256]{2,1,0:T(8,128)(2,1)S(1)}, u32[]{:S(2)}, u32[]{:S(2)}) async-start(bf16[8,192,256]{2,1,0:T(8,128)(2,1)} %get-tuple-element.7), calls=%async_computation | async-start | bytes 1572864 | tf_op jit(solution)/shard_map/all_to_all | solution.py:292
  12.5 17.7 %collective-permute-start.3 = (bf16[384,256]{1,0:T(8,128)(2,1)S(1)}, bf16[384,256]{1,0:T(8,128)(2,1)S(1)}, u32[]{:S(2)}, u32[]{:S(2)}) collective-permute-start(bf16[384,256]{1,0:T(8,128)(2,1)S(1)} %get-tuple-element.8.refs_0_), channel_id=1, source_target_pairs={{0,32},{32,0},{1,33},{33,1},{2,34},{34,2},{3,35},{35,3},{4,36},{36... | collective-permute-start | bytes 589832 | tf_op jit(solution)/shard_map/ppermute | solution.py:285
  21.6 11.2 %collective-permute-start = (bf16[384,256]{1,0:T(8,128)(2,1)S(1)}, bf16[384,256]{1,0:T(8,128)(2,1)S(1)}, u32[]{:S(2)}, u32[]{:S(2)}) collective-permute-start(bf16[384,256]{1,0:T(8,128)(2,1)S(1)} %get-tuple-element.8.refs_0_), channel_id=1, source_target_pairs={{0,64},{64,128},{128,192},{1,65},{65,129},{129,193},{2,66},{66,130... | collective-permute-start | bytes 589832 | tf_op jit(solution)/shard_map/ppermute | solution.py:288
  22.9 11.3 %collective-permute-start.1 = (bf16[384,256]{1,0:T(8,128)(2,1)S(1)}, bf16[384,256]{1,0:T(8,128)(2,1)S(1)}, u32[]{:S(2)}, u32[]{:S(2)}) collective-permute-start(bf16[384,256]{1,0:T(8,128)(2,1)S(1)} %get-tuple-element.8.refs_0_), channel_id=1, source_target_pairs={{0,128},{64,192},{1,129},{65,193},{2,130},{66,194},{3,131},{67,195... | collective-permute-start | bytes 589832 | tf_op jit(solution)/shard_map/ppermute | solution.py:288
  24.2 12.1 %collective-permute-start.2 = (bf16[384,256]{1,0:T(8,128)(2,1)S(1)}, bf16[384,256]{1,0:T(8,128)(2,1)S(1)}, u32[]{:S(2)}, u32[]{:S(2)}) collective-permute-start(bf16[384,256]{1,0:T(8,128)(2,1)S(1)} %get-tuple-element.8.refs_0_), channel_id=1, source_target_pairs={{0,192},{1,193},{2,194},{3,195},{4,196},{5,197},{6,198},{7,199},{8... | collective-permute-start | bytes 589832 | tf_op jit(solution)/shard_map/ppermute | solution.py:288
  30.2 8.6 %collective-permute-start.4 = (bf16[384,256]{1,0:T(8,128)(2,1)S(1)}, bf16[384,256]{1,0:T(8,128)(2,1)S(1)}, u32[]{:S(2)}, u32[]{:S(2)}) collective-permute-start(bf16[384,256]{1,0:T(8,128)(2,1)S(1)} %collective-permute-done.3.refs_4_), channel_id=1, source_target_pairs={{0,64},{64,128},{128,192},{1,65},{65,129},{129,193},{2,66},{66,130... | collective-permute-start | bytes 589832 | tf_op jit(solution)/shard_map/ppermute | solution.py:291
  31.5 10.2 %collective-permute-start.5 = (bf16[384,256]{1,0:T(8,128)(2,1)S(1)}, bf16[384,256]{1,0:T(8,128)(2,1)S(1)}, u32[]{:S(2)}, u32[]{:S(2)}) collective-permute-start(bf16[384,256]{1,0:T(8,128)(2,1)S(1)} %collective-permute-done.3.refs_4_), channel_id=1, source_target_pairs={{0,128},{64,192},{1,129},{65,193},{2,130},{66,194},{3,131},{67,195... | collective-permute-start | bytes 589832 | tf_op jit(solution)/shard_map/ppermute | solution.py:291
  32.8 13.0 %collective-permute-start.6 = (bf16[384,256]{1,0:T(8,128)(2,1)S(1)}, bf16[384,256]{1,0:T(8,128)(2,1)S(1)}, u32[]{:S(2)}, u32[]{:S(2)}) collective-permute-start(bf16[384,256]{1,0:T(8,128)(2,1)S(1)} %collective-permute-done.3.refs_4_), channel_id=1, source_target_pairs={{0,192},{1,193},{2,194},{3,195},{4,196},{5,197},{6,198},{7,199},{8... | collective-permute-start | bytes 589832 | tf_op jit(solution)/shard_map/ppermute | solution.py:291
  56.2 7.4 %copy-start = (bf16[1,128,4096]{2,1,0:T(8,128)(2,1)S(1)}, bf16[1,128,4096]{2,1,0:T(8,128)(2,1)}, u32[]{:S(2)}) copy-start(bf16[1,128,4096]{2,1,0:T(8,128)(2,1)} %nkv_ref.3) | copy-start | bytes 3145732
  56.2 46.5 %all-to-all-start.1 = ((bf16[8,208,256]{2,1,0:T(8,128)(2,1)}), bf16[8,208,256]{2,1,0:T(8,128)(2,1)S(1)}, u32[]{:S(2)}, u32[]{:S(2)}) async-start(bf16[8,208,256]{2,1,0:T(8,128)(2,1)} %partial_attention.1), calls=%async_computation.1 | async-start | bytes 1703936 | tf_op jit(solution)/shard_map/all_to_all | solution.py:304
  63.6 36.0 %copy-start.1 = (bf16[192,256]{1,0:T(8,128)(2,1)S(1)}, bf16[192,256]{1,0:T(8,128)(2,1)}, u32[]{:S(2)}) copy-start(bf16[192,256]{1,0:T(8,128)(2,1)} %q_ref.3) | copy-start | bytes 294916
  63.6 3.9 %collective-permute-start.7 = (bf16[128,2048]{1,0:T(8,128)(2,1)S(1)}, bf16[128,2048]{1,0:T(8,128)(2,1)S(1)}, u32[]{:S(2)}, u32[]{:S(2)}) collective-permute-start(bf16[128,2048]{1,0:T(8,128)(2,1)S(1)} %dynamic-slice_bitcast_fusion), channel_id=1, source_target_pairs={{0,256},{256,0},{1,257},{257,1},{2,258},{258,2},{3,259},{259,3},{4... | collective-permute-start | bytes 1572872 | tf_op jit(solution)/shard_map/ppermute | solution.py:297
  69.2 11.3 %collective-permute-start.8 = (bf16[2,128,512]{2,1,0:T(8,128)(2,1)}, bf16[2,128,512]{2,1,0:T(8,128)(2,1)S(1)}, u32[]{:S(2)}, u32[]{:S(2)}) collective-permute-start(bf16[2,128,512]{2,1,0:T(8,128)(2,1)} %get-tuple-element.9), channel_id=1, source_target_pairs={{0,1},{1,0},{2,3},{3,2},{4,5},{5,4},{6,7},{7,6},{8,9},{9,8},{10,11... | collective-permute-start | bytes 786440 | tf_op jit(solution)/shard_map/ppermute | solution.py:299
  71.5 7.0 %copy-start.5 = (s32[3,2]{0,1:T(2,128)S(1)}, s32[3,2]{0,1:T(2,128)}, u32[]{:S(2)}) copy-start(s32[3,2]{0,1:T(2,128)} %param.11) | copy-start | bytes 76
  71.5 20.7 %collective-permute-start.9 = (bf16[2,128,512]{2,1,0:T(8,128)(2,1)}, bf16[2,128,512]{2,1,0:T(8,128)(2,1)S(1)}, u32[]{:S(2)}, u32[]{:S(2)}) collective-permute-start(bf16[2,128,512]{2,1,0:T(8,128)(2,1)} %get-tuple-element.10), channel_id=1, source_target_pairs={{0,2},{1,3},{2,0},{3,1},{4,6},{5,7},{6,4},{7,5},{8,10},{9,11},{10,... | collective-permute-start | bytes 786440 | tf_op jit(solution)/shard_map/ppermute | solution.py:299
  73.9 25.7 %collective-permute-start.10 = (bf16[2,128,512]{2,1,0:T(8,128)(2,1)}, bf16[2,128,512]{2,1,0:T(8,128)(2,1)S(1)}, u32[]{:S(2)}, u32[]{:S(2)}) collective-permute-start(bf16[2,128,512]{2,1,0:T(8,128)(2,1)} %get-tuple-element.11), channel_id=1, source_target_pairs={{0,3},{1,2},{2,1},{3,0},{4,7},{5,6},{6,5},{7,4},{8,11},{9,10},{10,... | collective-permute-start | bytes 786440 | tf_op jit(solution)/shard_map/ppermute | solution.py:299

commit v6 on v4

--- a/solution.py
+++ b/solution.py
@@ -44,8 +44,8 @@
 
 
 def partial_kernel(place_ref, q_ref, *refs):
-    pieces, out_ref = refs[:NX], refs[NX]
-    k_scr, v_scr, s_scr, sem = refs[NX + 1:]
+    pieces, out_ref = refs[:PIECES], refs[PIECES]
+    k_scr, v_scr, s_scr, sem = refs[PIECES + 1:]
     x, zh, y = place_ref[0], place_ref[1], place_ref[2]
     i = pl.program_id(0)
 
@@ -53,7 +53,7 @@
     def _():
         copies = []
         for p in range(PIECES):
-            kv, at = pieces[p % NX], p // NX * 2 * ROWS
+            kv, at = pieces[p], 0
             for h in range(2):
                 copies.append(pltpu.make_async_copy(
                     kv.at[pl.ds(at, ROWS), pl.ds(h * HD, HD)],
@@ -66,7 +66,7 @@
         v_scr[:, HD:2 * HD] = jnp.ones((KEYS, HD), jnp.bfloat16)
         lane0 = lax.broadcasted_iota(jnp.int32, (ROWS, HD), 1) == 0
         for p in range(PIECES):
-            hidden = jnp.logical_or(x < p % NX, jnp.logical_and(zh == 0, p == NX))
+            hidden = jnp.logical_or(x < p // NZ, jnp.logical_and(zh == 0, p == 1))
             bias = jnp.where(hidden, LOW, 0.0)
             k_scr[pl.ds(p * ROWS, ROWS), HD:2 * HD] = jnp.where(lane0, bias, 0.0).astype(jnp.bfloat16)
         for c in copies:
@@ -76,36 +76,43 @@
     row = lax.broadcasted_iota(jnp.int32, (TILE, CHUNK), 0)
     col = lax.broadcasted_iota(jnp.int32, (TILE, CHUNK), 1)
     seen = jnp.logical_or(col >= ROWS, col - row <= i * TILE - y * ROWS)
-    coded = []
-    for h in range(2):
-        qh = q_ref[:, :, h * HD:(h + 1) * HD].reshape(TILE, HD)
-        qh = jnp.concatenate([qh, one] if h == 0 else [one, qh], axis=1)
-        top = jnp.full((TILE, HD), LOW, jnp.float32)
-        for c in range(KEYS // CHUNK):
-            kc = k_scr[pl.ds(c * CHUNK, CHUNK), h * HD:(h + 2) * HD]
-            s = lax.dot_general(qh, kc, (((1,), (1,)), ((), ())), preferred_element_type=jnp.float32)
-            if c == 0:
-                s = jnp.where(seen, s, LOW)
-            s_scr[:, c * CHUNK:(c + 1) * CHUNK] = s
-            top = jnp.maximum(top, jnp.maximum(s[:, :HD], s[:, HD:]))
-        top = jnp.broadcast_to(jnp.max(top, axis=1, keepdims=True), (TILE, HD))
-        off = jnp.maximum(top, -1e20) * C2
-        off = jnp.concatenate([off, off], axis=1)
-        acc = None
-        for c in range(KEYS // CHUNK):
-            p = jnp.exp2(s_scr[:, c * CHUNK:(c + 1) * CHUNK] * C2 - off).astype(jnp.bfloat16)
-            d = lax.dot_general(p, v_scr[pl.ds(c * CHUNK, CHUNK), h * HD:(h + 2) * HD],
-                                (((1,), (0,)), ((), ())), preferred_element_type=jnp.float32)
-            acc = d if acc is None else acc + d
-        main, total = (acc[:, :HD], acc[:, HD:]) if h == 0 else (acc[:, HD:], acc[:, :HD])
-        total = jnp.maximum(total, 1e-30)
-        out_ref[:, 0:ROWS, h * HD:(h + 1) * HD] = (main / total).astype(jnp.bfloat16).reshape(
-            SHARDS, ROWS, HD)
-        stat = jnp.where(top > 0.5 * LOW, top * SCALE + jnp.log(total), LOW)
-        coded.append([code_stat(stat[j * ROWS:(j + 1) * ROWS]) for j in range(SHARDS)])
-    for j in range(SHARDS):
-        out_ref[j, ROWS:, 0:ROWS] = jnp.concatenate([coded[0][j], coded[1][j]], axis=0).astype(jnp.bfloat16)
-        out_ref[j, ROWS:, ROWS:] = jnp.zeros((STAT_ROWS, WIDTH - ROWS), jnp.bfloat16)
+
+    def attend(chunks):
+        coded = []
+        for h in range(2):
+            qh = q_ref[:, :, h * HD:(h + 1) * HD].reshape(TILE, HD)
+            qh = jnp.concatenate([qh, one] if h == 0 else [one, qh], axis=1)
+            top = jnp.full((TILE, HD), LOW, jnp.float32)
+            for c in range(chunks):
+                kc = k_scr[pl.ds(c * CHUNK, CHUNK), h * HD:(h + 2) * HD]
+                s = lax.dot_general(qh, kc, (((1,), (1,)), ((), ())), preferred_element_type=jnp.float32)
+                if c == 0:
+                    s = jnp.where(seen, s, LOW)
+                s_scr[:, c * CHUNK:(c + 1) * CHUNK] = s
+                top = jnp.maximum(top, jnp.maximum(s[:, :HD], s[:, HD:]))
+            top = jnp.broadcast_to(jnp.max(top, axis=1, keepdims=True), (TILE, HD))
+            off = jnp.maximum(top, -1e20) * C2
+            off = jnp.concatenate([off, off], axis=1)
+            acc = None
+            for c in range(chunks):
+                p = jnp.exp2(s_scr[:, c * CHUNK:(c + 1) * CHUNK] * C2 - off).astype(jnp.bfloat16)
+                d = lax.dot_general(p, v_scr[pl.ds(c * CHUNK, CHUNK), h * HD:(h + 2) * HD],
+                                    (((1,), (0,)), ((), ())), preferred_element_type=jnp.float32)
+                acc = d if acc is None else acc + d
+            main, total = (acc[:, :HD], acc[:, HD:]) if h == 0 else (acc[:, HD:], acc[:, :HD])
+            total = jnp.maximum(total, 1e-30)
+            out_ref[:, 0:ROWS, h * HD:(h + 1) * HD] = (main / total).astype(jnp.bfloat16).reshape(
+                SHARDS, ROWS, HD)
+            stat = jnp.where(top > 0.5 * LOW, top * SCALE + jnp.log(total), LOW)
+            coded.append([code_stat(stat[j * ROWS:(j + 1) * ROWS]) for j in range(SHARDS)])
+        for j in range(SHARDS):
+            out_ref[j, ROWS:, 0:ROWS] = jnp.concatenate([coded[0][j], coded[1][j]], axis=0).astype(jnp.bfloat16)
+            out_ref[j, ROWS:, ROWS:] = jnp.zeros((STAT_ROWS, WIDTH - ROWS), jnp.bfloat16)
+
+    for rank in range(NX):
+        @pl.when(x == rank)
+        def _():
+            attend(pl.cdiv((rank + 1) * NZ * ROWS, CHUNK))
 
 
 def partial_attention(place, q_all, pieces):
@@ -113,7 +120,7 @@
         partial_kernel,
         out_shape=jax.ShapeDtypeStruct((NY, ROWS + STAT_ROWS, WIDTH), jnp.bfloat16),
         grid=(NY // SHARDS,),
-        in_specs=[IN_SMEM, pl.BlockSpec((SHARDS, ROWS, WIDTH), lambda i: (i, 0, 0))] + [ANY] * NX,
+        in_specs=[IN_SMEM, pl.BlockSpec((SHARDS, ROWS, WIDTH), lambda i: (i, 0, 0))] + [ANY] * PIECES,
         out_specs=pl.BlockSpec((SHARDS, ROWS + STAT_ROWS, WIDTH), lambda i: (i, 0, 0)),
         scratch_shapes=[
             pltpu.VMEM((KEYS, 3 * HD), jnp.bfloat16),
@@ -249,10 +256,10 @@
 
     kv = jnp.concatenate([key_self, value_self], axis=0)
     kvz = lax.ppermute(kv, "zh", [(0, 1), (1, 0)])
-    both = jnp.concatenate([kv, kvz], axis=0)
-    pieces = [both]
+    pieces = [kv, kvz]
     for k in range(1, NX):
-        pieces.append(lax.ppermute(both, "x", [(a, a + k) for a in range(NX - k)]))
+        pairs = [(a, a + k) for a in range(NX - k)]
+        pieces += [lax.ppermute(kv, "x", pairs), lax.ppermute(kvz, "x", pairs)]
     q_all = lax.all_to_all(
         jnp.broadcast_to(query_self[None], (NY, ROWS, WIDTH)), "y", 0, 0, tiled=True)
 

time: 111 us -> 103 us (0.928)
  waiting for transfers between devices: 51.5 us -> 39.3 us
  starting transfers between devices: 39.3 us -> 43.1 us
    ppermute x3 -> x6, waiting for transfers between devices: 20.1 us -> 11.6 us  [on_device(): pieces += [lax.ppermute(kv, 'x', pairs), lax.ppermute(kvz, 'x', pairs)]]
    ppermute x1, waiting for transfers between devices: 8.59 us -> 4.72 us  [on_device(): kvz = lax.ppermute(kv, 'zh', [(0, 1), (1, 0)])]
    ppermute x3 -> x6, starting transfers between devices: 3.88 us -> 7.74 us  [on_device(): pieces += [lax.ppermute(kv, 'x', pairs), lax.ppermute(kvz, 'x', pairs)]]
  transfers between devices with their start and end apart: 10 -> 13, of which waited for: 8 -> 9; matrix products, arithmetic and copies ran while one was open for 0% -> 0% of each run, Pallas kernels for 4% -> 5%
where the time goes in v6:
time: 103 us
  starting transfers between devices  43.1 us (42%)
  waiting for transfers between devices  39.3 us (38%)
  Pallas kernels  16.3 us (16%)
  local copies, waits for them, and re-layouts  2.96 us (3%)
    ppermute x3, waiting for transfers between devices, on_device(): lax.ppermute(outgoing[k - 1], 'head', [(a, a ^ k) for a in range(HEADS)])  21.1 us
    ppermute x6, waiting for transfers between devices, on_device(): pieces += [lax.ppermute(kv, 'x', pairs), lax.ppermute(kvz, 'x', pairs)]  11.6 us
    pallas_call x1, Pallas kernels, partial_attention(): pl.pallas_call(partial_kernel, out_shape=jax.ShapeDtypeStruct((NY, ROWS +...  10.4 us
    ppermute x3, starting transfers between devices, on_device(): lax.ppermute(outgoing[k - 1], 'head', [(a, a ^ k) for a in range(HEADS)])  9.21 us
    ppermute x1, starting transfers between devices, on_device(): kvz = lax.ppermute(kv, 'zh', [(0, 1), (1, 0)])  9.11 us
    ppermute x6, starting transfers between devices, on_device(): pieces += [lax.ppermute(kv, 'x', pairs), lax.ppermute(kvz, 'x', pairs)]  7.74 us
    all_to_all x1, starting transfers between devices, on_device(): lax.all_to_all(jnp.broadcast_to(query_self[None], (NY, ROWS, WIDTH)), 'y'...  7.68 us
    all_to_all x1, starting transfers between devices, on_device(): received = lax.all_to_all(parts, 'y', 0, 0, tiled=True)  7.35 us
  transfers between devices with their start and end apart: 13, of which 9 were waited for; matrix products, arithmetic and copies ran while one was open for 0% of the time, Pallas kernels for 5%

profile of v6, /device:TPU:142, one launch (start us, length us, event | category | flops | bytes accessed | tf_op | source)
XLA Modules:
  0.0 102.6 jit_solution(9460774025046538453)
XLA Ops:
  0.6 1.8 %broadcast_in_dim.2 = bf16[8,192,256]{2,1,0:T(8,128)(2,1)} broadcast(bf16[192,256]{1,0:T(8,128)(2,1)} %param.6), dimensions={1,2} | broadcast | bytes 884736 | tf_op jit(solution)/shard_map/broadcast_in_dim | solution.py:264
  2.5 0.0 copy-start.2
  2.5 7.7 %all-to-all-start = ((bf16[8,192,256]{2,1,0:T(8,128)(2,1)}), bf16[8,192,256]{2,1,0:T(8,128)(2,1)S(1)}, u32[]{:S(2)}, u32[]{:S(2)}) async-start(bf16[8,192,256]{2,1,0:T(8,128)(2,1)} %broadcast_in_dim.2), calls=%async_computation | async-start | bytes 1572864 | tf_op jit(solution)/shard_map/all_to_all | solution.py:263
  10.1 0.0 copy-done.2
  10.1 0.0 copy-start.3
  10.2 0.9 copy-done.3
  11.0 9.1 %collective-permute-start = (bf16[384,256]{1,0:T(8,128)(2,1)S(1)}, bf16[384,256]{1,0:T(8,128)(2,1)S(1)}, u32[]{:S(2)}, u32[]{:S(2)}) collective-permute-start(bf16[384,256]{1,0:T(8,128)(2,1)S(1)} %constant_dynamic-update-slice_fusion.refs_0_), channel_id=1, source_target_pairs={{0,32},{32,0},{1,33},{33,1},{2,34},{34,2},{3,35},{35,3},{4,36},{36... | collective-permute-start | bytes 589832 | tf_op jit(solution)/shard_map/ppermute | solution.py:258
  20.2 1.3 %collective-permute-start.1 = (bf16[384,256]{1,0:T(8,128)(2,1)S(1)}, bf16[384,256]{1,0:T(8,128)(2,1)S(1)}, u32[]{:S(2)}, u32[]{:S(2)}) collective-permute-start(bf16[384,256]{1,0:T(8,128)(2,1)S(1)} %constant_dynamic-update-slice_fusion.refs_0_), channel_id=1, source_target_pairs={{0,64},{64,128},{128,192},{1,65},{65,129},{129,193},{2,66},{66,130... | collective-permute-start | bytes 589832 | tf_op jit(solution)/shard_map/ppermute | solution.py:262
  21.5 1.3 %collective-permute-start.3 = (bf16[384,256]{1,0:T(8,128)(2,1)S(1)}, bf16[384,256]{1,0:T(8,128)(2,1)S(1)}, u32[]{:S(2)}, u32[]{:S(2)}) collective-permute-start(bf16[384,256]{1,0:T(8,128)(2,1)S(1)} %constant_dynamic-update-slice_fusion.refs_0_), channel_id=1, source_target_pairs={{0,128},{64,192},{1,129},{65,193},{2,130},{66,194},{3,131},{67,195... | collective-permute-start | bytes 589832 | tf_op jit(solution)/shard_map/ppermute | solution.py:262
  22.8 1.3 %collective-permute-start.5 = (bf16[384,256]{1,0:T(8,128)(2,1)S(1)}, bf16[384,256]{1,0:T(8,128)(2,1)S(1)}, u32[]{:S(2)}, u32[]{:S(2)}) collective-permute-start(bf16[384,256]{1,0:T(8,128)(2,1)S(1)} %constant_dynamic-update-slice_fusion.refs_0_), channel_id=1, source_target_pairs={{0,192},{1,193},{2,194},{3,195},{4,196},{5,197},{6,198},{7,199},{8... | collective-permute-start | bytes 589832 | tf_op jit(solution)/shard_map/ppermute | solution.py:262
  24.1 4.7 %collective-permute-done.refs_1_ = bf16[384,256]{1,0:T(8,128)(2,1)S(1)} collective-permute-done((bf16[384,256]{1,0:T(8,128)(2,1)S(1)}, bf16[384,256]{1,0:T(8,128)(2,1)S(1)}, u32[]{:S(2)}, u32[]{:S(2)}) %collective-permute-start) | collective-permute-done | bytes 196640 | tf_op jit(solution)/shard_map/ppermute | solution.py:258
  28.8 1.3 %collective-permute-start.2 = (bf16[384,256]{1,0:T(8,128)(2,1)S(1)}, bf16[384,256]{1,0:T(8,128)(2,1)S(1)}, u32[]{:S(2)}, u32[]{:S(2)}) collective-permute-start(bf16[384,256]{1,0:T(8,128)(2,1)S(1)} %collective-permute-done.refs_1_), channel_id=1, source_target_pairs={{0,64},{64,128},{128,192},{1,65},{65,129},{129,193},{2,66},{66,130... | collective-permute-start | bytes 589832 | tf_op jit(solution)/shard_map/ppermute | solution.py:262
  30.1 1.3 %collective-permute-start.4 = (bf16[384,256]{1,0:T(8,128)(2,1)S(1)}, bf16[384,256]{1,0:T(8,128)(2,1)S(1)}, u32[]{:S(2)}, u32[]{:S(2)}) collective-permute-start(bf16[384,256]{1,0:T(8,128)(2,1)S(1)} %collective-permute-done.refs_1_), channel_id=1, source_target_pairs={{0,128},{64,192},{1,129},{65,193},{2,130},{66,194},{3,131},{67,195... | collective-permute-start | bytes 589832 | tf_op jit(solution)/shard_map/ppermute | solution.py:262
  31.4 0.0 collective-permute-done.1.refs_2_
  31.4 1.3 %collective-permute-start.6 = (bf16[384,256]{1,0:T(8,128)(2,1)S(1)}, bf16[384,256]{1,0:T(8,128)(2,1)S(1)}, u32[]{:S(2)}, u32[]{:S(2)}) collective-permute-start(bf16[384,256]{1,0:T(8,128)(2,1)S(1)} %collective-permute-done.refs_1_), channel_id=1, source_target_pairs={{0,192},{1,193},{2,194},{3,195},{4,196},{5,197},{6,198},{7,199},{8... | collective-permute-start | bytes 589832 | tf_op jit(solution)/shard_map/ppermute | solution.py:262
  32.7 0.1 stack.23.place_ref
  32.8 0.0 collective-permute-done.3.refs_4_
  32.8 2.1 %collective-permute-done.5.refs_6_ = bf16[384,256]{1,0:T(8,128)(2,1)S(1)} collective-permute-done((bf16[384,256]{1,0:T(8,128)(2,1)S(1)}, bf16[384,256]{1,0:T(8,128)(2,1)S(1)}, u32[]{:S(2)}, u32[]{:S(2)}) %collective-permute-start.5) | collective-permute-done | bytes 196640 | tf_op jit(solution)/shard_map/ppermute | solution.py:262
  34.9 2.5 %collective-permute-done.2.refs_3_ = bf16[384,256]{1,0:T(8,128)(2,1)S(1)} collective-permute-done((bf16[384,256]{1,0:T(8,128)(2,1)S(1)}, bf16[384,256]{1,0:T(8,128)(2,1)S(1)}, u32[]{:S(2)}, u32[]{:S(2)}) %collective-permute-start.2) | collective-permute-done | bytes 196640 | tf_op jit(solution)/shard_map/ppermute | solution.py:262
  37.4 2.9 %collective-permute-done.4.refs_5_ = bf16[384,256]{1,0:T(8,128)(2,1)S(1)} collective-permute-done((bf16[384,256]{1,0:T(8,128)(2,1)S(1)}, bf16[384,256]{1,0:T(8,128)(2,1)S(1)}, u32[]{:S(2)}, u32[]{:S(2)}) %collective-permute-start.4) | collective-permute-done | bytes 196640 | tf_op jit(solution)/shard_map/ppermute | solution.py:262
  40.3 4.1 %collective-permute-done.6.refs_7_ = bf16[384,256]{1,0:T(8,128)(2,1)S(1)} collective-permute-done((bf16[384,256]{1,0:T(8,128)(2,1)S(1)}, bf16[384,256]{1,0:T(8,128)(2,1)S(1)}, u32[]{:S(2)}, u32[]{:S(2)}) %collective-permute-start.6) | collective-permute-done | bytes 196640 | tf_op jit(solution)/shard_map/ppermute | solution.py:262
  44.4 0.0 all-to-all-done.q_ref
  44.4 10.4 %partial_attention.1 = bf16[8,208,256]{2,1,0:T(8,128)(2,1)} custom-call(s32[5]{0:T(128)S(1)} %stack.23.place_ref, bf16[8,192,256]{2,1,0:T(8,128)(2,1)S(1)} %all-to-all-done.q_ref, bf16[384,256]{1,0:T(8,128)(2,1)S(1)} %constant_dynamic-update-slice_fusion.refs_0_, bf16[384,256]{1,0:T(8,128)(2,1)S(1)} %collective-permute-done.refs_1_, ...), custom_call_target="tpu_custom_call" | custom-call | flops 2415919104 | bytes 1572864 | tf_op jit(solution)/shard_map/partial_attention/pallas_call | solution.py:119
  54.8 0.0 copy-start
  54.8 7.3 %all-to-all-start.1 = ((bf16[8,208,256]{2,1,0:T(8,128)(2,1)}), bf16[8,208,256]{2,1,0:T(8,128)(2,1)S(1)}, u32[]{:S(2)}, u32[]{:S(2)}) async-start(bf16[8,208,256]{2,1,0:T(8,128)(2,1)} %partial_attention.1), calls=%async_computation.1 | async-start | bytes 1703936 | tf_op jit(solution)/shard_map/all_to_all | solution.py:276
  62.1 0.0 copy-done
  62.2 0.0 copy-start.1
  62.2 2.1 %collective-permute-start.7 = (bf16[128,2048]{1,0:T(8,128)(2,1)S(1)}, bf16[128,2048]{1,0:T(8,128)(2,1)S(1)}, u32[]{:S(2)}, u32[]{:S(2)}) collective-permute-start(bf16[128,2048]{1,0:T(8,128)(2,1)S(1)} %dynamic-slice_bitcast_fusion), channel_id=1, source_target_pairs={{0,256},{256,0},{1,257},{257,1},{2,258},{258,2},{3,259},{259,3},{4... | collective-permute-start | bytes 1572872 | tf_op jit(solution)/shard_map/ppermute | solution.py:269
  64.3 1.9 %collective-permute-done.7.twin_ref = bf16[128,2048]{1,0:T(8,128)(2,1)S(1)} collective-permute-done((bf16[128,2048]{1,0:T(8,128)(2,1)S(1)}, bf16[128,2048]{1,0:T(8,128)(2,1)S(1)}, u32[]{:S(2)}, u32[]{:S(2)}) %collective-permute-start.7) | collective-permute-done | bytes 524320 | tf_op jit(solution)/shard_map/ppermute | solution.py:269
  66.1 1.6 %split_groups.1 = (bf16[2,128,512]{2,1,0:T(8,128)(2,1)}, bf16[2,128,512]{2,1,0:T(8,128)(2,1)}, bf16[2,128,512]{2,1,0:T(8,128)(2,1)}) custom-call(s32[5]{0:T(128)S(1)} %stack.23.place_ref, bf16[1,128,4096]{2,1,0:T(8,128)(2,1)S(1)} %copy-done, bf16[128,2048]{1,0:T(8,128)(2,1)S(1)} %collective-permute-done.7.twin_ref), custom_call_target="tpu_custom_call" | custom-call | tf_op jit(solution)/shard_map/split_groups/pallas_call | solution.py:190
  67.8 2.3 %collective-permute-start.8 = (bf16[2,128,512]{2,1,0:T(8,128)(2,1)}, bf16[2,128,512]{2,1,0:T(8,128)(2,1)S(1)}, u32[]{:S(2)}, u32[]{:S(2)}) collective-permute-start(bf16[2,128,512]{2,1,0:T(8,128)(2,1)} %get-tuple-element.5), channel_id=1, source_target_pairs={{0,1},{1,0},{2,3},{3,2},{4,5},{5,4},{6,7},{7,6},{8,9},{9,8},{10,11... | collective-permute-start | bytes 786440 | tf_op jit(solution)/shard_map/ppermute | solution.py:271
  70.1 0.0 copy-start.4
  70.1 2.4 %collective-permute-start.9 = (bf16[2,128,512]{2,1,0:T(8,128)(2,1)}, bf16[2,128,512]{2,1,0:T(8,128)(2,1)S(1)}, u32[]{:S(2)}, u32[]{:S(2)}) collective-permute-start(bf16[2,128,512]{2,1,0:T(8,128)(2,1)} %get-tuple-element.6), channel_id=1, source_target_pairs={{0,2},{1,3},{2,0},{3,1},{4,6},{5,7},{6,4},{7,5},{8,10},{9,11},{10,... | collective-permute-start | bytes 786440 | tf_op jit(solution)/shard_map/ppermute | solution.py:271
  72.5 4.5 %collective-permute-start.10 = (bf16[2,128,512]{2,1,0:T(8,128)(2,1)}, bf16[2,128,512]{2,1,0:T(8,128)(2,1)S(1)}, u32[]{:S(2)}, u32[]{:S(2)}) collective-permute-start(bf16[2,128,512]{2,1,0:T(8,128)(2,1)} %get-tuple-element.7), channel_id=1, source_target_pairs={{0,3},{1,2},{2,1},{3,0},{4,7},{5,6},{6,5},{7,4},{8,11},{9,10},{10,... | collective-permute-start | bytes 786440 | tf_op jit(solution)/shard_map/ppermute | solution.py:271
  77.0 0.0 copy-done.4
  77.0 0.1 copy.8.map_ref
  77.1 1.9 %collective-permute-done.8.refs_0_ = bf16[2,128,512]{2,1,0:T(8,128)(2,1)S(1)} collective-permute-done((bf16[2,128,512]{2,1,0:T(8,128)(2,1)}, bf16[2,128,512]{2,1,0:T(8,128)(2,1)S(1)}, u32[]{:S(2)}, u32[]{:S(2)}) %collective-permute-start.8) | collective-permute-done | bytes 262176 | tf_op jit(solution)/shard_map/ppermute | solution.py:271
  79.0 11.7 %collective-permute-done.9.refs_1_ = bf16[2,128,512]{2,1,0:T(8,128)(2,1)S(1)} collective-permute-done((bf16[2,128,512]{2,1,0:T(8,128)(2,1)}, bf16[2,128,512]{2,1,0:T(8,128)(2,1)S(1)}, u32[]{:S(2)}, u32[]{:S(2)}) %collective-permute-start.9) | collective-permute-done | bytes 262176 | tf_op jit(solution)/shard_map/ppermute | solution.py:271
  90.7 7.4 %collective-permute-done.10.refs_2_ = bf16[2,128,512]{2,1,0:T(8,128)(2,1)S(1)} collective-permute-done((bf16[2,128,512]{2,1,0:T(8,128)(2,1)}, bf16[2,128,512]{2,1,0:T(8,128)(2,1)S(1)}, u32[]{:S(2)}, u32[]{:S(2)}) %collective-permute-start.10) | collective-permute-done | bytes 262176 | tf_op jit(solution)/shard_map/ppermute | solution.py:271
  98.2 0.0 copy-done.1
  98.2 3.0 %cross_attention.1 = bf16[192,256]{1,0:T(8,128)(2,1)} custom-call(s32[5]{0:T(128)S(1)} %stack.23.place_ref, s32[3,2]{1,0:T(4,128)S(1)} %copy.8.map_ref, bf16[192,256]{1,0:T(8,128)(2,1)S(1)} %copy-done.1, bf16[1,128,4096]{2,1,0:T(8,128)(2,1)S(1)} %copy-done, bf16[128,2048]{1,0:T(8,128)(2,1)S(1)} %collective-permute-done.7.twin_ref, ...), custom_call_target="tpu_custom_call" | custom-call | flops 100663296 | bytes 2097152 | tf_op jit(solution)/shard_map/cross_attention/pallas_call | solution.py:236
  101.2 0.0 all-to-all-done.1.part_ref
  101.2 1.3 %combine.1 = bf16[192,256]{1,0:T(8,128)(2,1)} custom-call(bf16[8,208,256]{2,1,0:T(8,128)(2,1)S(1)} %all-to-all-done.1.part_ref), custom_call_target="tpu_custom_call" | custom-call | tf_op jit(solution)/shard_map/combine/pallas_call | solution.py:161
  (3 shorter events, 0.1 us)
Async XLA Ops:
  2.5 7.7 %copy-start.2 = (bf16[192,256]{1,0:T(8,128)(2,1)S(1)}, bf16[192,256]{1,0:T(8,128)(2,1)}, u32[]{:S(2)}) copy-start(bf16[192,256]{1,0:T(8,128)(2,1)} %param.7) | copy-start | bytes 294916
  2.5 41.9 %all-to-all-start = ((bf16[8,192,256]{2,1,0:T(8,128)(2,1)}), bf16[8,192,256]{2,1,0:T(8,128)(2,1)S(1)}, u32[]{:S(2)}, u32[]{:S(2)}) async-start(bf16[8,192,256]{2,1,0:T(8,128)(2,1)} %broadcast_in_dim.2), calls=%async_computation | async-start | bytes 1572864 | tf_op jit(solution)/shard_map/all_to_all | solution.py:263
  10.1 0.9 copy-start.3
  11.0 17.7 %collective-permute-start = (bf16[384,256]{1,0:T(8,128)(2,1)S(1)}, bf16[384,256]{1,0:T(8,128)(2,1)S(1)}, u32[]{:S(2)}, u32[]{:S(2)}) collective-permute-start(bf16[384,256]{1,0:T(8,128)(2,1)S(1)} %constant_dynamic-update-slice_fusion.refs_0_), channel_id=1, source_target_pairs={{0,32},{32,0},{1,33},{33,1},{2,34},{34,2},{3,35},{35,3},{4,36},{36... | collective-permute-start | bytes 589832 | tf_op jit(solution)/shard_map/ppermute | solution.py:258
  20.2 11.2 %collective-permute-start.1 = (bf16[384,256]{1,0:T(8,128)(2,1)S(1)}, bf16[384,256]{1,0:T(8,128)(2,1)S(1)}, u32[]{:S(2)}, u32[]{:S(2)}) collective-permute-start(bf16[384,256]{1,0:T(8,128)(2,1)S(1)} %constant_dynamic-update-slice_fusion.refs_0_), channel_id=1, source_target_pairs={{0,64},{64,128},{128,192},{1,65},{65,129},{129,193},{2,66},{66,130... | collective-permute-start | bytes 589832 | tf_op jit(solution)/shard_map/ppermute | solution.py:262
  21.5 11.3 %collective-permute-start.3 = (bf16[384,256]{1,0:T(8,128)(2,1)S(1)}, bf16[384,256]{1,0:T(8,128)(2,1)S(1)}, u32[]{:S(2)}, u32[]{:S(2)}) collective-permute-start(bf16[384,256]{1,0:T(8,128)(2,1)S(1)} %constant_dynamic-update-slice_fusion.refs_0_), channel_id=1, source_target_pairs={{0,128},{64,192},{1,129},{65,193},{2,130},{66,194},{3,131},{67,195... | collective-permute-start | bytes 589832 | tf_op jit(solution)/shard_map/ppermute | solution.py:262
  22.8 12.1 %collective-permute-start.5 = (bf16[384,256]{1,0:T(8,128)(2,1)S(1)}, bf16[384,256]{1,0:T(8,128)(2,1)S(1)}, u32[]{:S(2)}, u32[]{:S(2)}) collective-permute-start(bf16[384,256]{1,0:T(8,128)(2,1)S(1)} %constant_dynamic-update-slice_fusion.refs_0_), channel_id=1, source_target_pairs={{0,192},{1,193},{2,194},{3,195},{4,196},{5,197},{6,198},{7,199},{8... | collective-permute-start | bytes 589832 | tf_op jit(solution)/shard_map/ppermute | solution.py:262
  28.8 8.6 %collective-permute-start.2 = (bf16[384,256]{1,0:T(8,128)(2,1)S(1)}, bf16[384,256]{1,0:T(8,128)(2,1)S(1)}, u32[]{:S(2)}, u32[]{:S(2)}) collective-permute-start(bf16[384,256]{1,0:T(8,128)(2,1)S(1)} %collective-permute-done.refs_1_), channel_id=1, source_target_pairs={{0,64},{64,128},{128,192},{1,65},{65,129},{129,193},{2,66},{66,130... | collective-permute-start | bytes 589832 | tf_op jit(solution)/shard_map/ppermute | solution.py:262
  30.1 10.2 %collective-permute-start.4 = (bf16[384,256]{1,0:T(8,128)(2,1)S(1)}, bf16[384,256]{1,0:T(8,128)(2,1)S(1)}, u32[]{:S(2)}, u32[]{:S(2)}) collective-permute-start(bf16[384,256]{1,0:T(8,128)(2,1)S(1)} %collective-permute-done.refs_1_), channel_id=1, source_target_pairs={{0,128},{64,192},{1,129},{65,193},{2,130},{66,194},{3,131},{67,195... | collective-permute-start | bytes 589832 | tf_op jit(solution)/shard_map/ppermute | solution.py:262
  31.4 13.0 %collective-permute-start.6 = (bf16[384,256]{1,0:T(8,128)(2,1)S(1)}, bf16[384,256]{1,0:T(8,128)(2,1)S(1)}, u32[]{:S(2)}, u32[]{:S(2)}) collective-permute-start(bf16[384,256]{1,0:T(8,128)(2,1)S(1)} %collective-permute-done.refs_1_), channel_id=1, source_target_pairs={{0,192},{1,193},{2,194},{3,195},{4,196},{5,197},{6,198},{7,199},{8... | collective-permute-start | bytes 589832 | tf_op jit(solution)/shard_map/ppermute | solution.py:262
  54.8 7.4 %copy-start = (bf16[1,128,4096]{2,1,0:T(8,128)(2,1)S(1)}, bf16[1,128,4096]{2,1,0:T(8,128)(2,1)}, u32[]{:S(2)}) copy-start(bf16[1,128,4096]{2,1,0:T(8,128)(2,1)} %nkv_ref.3) | copy-start | bytes 3145732
  54.8 46.5 %all-to-all-start.1 = ((bf16[8,208,256]{2,1,0:T(8,128)(2,1)}), bf16[8,208,256]{2,1,0:T(8,128)(2,1)S(1)}, u32[]{:S(2)}, u32[]{:S(2)}) async-start(bf16[8,208,256]{2,1,0:T(8,128)(2,1)} %partial_attention.1), calls=%async_computation.1 | async-start | bytes 1703936 | tf_op jit(solution)/shard_map/all_to_all | solution.py:276
  62.2 36.0 %copy-start.1 = (bf16[192,256]{1,0:T(8,128)(2,1)S(1)}, bf16[192,256]{1,0:T(8,128)(2,1)}, u32[]{:S(2)}) copy-start(bf16[192,256]{1,0:T(8,128)(2,1)} %q_ref.1) | copy-start | bytes 294916
  62.2 3.9 %collective-permute-start.7 = (bf16[128,2048]{1,0:T(8,128)(2,1)S(1)}, bf16[128,2048]{1,0:T(8,128)(2,1)S(1)}, u32[]{:S(2)}, u32[]{:S(2)}) collective-permute-start(bf16[128,2048]{1,0:T(8,128)(2,1)S(1)} %dynamic-slice_bitcast_fusion), channel_id=1, source_target_pairs={{0,256},{256,0},{1,257},{257,1},{2,258},{258,2},{3,259},{259,3},{4... | collective-permute-start | bytes 1572872 | tf_op jit(solution)/shard_map/ppermute | solution.py:269
  67.8 11.3 %collective-permute-start.8 = (bf16[2,128,512]{2,1,0:T(8,128)(2,1)}, bf16[2,128,512]{2,1,0:T(8,128)(2,1)S(1)}, u32[]{:S(2)}, u32[]{:S(2)}) collective-permute-start(bf16[2,128,512]{2,1,0:T(8,128)(2,1)} %get-tuple-element.5), channel_id=1, source_target_pairs={{0,1},{1,0},{2,3},{3,2},{4,5},{5,4},{6,7},{7,6},{8,9},{9,8},{10,11... | collective-permute-start | bytes 786440 | tf_op jit(solution)/shard_map/ppermute | solution.py:271
  70.1 7.0 %copy-start.4 = (s32[3,2]{0,1:T(2,128)S(1)}, s32[3,2]{0,1:T(2,128)}, u32[]{:S(2)}) copy-start(s32[3,2]{0,1:T(2,128)} %param.11) | copy-start | bytes 76
  70.1 20.7 %collective-permute-start.9 = (bf16[2,128,512]{2,1,0:T(8,128)(2,1)}, bf16[2,128,512]{2,1,0:T(8,128)(2,1)S(1)}, u32[]{:S(2)}, u32[]{:S(2)}) collective-permute-start(bf16[2,128,512]{2,1,0:T(8,128)(2,1)} %get-tuple-element.6), channel_id=1, source_target_pairs={{0,2},{1,3},{2,0},{3,1},{4,6},{5,7},{6,4},{7,5},{8,10},{9,11},{10,... | collective-permute-start | bytes 786440 | tf_op jit(solution)/shard_map/ppermute | solution.py:271
  72.5 25.7 %collective-permute-start.10 = (bf16[2,128,512]{2,1,0:T(8,128)(2,1)}, bf16[2,128,512]{2,1,0:T(8,128)(2,1)S(1)}, u32[]{:S(2)}, u32[]{:S(2)}) collective-permute-start(bf16[2,128,512]{2,1,0:T(8,128)(2,1)} %get-tuple-element.7), channel_id=1, source_target_pairs={{0,3},{1,2},{2,1},{3,0},{4,7},{5,6},{6,5},{7,4},{8,11},{9,10},{10,... | collective-permute-start | bytes 786440 | tf_op jit(solution)/shard_map/ppermute | solution.py:271

commit v7 on v6

--- a/solution.py
+++ b/solution.py
@@ -34,34 +34,27 @@
 IN_VMEM = pl.BlockSpec(memory_space=pltpu.VMEM)
 
 
-def code_stat(stat):
-    row = jnp.transpose(stat)[0:STAT_ROWS // 2, :]
-    hi = row.astype(jnp.bfloat16).astype(jnp.float32)
-    mid = (row - hi).astype(jnp.bfloat16).astype(jnp.float32)
-    low = row - hi - mid
-    at = lax.broadcasted_iota(jnp.int32, row.shape, 0)
-    return jnp.where(at == 0, hi, jnp.where(at == 1, mid, low))
-
-
 def partial_kernel(place_ref, q_ref, *refs):
     pieces, out_ref = refs[:PIECES], refs[PIECES]
     k_scr, v_scr, s_scr, sem = refs[PIECES + 1:]
     x, zh, y = place_ref[0], place_ref[1], place_ref[2]
     i = pl.program_id(0)
 
+    def key_copies():
+        return [pltpu.make_async_copy(
+            pieces[p].at[pl.ds(0, ROWS), pl.ds(h * HD, HD)],
+            k_scr.at[pl.ds(p * ROWS, ROWS), pl.ds(2 * h * HD, HD)], sem.at[p, h])
+            for h in range(2) for p in range(PIECES)]
+
+    def value_copies():
+        return [pltpu.make_async_copy(
+            pieces[p].at[pl.ds(ROWS, ROWS), pl.ds(h * HD, HD)],
+            v_scr.at[pl.ds(p * ROWS, ROWS), pl.ds(2 * h * HD, HD)], sem.at[p, 2 + h])
+            for h in range(2) for p in range(PIECES)]
+
     @pl.when(i == 0)
     def _():
-        copies = []
-        for p in range(PIECES):
-            kv, at = pieces[p], 0
-            for h in range(2):
-                copies.append(pltpu.make_async_copy(
-                    kv.at[pl.ds(at, ROWS), pl.ds(h * HD, HD)],
-                    k_scr.at[pl.ds(p * ROWS, ROWS), pl.ds(2 * h * HD, HD)], sem.at[p, h]))
-                copies.append(pltpu.make_async_copy(
-                    kv.at[pl.ds(at + ROWS, ROWS), pl.ds(h * HD, HD)],
-                    v_scr.at[pl.ds(p * ROWS, ROWS), pl.ds(2 * h * HD, HD)], sem.at[p, 2 + h]))
-        for c in copies:
+        for c in key_copies() + value_copies():
             c.start()
         v_scr[:, HD:2 * HD] = jnp.ones((KEYS, HD), jnp.bfloat16)
         lane0 = lax.broadcasted_iota(jnp.int32, (ROWS, HD), 1) == 0
@@ -69,16 +62,17 @@
             hidden = jnp.logical_or(x < p // NZ, jnp.logical_and(zh == 0, p == 1))
             bias = jnp.where(hidden, LOW, 0.0)
             k_scr[pl.ds(p * ROWS, ROWS), HD:2 * HD] = jnp.where(lane0, bias, 0.0).astype(jnp.bfloat16)
-        for c in copies:
+        for c in key_copies():
             c.wait()
 
     one = jnp.where(lax.broadcasted_iota(jnp.int32, (TILE, HD), 1) == 0, 1.0, 0.0).astype(jnp.bfloat16)
+    lane = lax.broadcasted_iota(jnp.int32, (ROWS, HD), 1)
     row = lax.broadcasted_iota(jnp.int32, (TILE, CHUNK), 0)
     col = lax.broadcasted_iota(jnp.int32, (TILE, CHUNK), 1)
     seen = jnp.logical_or(col >= ROWS, col - row <= i * TILE - y * ROWS)
 
     def attend(chunks):
-        coded = []
+        table = jnp.ones((ROWS, HD), jnp.float32)
         for h in range(2):
             qh = q_ref[:, :, h * HD:(h + 1) * HD].reshape(TILE, HD)
             qh = jnp.concatenate([qh, one] if h == 0 else [one, qh], axis=1)
@@ -90,6 +84,11 @@
                     s = jnp.where(seen, s, LOW)
                 s_scr[:, c * CHUNK:(c + 1) * CHUNK] = s
                 top = jnp.maximum(top, jnp.maximum(s[:, :HD], s[:, HD:]))
+            if h == 0:
+                @pl.when(i == 0)
+                def _():
+                    for c in value_copies():
+                        c.wait()
             top = jnp.broadcast_to(jnp.max(top, axis=1, keepdims=True), (TILE, HD))
             off = jnp.maximum(top, -1e20) * C2
             off = jnp.concatenate([off, off], axis=1)
@@ -103,10 +102,22 @@
             total = jnp.maximum(total, 1e-30)
             out_ref[:, 0:ROWS, h * HD:(h + 1) * HD] = (main / total).astype(jnp.bfloat16).reshape(
                 SHARDS, ROWS, HD)
-            stat = jnp.where(top > 0.5 * LOW, top * SCALE + jnp.log(total), LOW)
-            coded.append([code_stat(stat[j * ROWS:(j + 1) * ROWS]) for j in range(SHARDS)])
+            for j in range(SHARDS):
+                part = slice(j * ROWS, (j + 1) * ROWS)
+                table = jnp.where(lane == 2 * j + h, top[part], table)
+                table = jnp.where(lane == 2 * (SHARDS + j) + h, total[part], table)
+        turned = jnp.transpose(table)
+        tops, totals = turned[0:2 * SHARDS], turned[2 * SHARDS:4 * SHARDS]
+        stat = jnp.where(tops > 0.5 * LOW, tops * SCALE + jnp.log(totals), LOW)
+        hi = stat.astype(jnp.bfloat16).astype(jnp.float32)
+        mid = (stat - hi).astype(jnp.bfloat16).astype(jnp.float32)
+        low = stat - hi - mid
+        at = lax.broadcasted_iota(jnp.int32, (STAT_ROWS // 2, ROWS), 0)
         for j in range(SHARDS):
-            out_ref[j, ROWS:, 0:ROWS] = jnp.concatenate([coded[0][j], coded[1][j]], axis=0).astype(jnp.bfloat16)
+            rows = []
+            for r in (2 * j, 2 * j + 1):
+                rows.append(jnp.where(at == 0, hi[r:r + 1], jnp.where(at == 1, mid[r:r + 1], low[r:r + 1])))
+            out_ref[j, ROWS:, 0:ROWS] = jnp.concatenate(rows, axis=0).astype(jnp.bfloat16)
             out_ref[j, ROWS:, ROWS:] = jnp.zeros((STAT_ROWS, WIDTH - ROWS), jnp.bfloat16)
 
     for rank in range(NX):

time: 103 us -> 104 us (level)
  no operation moved by 1% of the time
where the time goes in v7:
time: 104 us; the launch traced here: 103 us
  starting transfers between devices  43.1 us (41%)
  waiting for transfers between devices  39.3 us (38%)
  Pallas kernels  16.8 us (16%)
  local copies, waits for them, and re-layouts  2.96 us (3%)
    ppermute x3, waiting for transfers between devices, on_device(): lax.ppermute(outgoing[k - 1], 'head', [(a, a ^ k) for a in range(HEADS)])  21.1 us
    ppermute x6, waiting for transfers between devices, on_device(): pieces += [lax.ppermute(kv, 'x', pairs), lax.ppermute(kvz, 'x', pairs)]  11.6 us
    pallas_call x1, Pallas kernels, partial_attention(): pl.pallas_call(partial_kernel, out_shape=jax.ShapeDtypeStruct((NY, ROWS +...  10.8 us
    ppermute x3, starting transfers between devices, on_device(): lax.ppermute(outgoing[k - 1], 'head', [(a, a ^ k) for a in range(HEADS)])  9.21 us
    ppermute x1, starting transfers between devices, on_device(): kvz = lax.ppermute(kv, 'zh', [(0, 1), (1, 0)])  9.11 us
    ppermute x6, starting transfers between devices, on_device(): pieces += [lax.ppermute(kv, 'x', pairs), lax.ppermute(kvz, 'x', pairs)]  7.74 us
    all_to_all x1, starting transfers between devices, on_device(): lax.all_to_all(jnp.broadcast_to(query_self[None], (NY, ROWS, WIDTH)), 'y'...  7.68 us
    all_to_all x1, starting transfers between devices, on_device(): received = lax.all_to_all(parts, 'y', 0, 0, tiled=True)  7.35 us
  transfers between devices with their start and end apart: 13, of which 9 were waited for; matrix products, arithmetic and copies ran while one was open for 0% of the time, Pallas kernels for 5%

profile of v7, /device:TPU:142, one launch (start us, length us, event | category | flops | bytes accessed | tf_op | source)
XLA Modules:
  0.0 103.0 jit_solution(18125783160886392878)
XLA Ops:
  0.6 1.8 %broadcast_in_dim.2 = bf16[8,192,256]{2,1,0:T(8,128)(2,1)} broadcast(bf16[192,256]{1,0:T(8,128)(2,1)} %param.6), dimensions={1,2} | broadcast | bytes 884736 | tf_op jit(solution)/shard_map/broadcast_in_dim | solution.py:275
  2.5 0.0 copy-start.2
  2.5 7.7 %all-to-all-start = ((bf16[8,192,256]{2,1,0:T(8,128)(2,1)}), bf16[8,192,256]{2,1,0:T(8,128)(2,1)S(1)}, u32[]{:S(2)}, u32[]{:S(2)}) async-start(bf16[8,192,256]{2,1,0:T(8,128)(2,1)} %broadcast_in_dim.2), calls=%async_computation | async-start | bytes 1572864 | tf_op jit(solution)/shard_map/all_to_all | solution.py:274
  10.1 0.0 copy-done.2
  10.1 0.0 copy-start.3
  10.2 0.9 copy-done.3
  11.0 9.1 %collective-permute-start = (bf16[384,256]{1,0:T(8,128)(2,1)S(1)}, bf16[384,256]{1,0:T(8,128)(2,1)S(1)}, u32[]{:S(2)}, u32[]{:S(2)}) collective-permute-start(bf16[384,256]{1,0:T(8,128)(2,1)S(1)} %constant_dynamic-update-slice_fusion.refs_0_), channel_id=1, source_target_pairs={{0,32},{32,0},{1,33},{33,1},{2,34},{34,2},{3,35},{35,3},{4,36},{36... | collective-permute-start | bytes 589832 | tf_op jit(solution)/shard_map/ppermute | solution.py:269
  20.2 1.3 %collective-permute-start.1 = (bf16[384,256]{1,0:T(8,128)(2,1)S(1)}, bf16[384,256]{1,0:T(8,128)(2,1)S(1)}, u32[]{:S(2)}, u32[]{:S(2)}) collective-permute-start(bf16[384,256]{1,0:T(8,128)(2,1)S(1)} %constant_dynamic-update-slice_fusion.refs_0_), channel_id=1, source_target_pairs={{0,64},{64,128},{128,192},{1,65},{65,129},{129,193},{2,66},{66,130... | collective-permute-start | bytes 589832 | tf_op jit(solution)/shard_map/ppermute | solution.py:273
  21.5 1.3 %collective-permute-start.3 = (bf16[384,256]{1,0:T(8,128)(2,1)S(1)}, bf16[384,256]{1,0:T(8,128)(2,1)S(1)}, u32[]{:S(2)}, u32[]{:S(2)}) collective-permute-start(bf16[384,256]{1,0:T(8,128)(2,1)S(1)} %constant_dynamic-update-slice_fusion.refs_0_), channel_id=1, source_target_pairs={{0,128},{64,192},{1,129},{65,193},{2,130},{66,194},{3,131},{67,195... | collective-permute-start | bytes 589832 | tf_op jit(solution)/shard_map/ppermute | solution.py:273
  22.8 1.3 %collective-permute-start.5 = (bf16[384,256]{1,0:T(8,128)(2,1)S(1)}, bf16[384,256]{1,0:T(8,128)(2,1)S(1)}, u32[]{:S(2)}, u32[]{:S(2)}) collective-permute-start(bf16[384,256]{1,0:T(8,128)(2,1)S(1)} %constant_dynamic-update-slice_fusion.refs_0_), channel_id=1, source_target_pairs={{0,192},{1,193},{2,194},{3,195},{4,196},{5,197},{6,198},{7,199},{8... | collective-permute-start | bytes 589832 | tf_op jit(solution)/shard_map/ppermute | solution.py:273
  24.1 4.7 %collective-permute-done.refs_1_ = bf16[384,256]{1,0:T(8,128)(2,1)S(1)} collective-permute-done((bf16[384,256]{1,0:T(8,128)(2,1)S(1)}, bf16[384,256]{1,0:T(8,128)(2,1)S(1)}, u32[]{:S(2)}, u32[]{:S(2)}) %collective-permute-start) | collective-permute-done | bytes 196640 | tf_op jit(solution)/shard_map/ppermute | solution.py:269
  28.8 1.3 %collective-permute-start.2 = (bf16[384,256]{1,0:T(8,128)(2,1)S(1)}, bf16[384,256]{1,0:T(8,128)(2,1)S(1)}, u32[]{:S(2)}, u32[]{:S(2)}) collective-permute-start(bf16[384,256]{1,0:T(8,128)(2,1)S(1)} %collective-permute-done.refs_1_), channel_id=1, source_target_pairs={{0,64},{64,128},{128,192},{1,65},{65,129},{129,193},{2,66},{66,130... | collective-permute-start | bytes 589832 | tf_op jit(solution)/shard_map/ppermute | solution.py:273
  30.1 1.3 %collective-permute-start.4 = (bf16[384,256]{1,0:T(8,128)(2,1)S(1)}, bf16[384,256]{1,0:T(8,128)(2,1)S(1)}, u32[]{:S(2)}, u32[]{:S(2)}) collective-permute-start(bf16[384,256]{1,0:T(8,128)(2,1)S(1)} %collective-permute-done.refs_1_), channel_id=1, source_target_pairs={{0,128},{64,192},{1,129},{65,193},{2,130},{66,194},{3,131},{67,195... | collective-permute-start | bytes 589832 | tf_op jit(solution)/shard_map/ppermute | solution.py:273
  31.4 0.0 collective-permute-done.1.refs_2_
  31.4 1.3 %collective-permute-start.6 = (bf16[384,256]{1,0:T(8,128)(2,1)S(1)}, bf16[384,256]{1,0:T(8,128)(2,1)S(1)}, u32[]{:S(2)}, u32[]{:S(2)}) collective-permute-start(bf16[384,256]{1,0:T(8,128)(2,1)S(1)} %collective-permute-done.refs_1_), channel_id=1, source_target_pairs={{0,192},{1,193},{2,194},{3,195},{4,196},{5,197},{6,198},{7,199},{8... | collective-permute-start | bytes 589832 | tf_op jit(solution)/shard_map/ppermute | solution.py:273
  32.7 0.1 stack.23.place_ref
  32.8 0.0 collective-permute-done.3.refs_4_
  32.8 2.1 %collective-permute-done.5.refs_6_ = bf16[384,256]{1,0:T(8,128)(2,1)S(1)} collective-permute-done((bf16[384,256]{1,0:T(8,128)(2,1)S(1)}, bf16[384,256]{1,0:T(8,128)(2,1)S(1)}, u32[]{:S(2)}, u32[]{:S(2)}) %collective-permute-start.5) | collective-permute-done | bytes 196640 | tf_op jit(solution)/shard_map/ppermute | solution.py:273
  34.9 2.5 %collective-permute-done.2.refs_3_ = bf16[384,256]{1,0:T(8,128)(2,1)S(1)} collective-permute-done((bf16[384,256]{1,0:T(8,128)(2,1)S(1)}, bf16[384,256]{1,0:T(8,128)(2,1)S(1)}, u32[]{:S(2)}, u32[]{:S(2)}) %collective-permute-start.2) | collective-permute-done | bytes 196640 | tf_op jit(solution)/shard_map/ppermute | solution.py:273
  37.4 2.9 %collective-permute-done.4.refs_5_ = bf16[384,256]{1,0:T(8,128)(2,1)S(1)} collective-permute-done((bf16[384,256]{1,0:T(8,128)(2,1)S(1)}, bf16[384,256]{1,0:T(8,128)(2,1)S(1)}, u32[]{:S(2)}, u32[]{:S(2)}) %collective-permute-start.4) | collective-permute-done | bytes 196640 | tf_op jit(solution)/shard_map/ppermute | solution.py:273
  40.3 4.1 %collective-permute-done.6.refs_7_ = bf16[384,256]{1,0:T(8,128)(2,1)S(1)} collective-permute-done((bf16[384,256]{1,0:T(8,128)(2,1)S(1)}, bf16[384,256]{1,0:T(8,128)(2,1)S(1)}, u32[]{:S(2)}, u32[]{:S(2)}) %collective-permute-start.6) | collective-permute-done | bytes 196640 | tf_op jit(solution)/shard_map/ppermute | solution.py:273
  44.4 0.0 all-to-all-done.q_ref
  44.4 10.8 %partial_attention.1 = bf16[8,208,256]{2,1,0:T(8,128)(2,1)} custom-call(s32[5]{0:T(128)S(1)} %stack.23.place_ref, bf16[8,192,256]{2,1,0:T(8,128)(2,1)S(1)} %all-to-all-done.q_ref, bf16[384,256]{1,0:T(8,128)(2,1)S(1)} %constant_dynamic-update-slice_fusion.refs_0_, bf16[384,256]{1,0:T(8,128)(2,1)S(1)} %collective-permute-done.refs_1_, ...), custom_call_target="tpu_custom_call" | custom-call | flops 2415919104 | bytes 1572864 | tf_op jit(solution)/shard_map/partial_attention/pallas_call | solution.py:130
  55.2 0.0 copy-start
  55.2 7.4 %all-to-all-start.1 = ((bf16[8,208,256]{2,1,0:T(8,128)(2,1)}), bf16[8,208,256]{2,1,0:T(8,128)(2,1)S(1)}, u32[]{:S(2)}, u32[]{:S(2)}) async-start(bf16[8,208,256]{2,1,0:T(8,128)(2,1)} %partial_attention.1), calls=%async_computation.1 | async-start | bytes 1703936 | tf_op jit(solution)/shard_map/all_to_all | solution.py:287
  62.6 0.0 copy-done
  62.6 0.0 copy-start.1
  62.6 2.1 %collective-permute-start.7 = (bf16[128,2048]{1,0:T(8,128)(2,1)S(1)}, bf16[128,2048]{1,0:T(8,128)(2,1)S(1)}, u32[]{:S(2)}, u32[]{:S(2)}) collective-permute-start(bf16[128,2048]{1,0:T(8,128)(2,1)S(1)} %dynamic-slice_bitcast_fusion), channel_id=1, source_target_pairs={{0,256},{256,0},{1,257},{257,1},{2,258},{258,2},{3,259},{259,3},{4... | collective-permute-start | bytes 1572872 | tf_op jit(solution)/shard_map/ppermute | solution.py:280
  64.7 1.9 %collective-permute-done.7.twin_ref = bf16[128,2048]{1,0:T(8,128)(2,1)S(1)} collective-permute-done((bf16[128,2048]{1,0:T(8,128)(2,1)S(1)}, bf16[128,2048]{1,0:T(8,128)(2,1)S(1)}, u32[]{:S(2)}, u32[]{:S(2)}) %collective-permute-start.7) | collective-permute-done | bytes 524320 | tf_op jit(solution)/shard_map/ppermute | solution.py:280
  66.6 1.6 %split_groups.1 = (bf16[2,128,512]{2,1,0:T(8,128)(2,1)}, bf16[2,128,512]{2,1,0:T(8,128)(2,1)}, bf16[2,128,512]{2,1,0:T(8,128)(2,1)}) custom-call(s32[5]{0:T(128)S(1)} %stack.23.place_ref, bf16[1,128,4096]{2,1,0:T(8,128)(2,1)S(1)} %copy-done, bf16[128,2048]{1,0:T(8,128)(2,1)S(1)} %collective-permute-done.7.twin_ref), custom_call_target="tpu_custom_call" | custom-call | tf_op jit(solution)/shard_map/split_groups/pallas_call | solution.py:201
  68.2 2.3 %collective-permute-start.8 = (bf16[2,128,512]{2,1,0:T(8,128)(2,1)}, bf16[2,128,512]{2,1,0:T(8,128)(2,1)S(1)}, u32[]{:S(2)}, u32[]{:S(2)}) collective-permute-start(bf16[2,128,512]{2,1,0:T(8,128)(2,1)} %get-tuple-element.5), channel_id=1, source_target_pairs={{0,1},{1,0},{2,3},{3,2},{4,5},{5,4},{6,7},{7,6},{8,9},{9,8},{10,11... | collective-permute-start | bytes 786440 | tf_op jit(solution)/shard_map/ppermute | solution.py:282
  70.5 0.0 copy-start.4
  70.5 2.5 %collective-permute-start.9 = (bf16[2,128,512]{2,1,0:T(8,128)(2,1)}, bf16[2,128,512]{2,1,0:T(8,128)(2,1)S(1)}, u32[]{:S(2)}, u32[]{:S(2)}) collective-permute-start(bf16[2,128,512]{2,1,0:T(8,128)(2,1)} %get-tuple-element.6), channel_id=1, source_target_pairs={{0,2},{1,3},{2,0},{3,1},{4,6},{5,7},{6,4},{7,5},{8,10},{9,11},{10,... | collective-permute-start | bytes 786440 | tf_op jit(solution)/shard_map/ppermute | solution.py:282
  73.0 4.5 %collective-permute-start.10 = (bf16[2,128,512]{2,1,0:T(8,128)(2,1)}, bf16[2,128,512]{2,1,0:T(8,128)(2,1)S(1)}, u32[]{:S(2)}, u32[]{:S(2)}) collective-permute-start(bf16[2,128,512]{2,1,0:T(8,128)(2,1)} %get-tuple-element.7), channel_id=1, source_target_pairs={{0,3},{1,2},{2,1},{3,0},{4,7},{5,6},{6,5},{7,4},{8,11},{9,10},{10,... | collective-permute-start | bytes 786440 | tf_op jit(solution)/shard_map/ppermute | solution.py:282
  77.4 0.0 copy-done.4
  77.5 0.1 copy.8.map_ref
  77.6 1.9 %collective-permute-done.8.refs_0_ = bf16[2,128,512]{2,1,0:T(8,128)(2,1)S(1)} collective-permute-done((bf16[2,128,512]{2,1,0:T(8,128)(2,1)}, bf16[2,128,512]{2,1,0:T(8,128)(2,1)S(1)}, u32[]{:S(2)}, u32[]{:S(2)}) %collective-permute-start.8) | collective-permute-done | bytes 262176 | tf_op jit(solution)/shard_map/ppermute | solution.py:282
  79.5 11.7 %collective-permute-done.9.refs_1_ = bf16[2,128,512]{2,1,0:T(8,128)(2,1)S(1)} collective-permute-done((bf16[2,128,512]{2,1,0:T(8,128)(2,1)}, bf16[2,128,512]{2,1,0:T(8,128)(2,1)S(1)}, u32[]{:S(2)}, u32[]{:S(2)}) %collective-permute-start.9) | collective-permute-done | bytes 262176 | tf_op jit(solution)/shard_map/ppermute | solution.py:282
  91.2 7.4 %collective-permute-done.10.refs_2_ = bf16[2,128,512]{2,1,0:T(8,128)(2,1)S(1)} collective-permute-done((bf16[2,128,512]{2,1,0:T(8,128)(2,1)}, bf16[2,128,512]{2,1,0:T(8,128)(2,1)S(1)}, u32[]{:S(2)}, u32[]{:S(2)}) %collective-permute-start.10) | collective-permute-done | bytes 262176 | tf_op jit(solution)/shard_map/ppermute | solution.py:282
  98.6 0.0 copy-done.1
  98.6 3.0 %cross_attention.1 = bf16[192,256]{1,0:T(8,128)(2,1)} custom-call(s32[5]{0:T(128)S(1)} %stack.23.place_ref, s32[3,2]{1,0:T(4,128)S(1)} %copy.8.map_ref, bf16[192,256]{1,0:T(8,128)(2,1)S(1)} %copy-done.1, bf16[1,128,4096]{2,1,0:T(8,128)(2,1)S(1)} %copy-done, bf16[128,2048]{1,0:T(8,128)(2,1)S(1)} %collective-permute-done.7.twin_ref, ...), custom_call_target="tpu_custom_call" | custom-call | flops 100663296 | bytes 2097152 | tf_op jit(solution)/shard_map/cross_attention/pallas_call | solution.py:247
  101.7 0.0 all-to-all-done.1.part_ref
  101.7 1.3 %combine.1 = bf16[192,256]{1,0:T(8,128)(2,1)} custom-call(bf16[8,208,256]{2,1,0:T(8,128)(2,1)S(1)} %all-to-all-done.1.part_ref), custom_call_target="tpu_custom_call" | custom-call | tf_op jit(solution)/shard_map/combine/pallas_call | solution.py:172
  (3 shorter events, 0.1 us)
Async XLA Ops:
  2.5 7.7 %copy-start.2 = (bf16[192,256]{1,0:T(8,128)(2,1)S(1)}, bf16[192,256]{1,0:T(8,128)(2,1)}, u32[]{:S(2)}) copy-start(bf16[192,256]{1,0:T(8,128)(2,1)} %param.7) | copy-start | bytes 294916
  2.5 41.9 %all-to-all-start = ((bf16[8,192,256]{2,1,0:T(8,128)(2,1)}), bf16[8,192,256]{2,1,0:T(8,128)(2,1)S(1)}, u32[]{:S(2)}, u32[]{:S(2)}) async-start(bf16[8,192,256]{2,1,0:T(8,128)(2,1)} %broadcast_in_dim.2), calls=%async_computation | async-start | bytes 1572864 | tf_op jit(solution)/shard_map/all_to_all | solution.py:274
  10.1 0.9 copy-start.3
  11.0 17.7 %collective-permute-start = (bf16[384,256]{1,0:T(8,128)(2,1)S(1)}, bf16[384,256]{1,0:T(8,128)(2,1)S(1)}, u32[]{:S(2)}, u32[]{:S(2)}) collective-permute-start(bf16[384,256]{1,0:T(8,128)(2,1)S(1)} %constant_dynamic-update-slice_fusion.refs_0_), channel_id=1, source_target_pairs={{0,32},{32,0},{1,33},{33,1},{2,34},{34,2},{3,35},{35,3},{4,36},{36... | collective-permute-start | bytes 589832 | tf_op jit(solution)/shard_map/ppermute | solution.py:269
  20.2 11.2 %collective-permute-start.1 = (bf16[384,256]{1,0:T(8,128)(2,1)S(1)}, bf16[384,256]{1,0:T(8,128)(2,1)S(1)}, u32[]{:S(2)}, u32[]{:S(2)}) collective-permute-start(bf16[384,256]{1,0:T(8,128)(2,1)S(1)} %constant_dynamic-update-slice_fusion.refs_0_), channel_id=1, source_target_pairs={{0,64},{64,128},{128,192},{1,65},{65,129},{129,193},{2,66},{66,130... | collective-permute-start | bytes 589832 | tf_op jit(solution)/shard_map/ppermute | solution.py:273
  21.5 11.3 %collective-permute-start.3 = (bf16[384,256]{1,0:T(8,128)(2,1)S(1)}, bf16[384,256]{1,0:T(8,128)(2,1)S(1)}, u32[]{:S(2)}, u32[]{:S(2)}) collective-permute-start(bf16[384,256]{1,0:T(8,128)(2,1)S(1)} %constant_dynamic-update-slice_fusion.refs_0_), channel_id=1, source_target_pairs={{0,128},{64,192},{1,129},{65,193},{2,130},{66,194},{3,131},{67,195... | collective-permute-start | bytes 589832 | tf_op jit(solution)/shard_map/ppermute | solution.py:273
  22.8 12.1 %collective-permute-start.5 = (bf16[384,256]{1,0:T(8,128)(2,1)S(1)}, bf16[384,256]{1,0:T(8,128)(2,1)S(1)}, u32[]{:S(2)}, u32[]{:S(2)}) collective-permute-start(bf16[384,256]{1,0:T(8,128)(2,1)S(1)} %constant_dynamic-update-slice_fusion.refs_0_), channel_id=1, source_target_pairs={{0,192},{1,193},{2,194},{3,195},{4,196},{5,197},{6,198},{7,199},{8... | collective-permute-start | bytes 589832 | tf_op jit(solution)/shard_map/ppermute | solution.py:273
  28.8 8.6 %collective-permute-start.2 = (bf16[384,256]{1,0:T(8,128)(2,1)S(1)}, bf16[384,256]{1,0:T(8,128)(2,1)S(1)}, u32[]{:S(2)}, u32[]{:S(2)}) collective-permute-start(bf16[384,256]{1,0:T(8,128)(2,1)S(1)} %collective-permute-done.refs_1_), channel_id=1, source_target_pairs={{0,64},{64,128},{128,192},{1,65},{65,129},{129,193},{2,66},{66,130... | collective-permute-start | bytes 589832 | tf_op jit(solution)/shard_map/ppermute | solution.py:273
  30.1 10.2 %collective-permute-start.4 = (bf16[384,256]{1,0:T(8,128)(2,1)S(1)}, bf16[384,256]{1,0:T(8,128)(2,1)S(1)}, u32[]{:S(2)}, u32[]{:S(2)}) collective-permute-start(bf16[384,256]{1,0:T(8,128)(2,1)S(1)} %collective-permute-done.refs_1_), channel_id=1, source_target_pairs={{0,128},{64,192},{1,129},{65,193},{2,130},{66,194},{3,131},{67,195... | collective-permute-start | bytes 589832 | tf_op jit(solution)/shard_map/ppermute | solution.py:273
  31.4 13.0 %collective-permute-start.6 = (bf16[384,256]{1,0:T(8,128)(2,1)S(1)}, bf16[384,256]{1,0:T(8,128)(2,1)S(1)}, u32[]{:S(2)}, u32[]{:S(2)}) collective-permute-start(bf16[384,256]{1,0:T(8,128)(2,1)S(1)} %collective-permute-done.refs_1_), channel_id=1, source_target_pairs={{0,192},{1,193},{2,194},{3,195},{4,196},{5,197},{6,198},{7,199},{8... | collective-permute-start | bytes 589832 | tf_op jit(solution)/shard_map/ppermute | solution.py:273
  55.2 7.4 %copy-start = (bf16[1,128,4096]{2,1,0:T(8,128)(2,1)S(1)}, bf16[1,128,4096]{2,1,0:T(8,128)(2,1)}, u32[]{:S(2)}) copy-start(bf16[1,128,4096]{2,1,0:T(8,128)(2,1)} %nkv_ref.3) | copy-start | bytes 3145732
  55.2 46.5 %all-to-all-start.1 = ((bf16[8,208,256]{2,1,0:T(8,128)(2,1)}), bf16[8,208,256]{2,1,0:T(8,128)(2,1)S(1)}, u32[]{:S(2)}, u32[]{:S(2)}) async-start(bf16[8,208,256]{2,1,0:T(8,128)(2,1)} %partial_attention.1), calls=%async_computation.1 | async-start | bytes 1703936 | tf_op jit(solution)/shard_map/all_to_all | solution.py:287
  62.6 36.0 %copy-start.1 = (bf16[192,256]{1,0:T(8,128)(2,1)S(1)}, bf16[192,256]{1,0:T(8,128)(2,1)}, u32[]{:S(2)}) copy-start(bf16[192,256]{1,0:T(8,128)(2,1)} %q_ref.1) | copy-start | bytes 294916
  62.6 3.9 %collective-permute-start.7 = (bf16[128,2048]{1,0:T(8,128)(2,1)S(1)}, bf16[128,2048]{1,0:T(8,128)(2,1)S(1)}, u32[]{:S(2)}, u32[]{:S(2)}) collective-permute-start(bf16[128,2048]{1,0:T(8,128)(2,1)S(1)} %dynamic-slice_bitcast_fusion), channel_id=1, source_target_pairs={{0,256},{256,0},{1,257},{257,1},{2,258},{258,2},{3,259},{259,3},{4... | collective-permute-start | bytes 1572872 | tf_op jit(solution)/shard_map/ppermute | solution.py:280
  68.2 11.3 %collective-permute-start.8 = (bf16[2,128,512]{2,1,0:T(8,128)(2,1)}, bf16[2,128,512]{2,1,0:T(8,128)(2,1)S(1)}, u32[]{:S(2)}, u32[]{:S(2)}) collective-permute-start(bf16[2,128,512]{2,1,0:T(8,128)(2,1)} %get-tuple-element.5), channel_id=1, source_target_pairs={{0,1},{1,0},{2,3},{3,2},{4,5},{5,4},{6,7},{7,6},{8,9},{9,8},{10,11... | collective-permute-start | bytes 786440 | tf_op jit(solution)/shard_map/ppermute | solution.py:282
  70.5 7.0 %copy-start.4 = (s32[3,2]{0,1:T(2,128)S(1)}, s32[3,2]{0,1:T(2,128)}, u32[]{:S(2)}) copy-start(s32[3,2]{0,1:T(2,128)} %param.11) | copy-start | bytes 76
  70.5 20.7 %collective-permute-start.9 = (bf16[2,128,512]{2,1,0:T(8,128)(2,1)}, bf16[2,128,512]{2,1,0:T(8,128)(2,1)S(1)}, u32[]{:S(2)}, u32[]{:S(2)}) collective-permute-start(bf16[2,128,512]{2,1,0:T(8,128)(2,1)} %get-tuple-element.6), channel_id=1, source_target_pairs={{0,2},{1,3},{2,0},{3,1},{4,6},{5,7},{6,4},{7,5},{8,10},{9,11},{10,... | collective-permute-start | bytes 786440 | tf_op jit(solution)/shard_map/ppermute | solution.py:282
  73.0 25.7 %collective-permute-start.10 = (bf16[2,128,512]{2,1,0:T(8,128)(2,1)}, bf16[2,128,512]{2,1,0:T(8,128)(2,1)S(1)}, u32[]{:S(2)}, u32[]{:S(2)}) collective-permute-start(bf16[2,128,512]{2,1,0:T(8,128)(2,1)} %get-tuple-element.7), channel_id=1, source_target_pairs={{0,3},{1,2},{2,1},{3,0},{4,7},{5,6},{6,5},{7,4},{8,11},{9,10},{10,... | collective-permute-start | bytes 786440 | tf_op jit(solution)/shard_map/ppermute | solution.py:282
